TPU v7x, 128 devices: a whole 4x4x4 slice. The times are simulated.
128 devices in a mesh: lat: 32 (over x, z, core), rad: 4 (over y).
Axes of the slice: x: 4, y: 4, z: 4, core: 2. Of those that a mesh axis runs over, the one named last changes fastest.
Arguments:
- kernel: bfloat16 [4096, 4, 64, 256], P(('lat', 'rad')), may hold values from -0.1875 to 0.1875
- target_device: int32 [4096, 4], P(('lat', 'rad')), may hold values from 0 to 127, all different within a row; in each aligned block of 32 rows (0 to 31, 32 to 63, ...) at most 2 rows name the same one
- target_block: int32 [4096, 4], P(('lat', 'rad')), may hold values from 0 to 127
- counts: int32 [4096], P(('lat', 'rad')), may hold values from 16 to 64
- traveltimes: float32 [4096, 64], P(('lat', 'rad')), may hold values from -6 to 6
- prior_residual: float32 [4096, 64], P(('lat', 'rad')), may hold values from -12 to 12
Outputs:
- model_update: float32 [32, 512, 256], P('rad', 'lat')
- data_vector: float32 [4096, 64], P(('lat', 'rad'))
Inputs may be any that keep to these rules, and one draw needn't show every extreme that they name: `target_device`: each ray block names 4 different devices; among the ray blocks of one device at most 2 name the same device, and some device is named by exactly 2 of them.
All inputs are finite; a program needn't handle non-finite values.
Results may differ from a plain program's by a relative error of at most 0.007.
Values may be sent and summed in bfloat16 or wider, within the bound.
No kernel may reach another device: no remote copies, remote signals or barrier semaphores. Data moves between devices by JAX's collectives and lax.ppermute only.
A program may use at most 128 MiB of HBM per device.

v0:
```python
import jax
import jax.numpy as jnp
from jax import lax
from jax.sharding import PartitionSpec as P

ITERS = 3
MB_R = 8
MB_L = 16


FREEDOM = 4.0
DAMPING = 0.3


def extended(cells, sides, width):
    for axis, dim in sides:
        count = lax.axis_size(axis)
        ends = count - 1
        head = lax.slice_in_dim(cells, 0, width, axis=dim)
        tail = lax.slice_in_dim(cells, cells.shape[dim] - width, cells.shape[dim], axis=dim)
        cells = jnp.concatenate(
            [
                lax.ppermute(tail, axis, [(i, (i + 1) % count) for i in range(ends)]),
                cells,
                lax.ppermute(head, axis, [((i + 1) % count, i) for i in range(ends)]),
            ],
            axis=dim,
        )
    return cells


def roughen(model_field):
    padded = extended(model_field, (("lat", 1), ("rad", 0)), 1)
    beside = padded[2:, 1:-1] + padded[:-2, 1:-1] + padded[1:-1, 2:] + padded[1:-1, :-2]
    return 4.0 * model_field - beside


def data_norm(data_vector, pen_vec):
    totals = lax.psum(
        (jnp.sum(data_vector * data_vector), jnp.sum(pen_vec * pen_vec)), ("lat", "rad")
    )
    return jnp.sqrt(totals[0] + totals[1])


def model_norm(model_dir):
    return jnp.sqrt(lax.psum(jnp.sum(model_dir * model_dir), ("lat", "rad")))


def body(kernel, target_device, target_block, counts, traveltimes, prior_residual):
    devices = lax.axis_size("lat") * lax.axis_size("rad")
    ray_blocks, fanout, ray_len, cell_len = kernel.shape
    capacity = max(2, 2 * ray_blocks * fanout // devices)
    entries = ray_blocks * fanout
    num_blocks = MB_R * MB_L
    targets = target_device.reshape(entries)
    onehot = (targets[:, None] == jnp.arange(devices, dtype=jnp.int32)[None, :]).astype(jnp.int32)
    earlier = jnp.cumsum(onehot, axis=0) - onehot
    slot_rank = jnp.sum(earlier * onehot, axis=1)
    position = targets * capacity + slot_rank
    requests = (
        jnp.full((devices * capacity,), -1, jnp.int32)
        .at[position]
        .set(target_block.reshape(entries))
    )
    wanted = lax.all_to_all(
        requests.reshape(devices, capacity), ("lat", "rad"), split_axis=0, concat_axis=0, tiled=True
    )
    present = wanted >= 0
    segment = jnp.where(present, wanted, num_blocks).reshape(devices * capacity)
    safe_index = jnp.maximum(wanted, 0)

    def collect(arrived):
        summed = jax.ops.segment_sum(
            arrived.reshape(devices * capacity, cell_len), segment, num_segments=num_blocks + 1
        )
        return summed[:num_blocks].reshape(MB_R, MB_L, cell_len)

    outgoing = jnp.zeros((devices * capacity, ray_len, cell_len), jnp.bfloat16)
    outgoing = outgoing.at[position].set(kernel.reshape(entries, ray_len, cell_len))
    held_tiles = lax.all_to_all(
        outgoing.reshape(devices, capacity, ray_len, cell_len),
        ("lat", "rad"),
        split_axis=0,
        concat_axis=0,
        tiled=True,
    )

    def adjoint(ray_values):
        rounded = ray_values.astype(jnp.bfloat16)
        spread = jnp.zeros((devices * capacity, ray_len), jnp.bfloat16)
        spread = spread.at[position].set(jnp.repeat(rounded, fanout, axis=0))
        arrived = lax.all_to_all(
            spread.reshape(devices, capacity, ray_len),
            ("lat", "rad"),
            split_axis=0,
            concat_axis=0,
            tiled=True,
        )
        partial_value = jnp.einsum(
            "sqrc,sqr->sqc", held_tiles, arrived, preferred_element_type=jnp.float32
        )
        return collect(partial_value)

    ray_mask = (jnp.arange(ray_len, dtype=jnp.int32)[None, :] < counts[:, None]).astype(jnp.float32)
    weights = ray_mask * jnp.sqrt((FREEDOM + 1.0) / (FREEDOM + prior_residual * prior_residual))
    data_vector = weights * traveltimes
    pen_vec = jnp.zeros((MB_R, MB_L, cell_len), jnp.float32)
    beta_norm = data_norm(data_vector, pen_vec)
    data_vector = data_vector / beta_norm
    model_dir = adjoint(weights * data_vector)
    alpha_norm = model_norm(model_dir)
    model_dir = model_dir / alpha_norm
    search_dir = model_dir
    model_update = jnp.zeros_like(model_dir)
    phi_bar = beta_norm
    rho_bar = alpha_norm
    for sweep in range(ITERS):
        flat_model = model_dir.reshape(num_blocks, cell_len).astype(jnp.bfloat16)
        blocks = jnp.where(present[:, :, None], flat_model[safe_index], jnp.zeros((), jnp.bfloat16))
        products = jnp.einsum(
            "sqrc,sqc->sqr", held_tiles, blocks, preferred_element_type=jnp.float32
        )
        returned = lax.all_to_all(products, ("lat", "rad"), split_axis=0, concat_axis=0, tiled=True)
        picked = returned.reshape(devices * capacity, ray_len)[position]
        data_vector = (
            weights * jnp.sum(picked.reshape(ray_blocks, fanout, ray_len), axis=1)
            - alpha_norm * data_vector
        )
        pen_vec = DAMPING * roughen(model_dir) - alpha_norm * pen_vec
        beta_norm = data_norm(data_vector, pen_vec)
        data_vector = data_vector / beta_norm
        pen_vec = pen_vec / beta_norm
        model_dir = (
            adjoint(weights * data_vector) + DAMPING * roughen(pen_vec) - beta_norm * model_dir
        )
        alpha_norm = model_norm(model_dir)
        model_dir = model_dir / alpha_norm
        rho_value = jnp.sqrt(rho_bar * rho_bar + beta_norm * beta_norm)
        cosine = rho_bar / rho_value
        sine = beta_norm / rho_value
        theta_value = sine * alpha_norm
        rho_bar = -cosine * alpha_norm
        phi_value = cosine * phi_bar
        phi_bar = sine * phi_bar
        model_update = model_update + phi_value / rho_value * search_dir
        search_dir = model_dir - theta_value / rho_value * search_dir
    return (model_update, data_vector)


def solution(mesh):
    in_specs = (
        P(("lat", "rad"), None, None, None),
        P(("lat", "rad"), None),
        P(("lat", "rad"), None),
        P(("lat", "rad")),
        P(("lat", "rad"), None),
        P(("lat", "rad"), None),
    )
    out_specs = (P("rad", "lat", None), P(("lat", "rad"), None))
    return jax.shard_map(body, mesh=mesh, in_specs=in_specs, out_specs=out_specs, check_vma=False)
```

profile of v0, /device:TPU:1, one launch (start us, length us, event | category | flops | bytes accessed | tf_op | source)
XLA Modules:
  0.0 810.6 jit_solution(6520203030804221693)
XLA Ops:
  6.9 11.5 %all-to-all-start = ((s32[128,1,2]{2,1,0:T(1,128)}), s32[128,1,2]{2,1,0:T(1,128)S(1)}, u32[]{:S(2)}, u32[]{:S(2)}) async-start(s32[128,1,2]{2,1,0:T(1,128)} %bitcast.2), calls=%async_computation | async-start | bytes 131072 | tf_op jit(solution)/shard_map/all_to_all | solution.py:65
  18.4 67.2 %psum.88 = f32[]{:T(128)} all-reduce(f32[]{:T(128)} %multiply_reduce_fusion.8), channel_id=1, replica_groups=mesh['lat'=32,'rad'=4] {'lat','rad'}, use_global_device_ids=true, to_apply=%region_5.6 | all-reduce | flops 1 | bytes 8 | tf_op jit(solution)/shard_map/psum | solution.py:39
  88.6 4.7 all-to-all-start.2
  93.4 4.3 broadcast_in_dim.58
  97.6 19.3 %scatter_fusion = bf16[256,64,256]{2,1,0:T(8,128)(2,1)} fusion(bf16[256,64,256]{2,1,0:T(8,128)(2,1)} %broadcast_in_dim.58, s32[128]{0:T(128)S(1)} %fusion.62, bf16[128,64,256]{2,1,0:T(8,128)(2,1)} %bitcast.62), kind=kCustom, calls=%fused_computation.7 | custom fusion | bytes 12583424 | tf_op jit(solution)/shard_map/scatter | solution.py:79
  117.0 10.2 %all-to-all-start.1 = ((bf16[128,2,64,256]{3,2,1,0:T(8,128)(2,1)}), bf16[128,2,64,256]{3,2,1,0:T(8,128)(2,1)}, u32[]{:S(2)}, u32[]{:S(2)}) async-start(bf16[128,2,64,256]{3,2,1,0:T(8,128)(2,1)} %bitcast.59), calls=%async_computation.1 | async-start | bytes 16777216 | tf_op jit(solution)/shard_map/all_to_all | solution.py:80
  129.2 102.7 %all-to-all-done.1 = bf16[128,2,64,256]{3,2,1,0:T(8,128)(2,1)} async-done(((bf16[128,2,64,256]{3,2,1,0:T(8,128)(2,1)}), bf16[128,2,64,256]{3,2,1,0:T(8,128)(2,1)}, u32[]{:S(2)}, u32[]{:S(2)}) %all-to-all-start.1) | async-done | bytes 8388640 | tf_op jit(solution)/shard_map/all_to_all | solution.py:80
  231.9 4.6 fusion.47
  239.6 62.8 %psum.79 = f32[]{:T(128)} all-reduce(f32[]{:T(128)} %multiply_reduce_fusion.4), channel_id=1, replica_groups=mesh['lat'=32,'rad'=4] {'lat','rad'}, use_global_device_ids=true, to_apply=%region_10.11 | all-reduce | flops 1 | bytes 8 | tf_op jit(solution)/shard_map/psum | solution.py:46
  312.7 4.2 collective-permute-start.3
  316.8 5.6 fusion.4
  323.2 8.7 %all-to-all-start.3 = ((f32[128,1,128]{2,1,0:T(1,128)}), f32[128,1,128]{2,1,0:T(1,128)S(1)}, u32[]{:S(2)}, u32[]{:S(2)}) async-start(f32[128,1,128]{2,1,0:T(1,128)} %reshape.323), calls=%async_computation.3 | async-start | bytes 131072 | tf_op jit(solution)/shard_map/all_to_all | solution.py:123
  332.6 9.1 %all-to-all-done.3 = f32[128,1,128]{2,1,0:T(1,128)S(1)} async-done(((f32[128,1,128]{2,1,0:T(1,128)}), f32[128,1,128]{2,1,0:T(1,128)S(1)}, u32[]{:S(2)}, u32[]{:S(2)}) %all-to-all-start.3) | async-done | bytes 65568 | tf_op jit(solution)/shard_map/all_to_all | solution.py:123
  345.9 62.6 %psum.89 = f32[]{:T(128)} all-reduce(f32[]{:T(128)S(6)} %add.151), channel_id=1, replica_groups=mesh['lat'=32,'rad'=4] {'lat','rad'}, use_global_device_ids=true, to_apply=%region_13.14 | all-reduce | flops 1 | bytes 8 | tf_op jit(solution)/shard_map/psum | solution.py:39
  415.9 6.9 all-to-all-start.4
  424.2 4.0 collective-permute-start.7
  428.2 4.4 all-to-all-done.4
  432.6 4.6 fusion.45
  440.2 62.7 %psum.82 = f32[]{:T(128)} all-reduce(f32[]{:T(128)} %get-tuple-element.16), channel_id=1, replica_groups=mesh['lat'=32,'rad'=4] {'lat','rad'}, use_global_device_ids=true, to_apply=%region_19.20 | all-reduce | flops 1 | bytes 8 | tf_op jit(solution)/shard_map/psum | solution.py:46
  512.9 4.0 collective-permute-start.11
  516.9 5.6 fusion.2
  523.4 8.8 %all-to-all-start.5 = ((f32[128,1,128]{2,1,0:T(1,128)}), f32[128,1,128]{2,1,0:T(1,128)S(1)}, u32[]{:S(2)}, u32[]{:S(2)}) async-start(f32[128,1,128]{2,1,0:T(1,128)} %reshape.325), calls=%async_computation.5 | async-start | bytes 131072 | tf_op jit(solution)/shard_map/all_to_all | solution.py:123
  532.9 9.1 %all-to-all-done.5 = f32[128,1,128]{2,1,0:T(1,128)S(1)} async-done(((f32[128,1,128]{2,1,0:T(1,128)}), f32[128,1,128]{2,1,0:T(1,128)S(1)}, u32[]{:S(2)}, u32[]{:S(2)}) %all-to-all-start.5) | async-done | bytes 65568 | tf_op jit(solution)/shard_map/all_to_all | solution.py:123
  545.6 62.6 %psum.90 = f32[]{:T(128)} all-reduce(f32[]{:T(128)S(6)} %add.160), channel_id=1, replica_groups=mesh['lat'=32,'rad'=4] {'lat','rad'}, use_global_device_ids=true, to_apply=%region_22.23 | all-reduce | flops 1 | bytes 8 | tf_op jit(solution)/shard_map/psum | solution.py:39
  615.6 6.9 all-to-all-start.6
  627.9 4.4 all-to-all-done.6
  632.4 4.6 fusion.43
  640.0 62.7 %psum.85 = f32[]{:T(128)} all-reduce(f32[]{:T(128)} %get-tuple-element.8), channel_id=1, replica_groups=mesh['lat'=32,'rad'=4] {'lat','rad'}, use_global_device_ids=true, to_apply=%region_28.29 | all-reduce | flops 1 | bytes 8 | tf_op jit(solution)/shard_map/psum | solution.py:46
  716.7 5.6 fusion
  723.1 8.8 %all-to-all-start.7 = ((f32[128,1,128]{2,1,0:T(1,128)}), f32[128,1,128]{2,1,0:T(1,128)S(1)}, u32[]{:S(2)}, u32[]{:S(2)}) async-start(f32[128,1,128]{2,1,0:T(1,128)} %reshape.327), calls=%async_computation.7 | async-start | bytes 131072 | tf_op jit(solution)/shard_map/all_to_all | solution.py:123
  732.7 9.0 %all-to-all-done.7 = f32[128,1,128]{2,1,0:T(1,128)S(1)} async-done(((f32[128,1,128]{2,1,0:T(1,128)}), f32[128,1,128]{2,1,0:T(1,128)S(1)}, u32[]{:S(2)}, u32[]{:S(2)}) %all-to-all-start.7) | async-done | bytes 65568 | tf_op jit(solution)/shard_map/all_to_all | solution.py:123
  745.4 62.6 %psum.91 = f32[]{:T(128)} all-reduce(f32[]{:T(128)S(6)} %add.170), channel_id=1, replica_groups=mesh['lat'=32,'rad'=4] {'lat','rad'}, use_global_device_ids=true, to_apply=%region_31.32 | all-reduce | flops 1 | bytes 8 | tf_op jit(solution)/shard_map/psum | solution.py:39
  (140 shorter events, 84.4 us)
Async XLA Ops:
  6.9 81.7 %all-to-all-start = ((s32[128,1,2]{2,1,0:T(1,128)}), s32[128,1,2]{2,1,0:T(1,128)S(1)}, u32[]{:S(2)}, u32[]{:S(2)}) async-start(s32[128,1,2]{2,1,0:T(1,128)} %bitcast.2), calls=%async_computation | async-start | bytes 131072 | tf_op jit(solution)/shard_map/all_to_all | solution.py:65
  88.6 28.4 %all-to-all-start.2 = ((bf16[128,2,64]{2,1,0:T(2,128)(2,1)}), bf16[128,2,64]{2,1,0:T(2,128)(2,1)S(1)}, u32[]{:S(2)}, u32[]{:S(2)}) async-start(bf16[128,2,64]{2,1,0:T(2,128)(2,1)} %bitcast.7), calls=%async_computation.2 | async-start | bytes 131072 | tf_op jit(solution)/shard_map/all_to_all | solution.py:92
  117.0 115.0 %all-to-all-start.1 = ((bf16[128,2,64,256]{3,2,1,0:T(8,128)(2,1)}), bf16[128,2,64,256]{3,2,1,0:T(8,128)(2,1)}, u32[]{:S(2)}, u32[]{:S(2)}) async-start(bf16[128,2,64,256]{3,2,1,0:T(8,128)(2,1)} %bitcast.59), calls=%async_computation.1 | async-start | bytes 16777216 | tf_op jit(solution)/shard_map/all_to_all | solution.py:80
  236.5 107.4 %copy-start = (f32[32,64]{1,0:T(8,128)S(1)}, f32[32,64]{1,0:T(8,128)}, u32[]{:S(2)}) copy-start(f32[32,64]{1,0:T(8,128)} %param.11) | copy-start | bytes 24580
  236.5 107.4 %copy-start.1 = (f32[32,64]{1,0:T(8,128)S(1)}, f32[32,64]{1,0:T(8,128)}, u32[]{:S(2)}) copy-start(f32[32,64]{1,0:T(8,128)} %param.10) | copy-start | bytes 24580
  236.5 107.4 %copy-start.2 = (s32[32]{0:T(128)S(1)}, s32[32]{0:T(128)}, u32[]{:S(2)}) copy-start(s32[32]{0:T(128)} %param.9) | copy-start | bytes 388
  303.2 6.6 collective-permute-start
  306.4 5.0 collective-permute-start.1
  311.4 20.6 %collective-permute-start.2 = (f32[1,18,256]{2,1,0:T(8,128)S(1)}, f32[1,18,256]{2,1,0:T(8,128)S(1)}, u32[]{:S(2)}, u32[]{:S(2)}) collective-permute-start(f32[1,18,256]{2,1,0:T(8,128)S(1)} %get-tuple-element.32), channel_id=1, source_target_pairs={{1,0},{2,1},{3,2},{5,4},{6,5},{7,6},{9,8},{10,9},{11,10},{13,12},{... | collective-permute-start | bytes 55304 | tf_op jit(solution)/shard_map/ppermute | solution.py:25
  312.7 19.3 %collective-permute-start.3 = (f32[1,18,256]{2,1,0:T(8,128)S(1)}, f32[1,18,256]{2,1,0:T(8,128)S(1)}, u32[]{:S(2)}, u32[]{:S(2)}) collective-permute-start(f32[1,18,256]{2,1,0:T(8,128)S(1)} %get-tuple-element.33), channel_id=1, source_target_pairs={{0,1},{1,2},{2,3},{4,5},{5,6},{6,7},{8,9},{9,10},{10,11},{12,13},{... | collective-permute-start | bytes 55304 | tf_op jit(solution)/shard_map/ppermute | solution.py:23
  323.2 18.5 %all-to-all-start.3 = ((f32[128,1,128]{2,1,0:T(1,128)}), f32[128,1,128]{2,1,0:T(1,128)S(1)}, u32[]{:S(2)}, u32[]{:S(2)}) async-start(f32[128,1,128]{2,1,0:T(1,128)} %reshape.323), calls=%async_computation.3 | async-start | bytes 131072 | tf_op jit(solution)/shard_map/all_to_all | solution.py:123
  409.2 13.6 %collective-permute-start.4 = (f32[8,1,256]{2,1,0:T(1,128)S(1)}, f32[8,1,256]{2,1,0:T(1,128)S(1)}, u32[]{:S(2)}, u32[]{:S(2)}) collective-permute-start(f32[8,1,256]{2,1,0:T(1,128)S(1)} %get-tuple-element.41), channel_id=1, source_target_pairs={{0,4},{4,8},{8,12},{12,16},{16,20},{20,24},{24,28},{28,32},{32,36}... | collective-permute-start | bytes 24584 | tf_op jit(solution)/shard_map/ppermute | solution.py:23
  412.2 10.6 %collective-permute-start.5 = (f32[8,1,256]{2,1,0:T(1,128)S(1)}, f32[8,1,256]{2,1,0:T(1,128)S(1)}, u32[]{:S(2)}, u32[]{:S(2)}) collective-permute-start(f32[8,1,256]{2,1,0:T(1,128)S(1)} %get-tuple-element.40), channel_id=1, source_target_pairs={{4,0},{8,4},{12,8},{16,12},{20,16},{24,20},{28,24},{32,28},{36,32}... | collective-permute-start | bytes 24584 | tf_op jit(solution)/shard_map/ppermute | solution.py:25
  415.9 16.8 %all-to-all-start.4 = ((bf16[128,2,64]{2,1,0:T(2,128)(2,1)}), bf16[128,2,64]{2,1,0:T(2,128)(2,1)S(1)}, u32[]{:S(2)}, u32[]{:S(2)}) async-start(bf16[128,2,64]{2,1,0:T(2,128)(2,1)} %bitcast.18), calls=%async_computation.4 | async-start | bytes 131072 | tf_op jit(solution)/shard_map/all_to_all | solution.py:92
  422.9 16.6 %collective-permute-start.6 = (f32[1,18,256]{2,1,0:T(8,128)S(1)}, f32[1,18,256]{2,1,0:T(8,128)S(1)}, u32[]{:S(2)}, u32[]{:S(2)}) collective-permute-start(f32[1,18,256]{2,1,0:T(8,128)S(1)} %get-tuple-element.30), channel_id=1, source_target_pairs={{1,0},{2,1},{3,2},{5,4},{6,5},{7,6},{9,8},{10,9},{11,10},{13,12},{... | collective-permute-start | bytes 55304 | tf_op jit(solution)/shard_map/ppermute | solution.py:25
  424.2 15.3 %collective-permute-start.7 = (f32[1,18,256]{2,1,0:T(8,128)S(1)}, f32[1,18,256]{2,1,0:T(8,128)S(1)}, u32[]{:S(2)}, u32[]{:S(2)}) collective-permute-start(f32[1,18,256]{2,1,0:T(8,128)S(1)} %get-tuple-element.31), channel_id=1, source_target_pairs={{0,1},{1,2},{2,3},{4,5},{5,6},{6,7},{8,9},{9,10},{10,11},{12,13},{... | collective-permute-start | bytes 55304 | tf_op jit(solution)/shard_map/ppermute | solution.py:23
  503.6 6.4 collective-permute-start.8
  506.6 5.0 collective-permute-start.9
  511.6 20.6 %collective-permute-start.10 = (f32[1,18,256]{2,1,0:T(8,128)S(1)}, f32[1,18,256]{2,1,0:T(8,128)S(1)}, u32[]{:S(2)}, u32[]{:S(2)}) collective-permute-start(f32[1,18,256]{2,1,0:T(8,128)S(1)} %get-tuple-element.28), channel_id=1, source_target_pairs={{1,0},{2,1},{3,2},{5,4},{6,5},{7,6},{9,8},{10,9},{11,10},{13,12},{... | collective-permute-start | bytes 55304 | tf_op jit(solution)/shard_map/ppermute | solution.py:25
  512.9 19.3 %collective-permute-start.11 = (f32[1,18,256]{2,1,0:T(8,128)S(1)}, f32[1,18,256]{2,1,0:T(8,128)S(1)}, u32[]{:S(2)}, u32[]{:S(2)}) collective-permute-start(f32[1,18,256]{2,1,0:T(8,128)S(1)} %get-tuple-element.29), channel_id=1, source_target_pairs={{0,1},{1,2},{2,3},{4,5},{5,6},{6,7},{8,9},{9,10},{10,11},{12,13},{... | collective-permute-start | bytes 55304 | tf_op jit(solution)/shard_map/ppermute | solution.py:23
  523.4 18.7 %all-to-all-start.5 = ((f32[128,1,128]{2,1,0:T(1,128)}), f32[128,1,128]{2,1,0:T(1,128)S(1)}, u32[]{:S(2)}, u32[]{:S(2)}) async-start(f32[128,1,128]{2,1,0:T(1,128)} %reshape.325), calls=%async_computation.5 | async-start | bytes 131072 | tf_op jit(solution)/shard_map/all_to_all | solution.py:123
  609.0 13.6 %collective-permute-start.12 = (f32[8,1,256]{2,1,0:T(1,128)S(1)}, f32[8,1,256]{2,1,0:T(1,128)S(1)}, u32[]{:S(2)}, u32[]{:S(2)}) collective-permute-start(f32[8,1,256]{2,1,0:T(1,128)S(1)} %get-tuple-element.37), channel_id=1, source_target_pairs={{0,4},{4,8},{8,12},{12,16},{16,20},{20,24},{24,28},{28,32},{32,36}... | collective-permute-start | bytes 24584 | tf_op jit(solution)/shard_map/ppermute | solution.py:23
  612.0 10.6 %collective-permute-start.13 = (f32[8,1,256]{2,1,0:T(1,128)S(1)}, f32[8,1,256]{2,1,0:T(1,128)S(1)}, u32[]{:S(2)}, u32[]{:S(2)}) collective-permute-start(f32[8,1,256]{2,1,0:T(1,128)S(1)} %get-tuple-element.36), channel_id=1, source_target_pairs={{4,0},{8,4},{12,8},{16,12},{20,16},{24,20},{28,24},{32,28},{36,32}... | collective-permute-start | bytes 24584 | tf_op jit(solution)/shard_map/ppermute | solution.py:25
  615.6 16.8 %all-to-all-start.6 = ((bf16[128,2,64]{2,1,0:T(2,128)(2,1)}), bf16[128,2,64]{2,1,0:T(2,128)(2,1)S(1)}, u32[]{:S(2)}, u32[]{:S(2)}) async-start(bf16[128,2,64]{2,1,0:T(2,128)(2,1)} %bitcast.29), calls=%async_computation.6 | async-start | bytes 131072 | tf_op jit(solution)/shard_map/all_to_all | solution.py:92
  622.6 16.6 %collective-permute-start.14 = (f32[1,18,256]{2,1,0:T(8,128)S(1)}, f32[1,18,256]{2,1,0:T(8,128)S(1)}, u32[]{:S(2)}, u32[]{:S(2)}) collective-permute-start(f32[1,18,256]{2,1,0:T(8,128)S(1)} %get-tuple-element.26), channel_id=1, source_target_pairs={{1,0},{2,1},{3,2},{5,4},{6,5},{7,6},{9,8},{10,9},{11,10},{13,12},{... | collective-permute-start | bytes 55304 | tf_op jit(solution)/shard_map/ppermute | solution.py:25
  623.9 15.3 %collective-permute-start.15 = (f32[1,18,256]{2,1,0:T(8,128)S(1)}, f32[1,18,256]{2,1,0:T(8,128)S(1)}, u32[]{:S(2)}, u32[]{:S(2)}) collective-permute-start(f32[1,18,256]{2,1,0:T(8,128)S(1)} %get-tuple-element.27), channel_id=1, source_target_pairs={{0,1},{1,2},{2,3},{4,5},{5,6},{6,7},{8,9},{9,10},{10,11},{12,13},{... | collective-permute-start | bytes 55304 | tf_op jit(solution)/shard_map/ppermute | solution.py:23
  703.4 6.4 collective-permute-start.16
  706.4 5.0 collective-permute-start.17
  711.4 20.6 %collective-permute-start.18 = (f32[1,18,256]{2,1,0:T(8,128)S(1)}, f32[1,18,256]{2,1,0:T(8,128)S(1)}, u32[]{:S(2)}, u32[]{:S(2)}) collective-permute-start(f32[1,18,256]{2,1,0:T(8,128)S(1)} %get-tuple-element.24), channel_id=1, source_target_pairs={{1,0},{2,1},{3,2},{5,4},{6,5},{7,6},{9,8},{10,9},{11,10},{13,12},{... | collective-permute-start | bytes 55304 | tf_op jit(solution)/shard_map/ppermute | solution.py:25
  712.7 19.3 %collective-permute-start.19 = (f32[1,18,256]{2,1,0:T(8,128)S(1)}, f32[1,18,256]{2,1,0:T(8,128)S(1)}, u32[]{:S(2)}, u32[]{:S(2)}) collective-permute-start(f32[1,18,256]{2,1,0:T(8,128)S(1)} %get-tuple-element.25), channel_id=1, source_target_pairs={{0,1},{1,2},{2,3},{4,5},{5,6},{6,7},{8,9},{9,10},{10,11},{12,13},{... | collective-permute-start | bytes 55304 | tf_op jit(solution)/shard_map/ppermute | solution.py:23
  723.1 18.6 %all-to-all-start.7 = ((f32[128,1,128]{2,1,0:T(1,128)}), f32[128,1,128]{2,1,0:T(1,128)S(1)}, u32[]{:S(2)}, u32[]{:S(2)}) async-start(f32[128,1,128]{2,1,0:T(1,128)} %reshape.327), calls=%async_computation.7 | async-start | bytes 131072 | tf_op jit(solution)/shard_map/all_to_all | solution.py:123
where the time goes:
time: 821 us; the launch traced here: 811 us
  blocking collectives  443 us (54%)
  waiting for transfers between devices  144 us (18%)
  starting transfers between devices  118 us (14%)
  local copies, waits for them, and re-layouts  42.7 us (5%)
  matrix products  30.6 us (4%)
  other arithmetic  21.3 us (3%)
  between operations  11 us (1%)
    psum x4, blocking collectives, data_norm(): lax.psum((jnp.sum(data_vector * data_vector), jnp.sum(pen_vec * pen_vec))...  255 us
    psum x3, blocking collectives, model_norm(): return jnp.sqrt(lax.psum(jnp.sum(model_dir * model_dir), ('lat', 'rad')))  188 us
    all_to_all x1, waiting for transfers between devices, body(): lax.all_to_all(outgoing.reshape(devices, capacity, ray_len, cell_len), ('...  103 us
    ppermute x10, starting transfers between devices, extended(): lax.ppermute(tail, axis, [(i, (i + 1) % count) for i in range(ends)])  35.3 us
    all_to_all x3, waiting for transfers between devices, body(): lax.all_to_all(products, ('lat', 'rad'), split_axis=0, concat_axis=0, til...  27.3 us
    all_to_all x3, starting transfers between devices, body(): lax.all_to_all(products, ('lat', 'rad'), split_axis=0, concat_axis=0, til...  26.4 us
    scatter x1, local copies, waits for them, and re-layouts, body(): outgoing.at[position].set(kernel.reshape(entries, ray_len, cell_len))  19.3 us
    all_to_all x3, starting transfers between devices, adjoint(): lax.all_to_all(spread.reshape(devices, capacity, ray_len), ('lat', 'rad')...  18.6 us
  transfers between devices with their start and end apart: 28, of which 9 were waited for; matrix products, arithmetic and copies ran while one was open for 9% of the time, Pallas kernels for 0%

commit v1 on v0

v1 whole, which is shorter than its diff:
```python
import functools

import jax
import jax.numpy as jnp
from jax import lax
from jax.experimental import pallas as pl
from jax.experimental.pallas import tpu as pltpu
from jax.sharding import PartitionSpec as P

ITERS = 3
MB_R = 8
MB_L = 16
FREEDOM = 4.0
DAMPING = 0.3

AXES = ("lat", "rad")
CHUNK = 8
NORM_ROW = 4
ID_ROW = 5
LANES = 128

F32 = jnp.float32
BF16 = jnp.bfloat16
NT = (((1,), (1,)), ((), ()))


def iota(shape, dim):
    return lax.broadcasted_iota(jnp.int32, shape, dim)


def matmul(a, b):
    return jnp.dot(a, b, preferred_element_type=F32)


def total(x):
    return jnp.sum(jnp.sum(x, axis=1, keepdims=True), axis=0, keepdims=True)


def norm_row(partial):
    high = partial.astype(BF16).astype(F32)
    middle = (partial - high).astype(BF16).astype(F32)
    low = partial - high - middle
    lane = iota((1, LANES), 1)
    return jnp.where(lane == 0, high, jnp.where(lane == 1, middle, jnp.where(lane == 2, low, 0.0)))


def with_norm(packed, partial):
    rows = iota(packed.shape, 0) % CHUNK
    return jnp.where(rows == NORM_ROW, norm_row(partial), packed).astype(BF16)


def received_norm(received):
    rows = received.shape[0]
    picks = jnp.where(iota((8, rows), 1) % CHUNK == NORM_ROW, 1.0, 0.0).astype(BF16)
    sums = matmul(picks, received)[0:1, :]
    return jnp.sqrt(jnp.sum(jnp.where(iota((1, LANES), 1) < 3, sums, 0.0), axis=1, keepdims=True))


def stacked(x):
    return jnp.concatenate([x[:, :LANES], x[:, LANES:]], axis=0)


def unstacked(x):
    half = x.shape[0] // 2
    return jnp.concatenate([x[:half], x[half:]], axis=1)


def adjoint_products(kernel_ref, y, out_ref, ray_blocks, fanout):
    high = y.astype(BF16).astype(F32)
    low = y - high
    high = jnp.concatenate([high] * fanout, axis=1)
    low = jnp.concatenate([low] * fanout, axis=1)
    width = high.shape[1]
    ray_len = width // fanout
    row, lane = iota((2 * fanout, width), 0), iota((2 * fanout, width), 1)
    own = lane // ray_len == row % fanout
    for b in range(ray_blocks):
        lhs = jnp.where(row < fanout, high[b : b + 1], low[b : b + 1])
        lhs = jnp.where(own, lhs, 0.0).astype(BF16)
        both = matmul(lhs, kernel_ref[b * width : (b + 1) * width, :])
        out_ref[b * fanout : (b + 1) * fanout, :] = both[:fanout] + both[fanout:]


def forward_products(kernel_ref, blocks, ray_blocks, fanout, ray_len):
    entries = ray_blocks * fanout
    lane = iota((ray_len, entries), 1)
    picked = jnp.zeros((ray_len, entries), F32)
    group = 16
    for start in range(0, entries, group):
        products = lax.dot_general(
            kernel_ref[start * ray_len : (start + group) * ray_len, :], blocks, NT, preferred_element_type=F32
        )
        for i in range(group):
            picked = jnp.where(lane == start + i, products[i * ray_len : (i + 1) * ray_len], picked)
    member = jnp.where(iota((ray_blocks, entries), 1) // fanout == iota((ray_blocks, entries), 0), 1.0, 0.0)
    return lax.dot_general(member, picked, NT, preferred_element_type=F32, precision=lax.Precision.HIGHEST)


def roughen(field, up, down, left, right):
    rows = field.shape[0]
    place = iota(field.shape, 0) % MB_L
    spread = lambda side: jnp.concatenate(
        [jnp.broadcast_to(side[r : r + 1], (MB_L, side.shape[1])) for r in range(MB_R)], axis=0
    )
    north = jnp.concatenate([up, field[: rows - MB_L]], axis=0)
    south = jnp.concatenate([field[MB_L:], down], axis=0)
    west = jnp.where(place == 0, spread(left), pltpu.roll(field, 1, 0))
    east = jnp.where(place == MB_L - 1, spread(right), pltpu.roll(field, rows - 1, 0))
    return 4.0 * field - (south + north + east + west)


def write_edges(field, first, last, lefts, rights):
    rows = field.shape[0]
    first[...] = field[:MB_L]
    last[...] = field[rows - MB_L :]
    for r in range(MB_R):
        lefts[r : r + 1, :] = field[r * MB_L : r * MB_L + 1]
        rights[r : r + 1, :] = field[(r + 1) * MB_L - 1 : (r + 1) * MB_L]


def start_kernel(
    kernel_ref, device_ref, block_ref, counts_ref, times_ref, prior_ref,
    send_ref, weights_ref, data_ref, pick_ref, place_ref, partial_ref,
):
    ray_blocks, fanout = device_ref.shape
    ray_len = times_ref.shape[1]
    entries = ray_blocks * fanout
    rows = send_ref.shape[0]

    member = jnp.where(iota((entries, ray_blocks), 0) // fanout == iota((entries, ray_blocks), 1), 1.0, 0.0)
    turn = iota((entries, fanout), 0) % fanout == iota((entries, fanout), 1)

    def column(table_ref):
        spread = matmul(member.astype(BF16), table_ref[...].astype(F32).astype(BF16))
        return jnp.sum(jnp.where(turn, spread, 0.0), axis=1, keepdims=True)

    diagonal = iota((entries, entries), 0) == iota((entries, entries), 1)

    def as_row(col):
        return jnp.sum(jnp.where(diagonal, col, 0.0), axis=0, keepdims=True)

    target = column(device_ref)
    block = column(block_ref)
    target_row = as_row(target)
    earlier = iota((entries, entries), 1) < iota((entries, entries), 0)
    rank = jnp.sum(jnp.where(earlier & (target == target_row), 1.0, 0.0), axis=1, keepdims=True)
    first = target * CHUNK + 2.0 * rank
    first_row = as_row(first)

    to_col = jnp.concatenate([first, first + 1.0], axis=0).astype(jnp.int32)
    pick_ref[...] = jnp.where(iota((2 * entries, rows), 1) == to_col, 1.0, 0.0).astype(BF16)
    to_row = jnp.concatenate([first_row, first_row + 1.0], axis=1).astype(jnp.int32)
    place_ref[...] = jnp.where(iota((rows, 2 * entries), 0) == to_row, 1.0, 0.0).astype(BF16)

    same = iota((ray_blocks, ray_blocks), 0) == iota((ray_blocks, ray_blocks), 1)
    counts = jnp.sum(jnp.where(same, counts_ref[...].astype(F32), 0.0), axis=1, keepdims=True)
    mask = jnp.where(iota((ray_blocks, ray_len), 1).astype(F32) < counts, 1.0, 0.0)
    prior = prior_ref[...]
    weights = mask * jnp.sqrt((FREEDOM + 1.0) / (FREEDOM + prior * prior))
    weights_ref[...] = weights
    data = weights * times_ref[...]
    data_ref[...] = data

    adjoint_products(kernel_ref, weights * data, partial_ref, ray_blocks, fanout)
    ids = jnp.where(iota((entries, LANES), 1).astype(F32) == rank, block + 1.0, 0.0).astype(BF16)
    id_rows = (target_row * CHUNK + ID_ROW).astype(jnp.int32)
    id_place = jnp.where(iota((rows, entries), 0) == id_rows, 1.0, 0.0).astype(BF16)
    packed = matmul(place_ref[...], stacked(partial_ref[...].astype(BF16))) + matmul(id_place, ids)
    send_ref[...] = with_norm(packed, total(data * data))


def scalars_row(*values):
    lane = iota((8, LANES), 1)
    out = jnp.zeros((8, LANES), F32)
    for i, value in enumerate(values):
        out = jnp.where(lane == i, value, out)
    return out


def first_model_kernel(
    received_ref,
    send_ref, field_ref, scalar_ref, gather_ref, scatter_ref, first_ref, last_ref, left_ref, right_ref,
):
    received = received_ref[...]
    rows = received.shape[0]
    devices = rows // CHUNK
    blocks = MB_R * MB_L
    pick = jnp.where(iota((devices, rows), 1) == iota((devices, rows), 0) * CHUNK + ID_ROW, 1.0, 0.0).astype(BF16)
    ids = matmul(pick, received).astype(BF16)
    owner = jnp.where(iota((rows, devices), 0) // CHUNK == iota((rows, devices), 1), 1.0, 0.0).astype(BF16)
    spread = matmul(owner, ids)
    place = iota((rows, LANES), 0) % CHUNK
    slot = (place < NORM_ROW) & (iota((rows, LANES), 1) == place // 2)
    ident = jnp.sum(jnp.where(slot, spread, 0.0), axis=1, keepdims=True) - 1.0
    wide = jnp.broadcast_to(ident, (rows, LANES))
    lane = iota((rows, LANES), 1)
    hit = wide == lane.astype(F32)
    for half in range(2):
        chosen = jnp.where(hit & (place % 2 == half), 1.0, 0.0)
        gather_ref[:, half * LANES : (half + 1) * LANES] = chosen.astype(BF16)
        scatter_ref[half * blocks : (half + 1) * blocks, :] = chosen.T.astype(BF16)

    beta = received_norm(received)
    field = unstacked(matmul(scatter_ref[...], received)) / beta
    field_ref[...] = field
    write_edges(field, first_ref, last_ref, left_ref, right_ref)
    scalar_ref[...] = scalars_row(beta)
    send_ref[...] = with_norm(matmul(gather_ref[...], stacked(field.astype(BF16))), total(field * field))


def ray_step(
    sweep, received_ref, kernel_ref, pick_ref, weights_ref, data_ref, field_ref, scalar_ref,
    up_ref, down_ref, west_ref, east_ref, pen_ref, search_ref, state_ref,
):
    received = received_ref[...]
    ray_blocks, ray_len = data_ref.shape
    fanout = pick_ref.shape[0] // 2 // ray_blocks
    alpha = received_norm(received)
    blocks = unstacked(matmul(pick_ref[...], received)).astype(BF16)
    products = forward_products(kernel_ref, blocks, ray_blocks, fanout, ray_len)
    beta = scalar_ref[0:1, 0:1]
    data = weights_ref[...] * (products / alpha) - alpha * (data_ref[...] / beta)
    field = field_ref[...]
    pen = DAMPING * (roughen(field, up_ref[...], down_ref[...], west_ref[...], east_ref[...]) / alpha)
    if sweep:
        pen = pen - alpha * (pen_ref[...] / beta)
    direction = field / alpha
    if sweep:
        phi_bar, rho, cosine, sine = [state_ref[0:1, i : i + 1] for i in range(4)]
        search = direction - (sine * alpha / rho) * search_ref[...]
        rho_bar = -cosine * alpha
    else:
        phi_bar, rho_bar = beta, alpha
        search = direction
    partial = total(data * data) + total(pen * pen)
    return data, pen, direction, search, phi_bar, rho_bar, partial


def ray_kernel(sweep, *refs):
    inputs = 15 if sweep else 12
    if sweep:
        (received_ref, kernel_ref, pick_ref, place_ref, weights_ref, data_ref, field_ref, scalar_ref,
         up_ref, down_ref, west_ref, east_ref, pen_ref, search_ref, state_ref) = refs[:inputs]
    else:
        (received_ref, kernel_ref, pick_ref, place_ref, weights_ref, data_ref, field_ref, scalar_ref,
         up_ref, down_ref, west_ref, east_ref) = refs[:inputs]
        pen_ref = search_ref = state_ref = None
    (send_ref, data_out, pen_out, direction_out, search_out, state_out,
     first_ref, last_ref, left_ref, right_ref, partial_ref) = refs[inputs:]
    data, pen, direction, search, phi_bar, rho_bar, partial = ray_step(
        sweep, received_ref, kernel_ref, pick_ref, weights_ref, data_ref, field_ref, scalar_ref,
        up_ref, down_ref, west_ref, east_ref, pen_ref, search_ref, state_ref,
    )
    data_out[...] = data
    pen_out[...] = pen
    direction_out[...] = direction
    search_out[...] = search
    state_out[...] = scalars_row(phi_bar, rho_bar)
    write_edges(pen, first_ref, last_ref, left_ref, right_ref)
    ray_blocks = data.shape[0]
    fanout = pick_ref.shape[0] // 2 // ray_blocks
    adjoint_products(kernel_ref, weights_ref[...] * data, partial_ref, ray_blocks, fanout)
    send_ref[...] = with_norm(matmul(place_ref[...], stacked(partial_ref[...].astype(BF16))), partial)


def last_ray_kernel(
    sweep, received_ref, kernel_ref, pick_ref, weights_ref, data_ref, field_ref, scalar_ref,
    up_ref, down_ref, west_ref, east_ref, pen_ref, search_ref, state_ref,
    send_ref, data_out, search_out, state_out,
):
    data, pen, direction, search, phi_bar, rho_bar, partial = ray_step(
        sweep, received_ref, kernel_ref, pick_ref, weights_ref, data_ref, field_ref, scalar_ref,
        up_ref, down_ref, west_ref, east_ref, pen_ref, search_ref, state_ref,
    )
    data_out[...] = data
    search_out[...] = search
    state_out[...] = scalars_row(phi_bar, rho_bar)
    send_ref[...] = jnp.broadcast_to(partial, send_ref.shape)


def rotate(beta, state_ref):
    phi_bar, rho_bar = state_ref[0:1, 0:1], state_ref[0:1, 1:2]
    rho = jnp.sqrt(rho_bar * rho_bar + beta * beta)
    cosine, sine = rho_bar / rho, beta / rho
    return cosine * phi_bar / rho, sine * phi_bar, rho, cosine, sine


def model_kernel(
    sweep, received_ref, scatter_ref, gather_ref, pen_ref, direction_ref, search_ref, update_ref, state_ref,
    up_ref, down_ref, west_ref, east_ref,
    send_ref, field_ref, scalar_ref, update_out, state_out, first_ref, last_ref, left_ref, right_ref,
):
    received = received_ref[...]
    beta = received_norm(received)
    gathered = unstacked(matmul(scatter_ref[...], received))
    rough = roughen(pen_ref[...], up_ref[...], down_ref[...], west_ref[...], east_ref[...])
    field = (gathered + DAMPING * rough) / beta - beta * direction_ref[...]
    field_ref[...] = field
    write_edges(field, first_ref, last_ref, left_ref, right_ref)
    send_ref[...] = with_norm(matmul(gather_ref[...], stacked(field.astype(BF16))), total(field * field))
    scalar_ref[...] = scalars_row(beta)
    step, phi_bar, rho, cosine, sine = rotate(beta, state_ref)
    update = step * search_ref[...]
    update_out[...] = update if sweep == 0 else update_ref[...] + update
    state_out[...] = scalars_row(phi_bar, rho, cosine, sine)


def last_kernel(norms_ref, data_ref, search_ref, update_ref, state_ref, update_out, data_out):
    beta = jnp.sqrt(jnp.sum(norms_ref[...], axis=0, keepdims=True)[:, 0:1])
    step = rotate(beta, state_ref)[0]
    update_out[...] = update_ref[...] + step * search_ref[...]
    data_out[...] = data_ref[...] / beta


def call(kernel, name, outputs, scratch, operands, flops=0):
    bytes_accessed = sum(x.size * x.dtype.itemsize for x in operands)
    return pl.pallas_call(
        kernel,
        name=name,
        out_shape=[jax.ShapeDtypeStruct(shape, dtype) for shape, dtype in outputs],
        in_specs=[pl.BlockSpec(memory_space=pltpu.VMEM)] * len(operands),
        out_specs=[pl.BlockSpec(memory_space=pltpu.VMEM)] * len(outputs),
        scratch_shapes=scratch,
        compiler_params=pltpu.CompilerParams(vmem_limit_bytes=40 << 20),
        cost_estimate=pl.CostEstimate(flops=flops, bytes_accessed=bytes_accessed, transcendentals=0),
    )(*operands)


def exchange(packed, devices):
    rows, lanes = packed.shape
    chunks = packed.reshape(devices, rows // devices, lanes)
    return lax.all_to_all(chunks, AXES, split_axis=0, concat_axis=0, tiled=True).reshape(rows, lanes)


def halos(first, last, left, right):
    def shift(x, axis, step):
        count = lax.axis_size(axis)
        pairs = [(i, i + step) for i in range(count) if 0 <= i + step < count]
        return lax.ppermute(x, axis, pairs)
    return shift(last, "rad", 1), shift(first, "rad", -1), shift(right, "lat", 1), shift(left, "lat", -1)


def body(kernel, target_device, target_block, counts, traveltimes, prior_residual):
    devices = lax.axis_size("lat") * lax.axis_size("rad")
    ray_blocks, fanout, ray_len, cells = kernel.shape
    entries = ray_blocks * fanout
    rows = devices * CHUNK
    blocks = MB_R * MB_L
    tiles = kernel.reshape(entries * ray_len, cells)
    flops = 4 * entries * ray_len * cells

    packet = ((rows, LANES), BF16)
    ray = ((ray_blocks, ray_len), F32)
    model = ((blocks, cells), F32)
    scalar = ((8, LANES), F32)
    edges = [((MB_L, cells), F32)] * 2 + [((MB_R, cells), F32)] * 2
    partials = [pltpu.VMEM((entries, cells), F32)]

    send, weights, data, pick, place = call(
        start_kernel, "start",
        [packet, ray, ray, ((2 * entries, rows), BF16), ((rows, 2 * entries), BF16)], partials,
        (tiles, target_device, target_block, counts.reshape(1, ray_blocks), traveltimes, prior_residual), flops,
    )
    received = exchange(send, devices)
    send, field, scalars, gather, scatter, *edge = call(
        first_model_kernel, "first_model",
        [packet, model, scalar, ((rows, 2 * blocks), BF16), ((2 * blocks, rows), BF16)] + edges, [],
        (received,), flops,
    )
    pen = search = update = state = None
    for sweep in range(ITERS):
        around = halos(*edge)
        received = exchange(send, devices)
        carried = (pen, search, state) if sweep else ()
        if sweep == ITERS - 1:
            send, data, search, state = call(
                functools.partial(last_ray_kernel, sweep), "last_ray",
                [((devices, LANES), F32), ray, model, scalar], [],
                (received, tiles, pick, weights, data, field, scalars, *around, *carried), flops,
            )
            norms = lax.all_to_all(
                send.reshape(devices, 1, LANES), AXES, split_axis=0, concat_axis=0, tiled=True
            ).reshape(devices, LANES)
            update, data = call(last_kernel, "last", [model, ray], [], (norms, data, search, update, state))
            break
        send, data, pen, direction, search, state, *edge = call(
            functools.partial(ray_kernel, sweep), "ray",
            [packet, ray, model, model, model, scalar] + edges, partials,
            (received, tiles, pick, place, weights, data, field, scalars, *around, *carried), flops,
        )
        around = halos(*edge)
        received = exchange(send, devices)
        before = update if sweep else search
        send, field, scalars, update, state, *edge = call(
            functools.partial(model_kernel, sweep), "model",
            [packet, model, scalar, model, scalar] + edges, [],
            (received, scatter, gather, pen, direction, search, before, state, *around), flops,
        )
    return (update.reshape(MB_R, MB_L, cells), data)


def solution(mesh):
    in_specs = (
        P(("lat", "rad"), None, None, None),
        P(("lat", "rad"), None),
        P(("lat", "rad"), None),
        P(("lat", "rad")),
        P(("lat", "rad"), None),
        P(("lat", "rad"), None),
    )
    out_specs = (P("rad", "lat", None), P(("lat", "rad"), None))
    return jax.shard_map(body, mesh=mesh, in_specs=in_specs, out_specs=out_specs, check_vma=False)
```

time: 821 us -> 190 us (0.23); the launches traced: 811 us -> 189 us
  blocking collectives: 443 us -> 43.6 us
  waiting for transfers between devices: 144 us -> 15 us
  matrix products: 30.6 us -> 0 us
  local copies, waits for them, and re-layouts: 42.7 us -> 12.3 us
  other arithmetic: 21.3 us -> 0 us
  starting transfers between devices: 118 us -> 101 us
  Pallas kernels: 0 us -> 16.2 us
  between operations: 11 us -> 0.94 us
    psum x7 -> x0, blocking collectives: 443 us -> none  [the longest x4 255 us: data_norm(): lax.psum((jnp.sum(data_vector * data_vector), jnp.sum(pen_vec * pen_vec))...]
    all_to_all x8 -> x5, waiting for transfers between devices: 139 us -> 0.01 us  [exchange(): lax.all_to_all(chunks, AXES, split_axis=0, concat_axis=0, tiled=True)]
    all_to_all x0 -> x2, blocking collectives: none -> 43.6 us  [the longest x1 22.6 us: exchange(): lax.all_to_all(chunks, AXES, split_axis=0, concat_axis=0, tiled=True)]
    dot_general x6 -> x0, matrix products: 30.6 us -> none  [the longest x3 16.9 us: body(): jnp.einsum('sqrc,sqc->sqr', held_tiles, blocks, preferred_element_type=jn...]
    scatter x5 -> x0, local copies, waits for them, and re-layouts: 24.7 us -> none  [the longest x1 19.3 us: body(): outgoing.at[position].set(kernel.reshape(entries, ray_len, cell_len))]
    all_to_all x8 -> x5, starting transfers between devices: 66.7 us -> 49.1 us  [exchange(): lax.all_to_all(chunks, AXES, split_axis=0, concat_axis=0, tiled=True)]
    pallas_call x0 -> x8, Pallas kernels: none -> 16.2 us  [call(): pl.pallas_call(kernel, name=name, out_shape=[jax.ShapeDtypeStruct(shape,...]
    ppermute x20, waiting for transfers between devices: 4.78 us -> 15 us  [shift(): return lax.ppermute(x, axis, pairs)]
  transfers between devices with their start and end apart: 28 -> 25, of which waited for: 9 -> 5; matrix products, arithmetic and copies ran while one was open for 9% -> 0% of each run, Pallas kernels for 0% -> 0%
where the time goes in v1:
time: 190 us; the launch traced here: 189 us
  starting transfers between devices  101 us (53%)
  blocking collectives  43.6 us (23%)
  Pallas kernels  16.2 us (9%)
  waiting for transfers between devices  15 us (8%)
  local copies, waits for them, and re-layouts  12.3 us (6%)
    ppermute x20, starting transfers between devices, shift(): return lax.ppermute(x, axis, pairs)  51.7 us
    all_to_all x5, starting transfers between devices, exchange(): lax.all_to_all(chunks, AXES, split_axis=0, concat_axis=0, tiled=True)  49.1 us
    all_to_all x1, blocking collectives, exchange(): lax.all_to_all(chunks, AXES, split_axis=0, concat_axis=0, tiled=True)  22.6 us
    all_to_all x1, blocking collectives, body(): lax.all_to_all(send.reshape(devices, 1, LANES), AXES, split_axis=0, conca...  21 us
    pallas_call x8, Pallas kernels, call(): pl.pallas_call(kernel, name=name, out_shape=[jax.ShapeDtypeStruct(shape,...  16.2 us
    ppermute x20, waiting for transfers between devices, shift(): return lax.ppermute(x, axis, pairs)  15 us
    unnamed x16, local copies, waits for them, and re-layouts  12.3 us
  transfers between devices with their start and end apart: 25, of which 5 were waited for; matrix products, arithmetic and copies ran while one was open for 0% of the time, Pallas kernels for 0%

profile of v1, /device:TPU:1, one launch (start us, length us, event | category | flops | bytes accessed | tf_op | source)
XLA Modules:
  0.0 189.0 jit_solution(13017307039560309880)
XLA Ops:
  2.2 2.2 %copy-done = bf16[32,4,64,256]{3,2,1,0:T(8,128)(2,1)S(1)} copy-done((bf16[32,4,64,256]{3,2,1,0:T(8,128)(2,1)S(1)}, bf16[32,4,64,256]{3,2,1,0:T(8,128)(2,1)}, u32[]{:S(2)}) %copy-start) | copy-done | bytes 4194328
  7.6 22.6 %all_to_all.35 = bf16[128,8,128]{2,1,0:T(8,128)(2,1)S(1)} all-to-all(bf16[128,8,128]{2,1,0:T(8,128)(2,1)S(1)} %bitcast.29), channel_id=1, replica_groups=mesh['lat'=32,'rad'=4] {'lat','rad'}, dimensions={0} | all-to-all | bytes 524288 | tf_op jit(solution)/shard_map/all_to_all | solution.py:332
  30.3 2.0 %first_model.1 = (bf16[1024,128]{1,0:T(8,128)(2,1)}, f32[128,256]{1,0:T(8,128)S(1)}, f32[8,128]{1,0:T(8,128)S(1)}, bf16[1024,256]{1,0:T(8,128)(2,1)S(1)}, bf16[2...) custom-call(bf16[1024,128]{1,0:T(8,128)(2,1)S(1)} %bitcast.27), custom_call_target="tpu_custom_call" | custom-call | flops 8388608 | bytes 262144 | tf_op jit(solution)/shard_map/first_model/pallas_call | solution.py:317
  32.3 3.9 %all-to-all-start.1 = ((bf16[128,8,128]{2,1,0:T(8,128)(2,1)}), bf16[128,8,128]{2,1,0:T(8,128)(2,1)S(1)}, u32[]{:S(2)}, u32[]{:S(2)}) async-start(bf16[128,8,128]{2,1,0:T(8,128)(2,1)} %bitcast.4), calls=%async_computation.1 | async-start | bytes 524288 | tf_op jit(solution)/shard_map/all_to_all | solution.py:332
  36.1 3.3 %collective-permute-start = (f32[16,256]{1,0:T(8,128)S(1)}, f32[16,256]{1,0:T(8,128)S(1)}, u32[]{:S(2)}, u32[]{:S(2)}) collective-permute-start(f32[16,256]{1,0:T(8,128)S(1)} %get-tuple-element.68), channel_id=1, source_target_pairs={{0,1},{1,2},{2,3},{4,5},{5,6},{6,7},{8,9},{9,10},{10,11},{12,13},{... | collective-permute-start | bytes 49160 | tf_op jit(solution)/shard_map/ppermute | solution.py:339
  40.7 3.8 %collective-permute-start.2 = (f32[8,256]{1,0:T(8,128)S(1)}, f32[8,256]{1,0:T(8,128)S(1)}, u32[]{:S(2)}, u32[]{:S(2)}) collective-permute-start(f32[8,256]{1,0:T(8,128)S(1)} %get-tuple-element.70), channel_id=1, source_target_pairs={{0,4},{4,8},{8,12},{12,16},{16,20},{20,24},{24,28},{28,32},{32,36}... | collective-permute-start | bytes 24584 | tf_op jit(solution)/shard_map/ppermute | solution.py:339
  46.5 3.0 %collective-permute-done.3.refs_11_ = f32[8,256]{1,0:T(8,128)S(1)} collective-permute-done((f32[8,256]{1,0:T(8,128)S(1)}, f32[8,256]{1,0:T(8,128)S(1)}, u32[]{:S(2)}, u32[]{:S(2)}) %collective-permute-start.3) | collective-permute-done | bytes 8224 | tf_op jit(solution)/shard_map/ppermute | solution.py:339
  49.6 2.2 %copy-done.1 = bf16[32,4,64,256]{3,2,1,0:T(8,128)(2,1)S(1)} copy-done((bf16[32,4,64,256]{3,2,1,0:T(8,128)(2,1)S(1)}, bf16[32,4,64,256]{3,2,1,0:T(8,128)(2,1)}, u32[]{:S(2)}) %copy-start.1) | copy-done | bytes 4194328
  51.7 3.8 %ray.2 = (bf16[1024,128]{1,0:T(8,128)(2,1)}, f32[32,64]{1,0:T(8,128)S(1)}, f32[128,256]{1,0:T(8,128)S(1)}, f32[128,256]{1,0:T(8,128)S(1)}, f32[128,256]{1,0:T(8,...) custom-call(bf16[1024,128]{1,0:T(8,128)(2,1)S(1)} %bitcast.25, ...), custom_call_target="tpu_custom_call" | custom-call | flops 8388608 | bytes 5705728 | tf_op jit(solution)/shard_map/ray/pallas_call | solution.py:317
  55.5 11.3 %all-to-all-start.2 = ((bf16[128,8,128]{2,1,0:T(8,128)(2,1)}), bf16[128,8,128]{2,1,0:T(8,128)(2,1)S(1)}, u32[]{:S(2)}, u32[]{:S(2)}) async-start(bf16[128,8,128]{2,1,0:T(8,128)(2,1)} %bitcast.6), calls=%async_computation.2 | async-start | bytes 524288 | tf_op jit(solution)/shard_map/all_to_all | solution.py:332
  66.8 3.3 %collective-permute-start.4 = (f32[16,256]{1,0:T(8,128)S(1)}, f32[16,256]{1,0:T(8,128)S(1)}, u32[]{:S(2)}, u32[]{:S(2)}) collective-permute-start(f32[16,256]{1,0:T(8,128)S(1)} %get-tuple-element.79), channel_id=1, source_target_pairs={{0,1},{1,2},{2,3},{4,5},{5,6},{6,7},{8,9},{9,10},{10,11},{12,13},{... | collective-permute-start | bytes 49160 | tf_op jit(solution)/shard_map/ppermute | solution.py:339
  71.4 3.8 %collective-permute-start.6 = (f32[8,256]{1,0:T(8,128)S(1)}, f32[8,256]{1,0:T(8,128)S(1)}, u32[]{:S(2)}, u32[]{:S(2)}) collective-permute-start(f32[8,256]{1,0:T(8,128)S(1)} %get-tuple-element.81), channel_id=1, source_target_pairs={{0,4},{4,8},{8,12},{12,16},{16,20},{20,24},{24,28},{28,32},{32,36}... | collective-permute-start | bytes 24584 | tf_op jit(solution)/shard_map/ppermute | solution.py:339
  75.2 1.9 %collective-permute-start.7 = (f32[8,256]{1,0:T(8,128)S(1)}, f32[8,256]{1,0:T(8,128)S(1)}, u32[]{:S(2)}, u32[]{:S(2)}) collective-permute-start(f32[8,256]{1,0:T(8,128)S(1)} %get-tuple-element.82), channel_id=1, source_target_pairs={{4,0},{8,4},{12,8},{16,12},{20,16},{24,20},{28,24},{32,28},{36,32}... | collective-permute-start | bytes 24584 | tf_op jit(solution)/shard_map/ppermute | solution.py:339
  77.2 3.0 %collective-permute-done.7.east_ref = f32[8,256]{1,0:T(8,128)S(1)} collective-permute-done((f32[8,256]{1,0:T(8,128)S(1)}, f32[8,256]{1,0:T(8,128)S(1)}, u32[]{:S(2)}, u32[]{:S(2)}) %collective-permute-start.7) | collective-permute-done | bytes 8224 | tf_op jit(solution)/shard_map/ppermute | solution.py:339
  81.5 11.3 %all-to-all-start.3 = ((bf16[128,8,128]{2,1,0:T(8,128)(2,1)}), bf16[128,8,128]{2,1,0:T(8,128)(2,1)S(1)}, u32[]{:S(2)}, u32[]{:S(2)}) async-start(bf16[128,8,128]{2,1,0:T(8,128)(2,1)} %bitcast.8), calls=%async_computation.3 | async-start | bytes 524288 | tf_op jit(solution)/shard_map/all_to_all | solution.py:332
  92.8 3.3 %collective-permute-start.8 = (f32[16,256]{1,0:T(8,128)S(1)}, f32[16,256]{1,0:T(8,128)S(1)}, u32[]{:S(2)}, u32[]{:S(2)}) collective-permute-start(f32[16,256]{1,0:T(8,128)S(1)} %get-tuple-element.87), channel_id=1, source_target_pairs={{0,1},{1,2},{2,3},{4,5},{5,6},{6,7},{8,9},{9,10},{10,11},{12,13},{... | collective-permute-start | bytes 49160 | tf_op jit(solution)/shard_map/ppermute | solution.py:339
  97.4 3.8 %collective-permute-start.10 = (f32[8,256]{1,0:T(8,128)S(1)}, f32[8,256]{1,0:T(8,128)S(1)}, u32[]{:S(2)}, u32[]{:S(2)}) collective-permute-start(f32[8,256]{1,0:T(8,128)S(1)} %get-tuple-element.89), channel_id=1, source_target_pairs={{0,4},{4,8},{8,12},{12,16},{16,20},{20,24},{24,28},{28,32},{32,36}... | collective-permute-start | bytes 24584 | tf_op jit(solution)/shard_map/ppermute | solution.py:339
  103.2 3.0 %collective-permute-done.11.refs_11_ = f32[8,256]{1,0:T(8,128)S(1)} collective-permute-done((f32[8,256]{1,0:T(8,128)S(1)}, f32[8,256]{1,0:T(8,128)S(1)}, u32[]{:S(2)}, u32[]{:S(2)}) %collective-permute-start.11) | collective-permute-done | bytes 8224 | tf_op jit(solution)/shard_map/ppermute | solution.py:339
  106.2 2.2 %copy-done.2 = bf16[32,4,64,256]{3,2,1,0:T(8,128)(2,1)S(1)} copy-done((bf16[32,4,64,256]{3,2,1,0:T(8,128)(2,1)S(1)}, bf16[32,4,64,256]{3,2,1,0:T(8,128)(2,1)}, u32[]{:S(2)}) %copy-start.2) | copy-done | bytes 4194328
  108.4 3.8 %ray.3 = (bf16[1024,128]{1,0:T(8,128)(2,1)}, f32[32,64]{1,0:T(8,128)S(1)}, f32[128,256]{1,0:T(8,128)S(1)}, f32[128,256]{1,0:T(8,128)S(1)}, f32[128,256]{1,0:T(8,...) custom-call(bf16[1024,128]{1,0:T(8,128)(2,1)S(1)} %bitcast.23, ...), custom_call_target="tpu_custom_call" | custom-call | flops 8388608 | bytes 5971968 | tf_op jit(solution)/shard_map/ray/pallas_call | solution.py:317
  112.2 11.3 %all-to-all-start.4 = ((bf16[128,8,128]{2,1,0:T(8,128)(2,1)}), bf16[128,8,128]{2,1,0:T(8,128)(2,1)S(1)}, u32[]{:S(2)}, u32[]{:S(2)}) async-start(bf16[128,8,128]{2,1,0:T(8,128)(2,1)} %bitcast.10), calls=%async_computation.4 | async-start | bytes 524288 | tf_op jit(solution)/shard_map/all_to_all | solution.py:332
  123.5 3.3 %collective-permute-start.12 = (f32[16,256]{1,0:T(8,128)S(1)}, f32[16,256]{1,0:T(8,128)S(1)}, u32[]{:S(2)}, u32[]{:S(2)}) collective-permute-start(f32[16,256]{1,0:T(8,128)S(1)} %get-tuple-element.98), channel_id=1, source_target_pairs={{0,1},{1,2},{2,3},{4,5},{5,6},{6,7},{8,9},{9,10},{10,11},{12,13},{... | collective-permute-start | bytes 49160 | tf_op jit(solution)/shard_map/ppermute | solution.py:339
  128.1 3.8 %collective-permute-start.14 = (f32[8,256]{1,0:T(8,128)S(1)}, f32[8,256]{1,0:T(8,128)S(1)}, u32[]{:S(2)}, u32[]{:S(2)}) collective-permute-start(f32[8,256]{1,0:T(8,128)S(1)} %get-tuple-element.100), channel_id=1, source_target_pairs={{0,4},{4,8},{8,12},{12,16},{16,20},{20,24},{24,28},{28,32},{32,36}... | collective-permute-start | bytes 24584 | tf_op jit(solution)/shard_map/ppermute | solution.py:339
  131.9 2.1 %collective-permute-start.15 = (f32[8,256]{1,0:T(8,128)S(1)}, f32[8,256]{1,0:T(8,128)S(1)}, u32[]{:S(2)}, u32[]{:S(2)}) collective-permute-start(f32[8,256]{1,0:T(8,128)S(1)} %get-tuple-element.101), channel_id=1, source_target_pairs={{4,0},{8,4},{12,8},{16,12},{20,16},{24,20},{28,24},{32,28},{36,32}... | collective-permute-start | bytes 24584 | tf_op jit(solution)/shard_map/ppermute | solution.py:339
  134.1 2.9 %collective-permute-done.15.east_ref = f32[8,256]{1,0:T(8,128)S(1)} collective-permute-done((f32[8,256]{1,0:T(8,128)S(1)}, f32[8,256]{1,0:T(8,128)S(1)}, u32[]{:S(2)}, u32[]{:S(2)}) %collective-permute-start.15) | collective-permute-done | bytes 8224 | tf_op jit(solution)/shard_map/ppermute | solution.py:339
  138.2 11.3 %all-to-all-start.5 = ((bf16[128,8,128]{2,1,0:T(8,128)(2,1)}), bf16[128,8,128]{2,1,0:T(8,128)(2,1)S(1)}, u32[]{:S(2)}, u32[]{:S(2)}) async-start(bf16[128,8,128]{2,1,0:T(8,128)(2,1)} %bitcast.12), calls=%async_computation.5 | async-start | bytes 524288 | tf_op jit(solution)/shard_map/all_to_all | solution.py:332
  149.5 3.3 %collective-permute-start.16 = (f32[16,256]{1,0:T(8,128)S(1)}, f32[16,256]{1,0:T(8,128)S(1)}, u32[]{:S(2)}, u32[]{:S(2)}) collective-permute-start(f32[16,256]{1,0:T(8,128)S(1)} %get-tuple-element.106), channel_id=1, source_target_pairs={{0,1},{1,2},{2,3},{4,5},{5,6},{6,7},{8,9},{9,10},{10,11},{12,13},{... | collective-permute-start | bytes 49160 | tf_op jit(solution)/shard_map/ppermute | solution.py:339
  154.1 3.8 %collective-permute-start.18 = (f32[8,256]{1,0:T(8,128)S(1)}, f32[8,256]{1,0:T(8,128)S(1)}, u32[]{:S(2)}, u32[]{:S(2)}) collective-permute-start(f32[8,256]{1,0:T(8,128)S(1)} %get-tuple-element.108), channel_id=1, source_target_pairs={{0,4},{4,8},{8,12},{12,16},{16,20},{20,24},{24,28},{28,32},{32,36}... | collective-permute-start | bytes 24584 | tf_op jit(solution)/shard_map/ppermute | solution.py:339
  159.9 3.0 %collective-permute-done.19.east_ref = f32[8,256]{1,0:T(8,128)S(1)} collective-permute-done((f32[8,256]{1,0:T(8,128)S(1)}, f32[8,256]{1,0:T(8,128)S(1)}, u32[]{:S(2)}, u32[]{:S(2)}) %collective-permute-start.19) | collective-permute-done | bytes 8224 | tf_op jit(solution)/shard_map/ppermute | solution.py:339
  163.0 2.2 %copy-done.3 = bf16[32,4,64,256]{3,2,1,0:T(8,128)(2,1)S(1)} copy-done((bf16[32,4,64,256]{3,2,1,0:T(8,128)(2,1)S(1)}, bf16[32,4,64,256]{3,2,1,0:T(8,128)(2,1)}, u32[]{:S(2)}) %copy-start.3) | copy-done | bytes 4194328
  165.1 1.9 %last_ray.1 = (f32[128,128]{1,0:T(8,128)S(1)}, f32[32,64]{1,0:T(8,128)S(1)}, f32[128,256]{1,0:T(8,128)S(1)}, f32[8,128]{1,0:T(8,128)S(1)}) custom-call(bf16[1024,128]{1,0:T(8,128)(2,1)S(1)} %bitcast.28, bf16[8192,256]{1,0:T(8,128)(2,1)S(1)} %bitcast.22, bf16[256,1024]{1,0:T(8,128)(2,1)S(1)} %get-tuple-element.62.refs_2_.pick_ref, ...), custom_call_target="tpu_custom_call" | custom-call | flops 8388608 | bytes 5447680 | tf_op jit(solution)/shard_map/last_ray/pallas_call | solution.py:317
  167.1 21.0 %all_to_all.36 = f32[128,1,128]{2,1,0:T(1,128)S(1)} all-to-all(f32[128,1,128]{2,1,0:T(1,128)S(1)} %bitcast.31), channel_id=1, replica_groups=mesh['lat'=32,'rad'=4] {'lat','rad'}, dimensions={0} | all-to-all | bytes 131072 | tf_op jit(solution)/shard_map/all_to_all | solution.py:381
  (44 shorter events, 20.6 us)
Async XLA Ops:
  2.2 2.2 %copy-start = (bf16[32,4,64,256]{3,2,1,0:T(8,128)(2,1)S(1)}, bf16[32,4,64,256]{3,2,1,0:T(8,128)(2,1)}, u32[]{:S(2)}) copy-start(bf16[32,4,64,256]{3,2,1,0:T(8,128)(2,1)} %param.6) | copy-start | bytes 12582916
  4.3 0.7 copy-start.4
  5.1 0.7 copy-start.5
  5.8 0.7 copy-start.6
  32.3 17.3 %all-to-all-start.1 = ((bf16[128,8,128]{2,1,0:T(8,128)(2,1)}), bf16[128,8,128]{2,1,0:T(8,128)(2,1)S(1)}, u32[]{:S(2)}, u32[]{:S(2)}) async-start(bf16[128,8,128]{2,1,0:T(8,128)(2,1)} %bitcast.4), calls=%async_computation.1 | async-start | bytes 524288 | tf_op jit(solution)/shard_map/all_to_all | solution.py:332
  36.1 13.4 %collective-permute-start = (f32[16,256]{1,0:T(8,128)S(1)}, f32[16,256]{1,0:T(8,128)S(1)}, u32[]{:S(2)}, u32[]{:S(2)}) collective-permute-start(f32[16,256]{1,0:T(8,128)S(1)} %get-tuple-element.68), channel_id=1, source_target_pairs={{0,1},{1,2},{2,3},{4,5},{5,6},{6,7},{8,9},{9,10},{10,11},{12,13},{... | collective-permute-start | bytes 49160 | tf_op jit(solution)/shard_map/ppermute | solution.py:339
  39.4 10.1 %collective-permute-start.1 = (f32[16,256]{1,0:T(8,128)S(1)}, f32[16,256]{1,0:T(8,128)S(1)}, u32[]{:S(2)}, u32[]{:S(2)}) collective-permute-start(f32[16,256]{1,0:T(8,128)S(1)} %get-tuple-element.69), channel_id=1, source_target_pairs={{1,0},{2,1},{3,2},{5,4},{6,5},{7,6},{9,8},{10,9},{11,10},{13,12},{... | collective-permute-start | bytes 49160 | tf_op jit(solution)/shard_map/ppermute | solution.py:339
  40.7 5.7 %collective-permute-start.2 = (f32[8,256]{1,0:T(8,128)S(1)}, f32[8,256]{1,0:T(8,128)S(1)}, u32[]{:S(2)}, u32[]{:S(2)}) collective-permute-start(f32[8,256]{1,0:T(8,128)S(1)} %get-tuple-element.70), channel_id=1, source_target_pairs={{0,4},{4,8},{8,12},{12,16},{16,20},{20,24},{24,28},{28,32},{32,36}... | collective-permute-start | bytes 24584 | tf_op jit(solution)/shard_map/ppermute | solution.py:339
  44.6 5.0 %collective-permute-start.3 = (f32[8,256]{1,0:T(8,128)S(1)}, f32[8,256]{1,0:T(8,128)S(1)}, u32[]{:S(2)}, u32[]{:S(2)}) collective-permute-start(f32[8,256]{1,0:T(8,128)S(1)} %get-tuple-element.71), channel_id=1, source_target_pairs={{4,0},{8,4},{12,8},{16,12},{20,16},{24,20},{28,24},{32,28},{36,32}... | collective-permute-start | bytes 24584 | tf_op jit(solution)/shard_map/ppermute | solution.py:339
  49.5 2.2 %copy-start.1 = (bf16[32,4,64,256]{3,2,1,0:T(8,128)(2,1)S(1)}, bf16[32,4,64,256]{3,2,1,0:T(8,128)(2,1)}, u32[]{:S(2)}) copy-start(bf16[32,4,64,256]{3,2,1,0:T(8,128)(2,1)} %param.6) | copy-start | bytes 12582916
  55.5 24.7 %all-to-all-start.2 = ((bf16[128,8,128]{2,1,0:T(8,128)(2,1)}), bf16[128,8,128]{2,1,0:T(8,128)(2,1)S(1)}, u32[]{:S(2)}, u32[]{:S(2)}) async-start(bf16[128,8,128]{2,1,0:T(8,128)(2,1)} %bitcast.6), calls=%async_computation.2 | async-start | bytes 524288 | tf_op jit(solution)/shard_map/all_to_all | solution.py:332
  66.8 13.4 %collective-permute-start.4 = (f32[16,256]{1,0:T(8,128)S(1)}, f32[16,256]{1,0:T(8,128)S(1)}, u32[]{:S(2)}, u32[]{:S(2)}) collective-permute-start(f32[16,256]{1,0:T(8,128)S(1)} %get-tuple-element.79), channel_id=1, source_target_pairs={{0,1},{1,2},{2,3},{4,5},{5,6},{6,7},{8,9},{9,10},{10,11},{12,13},{... | collective-permute-start | bytes 49160 | tf_op jit(solution)/shard_map/ppermute | solution.py:339
  70.1 10.1 %collective-permute-start.5 = (f32[16,256]{1,0:T(8,128)S(1)}, f32[16,256]{1,0:T(8,128)S(1)}, u32[]{:S(2)}, u32[]{:S(2)}) collective-permute-start(f32[16,256]{1,0:T(8,128)S(1)} %get-tuple-element.80), channel_id=1, source_target_pairs={{1,0},{2,1},{3,2},{5,4},{6,5},{7,6},{9,8},{10,9},{11,10},{13,12},{... | collective-permute-start | bytes 49160 | tf_op jit(solution)/shard_map/ppermute | solution.py:339
  71.4 5.7 %collective-permute-start.6 = (f32[8,256]{1,0:T(8,128)S(1)}, f32[8,256]{1,0:T(8,128)S(1)}, u32[]{:S(2)}, u32[]{:S(2)}) collective-permute-start(f32[8,256]{1,0:T(8,128)S(1)} %get-tuple-element.81), channel_id=1, source_target_pairs={{0,4},{4,8},{8,12},{12,16},{16,20},{20,24},{24,28},{28,32},{32,36}... | collective-permute-start | bytes 24584 | tf_op jit(solution)/shard_map/ppermute | solution.py:339
  75.2 5.0 %collective-permute-start.7 = (f32[8,256]{1,0:T(8,128)S(1)}, f32[8,256]{1,0:T(8,128)S(1)}, u32[]{:S(2)}, u32[]{:S(2)}) collective-permute-start(f32[8,256]{1,0:T(8,128)S(1)} %get-tuple-element.82), channel_id=1, source_target_pairs={{4,0},{8,4},{12,8},{16,12},{20,16},{24,20},{28,24},{32,28},{36,32}... | collective-permute-start | bytes 24584 | tf_op jit(solution)/shard_map/ppermute | solution.py:339
  81.5 24.7 %all-to-all-start.3 = ((bf16[128,8,128]{2,1,0:T(8,128)(2,1)}), bf16[128,8,128]{2,1,0:T(8,128)(2,1)S(1)}, u32[]{:S(2)}, u32[]{:S(2)}) async-start(bf16[128,8,128]{2,1,0:T(8,128)(2,1)} %bitcast.8), calls=%async_computation.3 | async-start | bytes 524288 | tf_op jit(solution)/shard_map/all_to_all | solution.py:332
  92.8 13.4 %collective-permute-start.8 = (f32[16,256]{1,0:T(8,128)S(1)}, f32[16,256]{1,0:T(8,128)S(1)}, u32[]{:S(2)}, u32[]{:S(2)}) collective-permute-start(f32[16,256]{1,0:T(8,128)S(1)} %get-tuple-element.87), channel_id=1, source_target_pairs={{0,1},{1,2},{2,3},{4,5},{5,6},{6,7},{8,9},{9,10},{10,11},{12,13},{... | collective-permute-start | bytes 49160 | tf_op jit(solution)/shard_map/ppermute | solution.py:339
  96.1 10.1 %collective-permute-start.9 = (f32[16,256]{1,0:T(8,128)S(1)}, f32[16,256]{1,0:T(8,128)S(1)}, u32[]{:S(2)}, u32[]{:S(2)}) collective-permute-start(f32[16,256]{1,0:T(8,128)S(1)} %get-tuple-element.88), channel_id=1, source_target_pairs={{1,0},{2,1},{3,2},{5,4},{6,5},{7,6},{9,8},{10,9},{11,10},{13,12},{... | collective-permute-start | bytes 49160 | tf_op jit(solution)/shard_map/ppermute | solution.py:339
  97.4 5.7 %collective-permute-start.10 = (f32[8,256]{1,0:T(8,128)S(1)}, f32[8,256]{1,0:T(8,128)S(1)}, u32[]{:S(2)}, u32[]{:S(2)}) collective-permute-start(f32[8,256]{1,0:T(8,128)S(1)} %get-tuple-element.89), channel_id=1, source_target_pairs={{0,4},{4,8},{8,12},{12,16},{16,20},{20,24},{24,28},{28,32},{32,36}... | collective-permute-start | bytes 24584 | tf_op jit(solution)/shard_map/ppermute | solution.py:339
  101.2 5.0 %collective-permute-start.11 = (f32[8,256]{1,0:T(8,128)S(1)}, f32[8,256]{1,0:T(8,128)S(1)}, u32[]{:S(2)}, u32[]{:S(2)}) collective-permute-start(f32[8,256]{1,0:T(8,128)S(1)} %get-tuple-element.90), channel_id=1, source_target_pairs={{4,0},{8,4},{12,8},{16,12},{20,16},{24,20},{28,24},{32,28},{36,32}... | collective-permute-start | bytes 24584 | tf_op jit(solution)/shard_map/ppermute | solution.py:339
  106.2 2.2 %copy-start.2 = (bf16[32,4,64,256]{3,2,1,0:T(8,128)(2,1)S(1)}, bf16[32,4,64,256]{3,2,1,0:T(8,128)(2,1)}, u32[]{:S(2)}) copy-start(bf16[32,4,64,256]{3,2,1,0:T(8,128)(2,1)} %param.6) | copy-start | bytes 12582916
  112.2 24.7 %all-to-all-start.4 = ((bf16[128,8,128]{2,1,0:T(8,128)(2,1)}), bf16[128,8,128]{2,1,0:T(8,128)(2,1)S(1)}, u32[]{:S(2)}, u32[]{:S(2)}) async-start(bf16[128,8,128]{2,1,0:T(8,128)(2,1)} %bitcast.10), calls=%async_computation.4 | async-start | bytes 524288 | tf_op jit(solution)/shard_map/all_to_all | solution.py:332
  123.5 13.4 %collective-permute-start.12 = (f32[16,256]{1,0:T(8,128)S(1)}, f32[16,256]{1,0:T(8,128)S(1)}, u32[]{:S(2)}, u32[]{:S(2)}) collective-permute-start(f32[16,256]{1,0:T(8,128)S(1)} %get-tuple-element.98), channel_id=1, source_target_pairs={{0,1},{1,2},{2,3},{4,5},{5,6},{6,7},{8,9},{9,10},{10,11},{12,13},{... | collective-permute-start | bytes 49160 | tf_op jit(solution)/shard_map/ppermute | solution.py:339
  126.8 10.1 %collective-permute-start.13 = (f32[16,256]{1,0:T(8,128)S(1)}, f32[16,256]{1,0:T(8,128)S(1)}, u32[]{:S(2)}, u32[]{:S(2)}) collective-permute-start(f32[16,256]{1,0:T(8,128)S(1)} %get-tuple-element.99), channel_id=1, source_target_pairs={{1,0},{2,1},{3,2},{5,4},{6,5},{7,6},{9,8},{10,9},{11,10},{13,12},{... | collective-permute-start | bytes 49160 | tf_op jit(solution)/shard_map/ppermute | solution.py:339
  128.1 5.9 %collective-permute-start.14 = (f32[8,256]{1,0:T(8,128)S(1)}, f32[8,256]{1,0:T(8,128)S(1)}, u32[]{:S(2)}, u32[]{:S(2)}) collective-permute-start(f32[8,256]{1,0:T(8,128)S(1)} %get-tuple-element.100), channel_id=1, source_target_pairs={{0,4},{4,8},{8,12},{12,16},{16,20},{20,24},{24,28},{28,32},{32,36}... | collective-permute-start | bytes 24584 | tf_op jit(solution)/shard_map/ppermute | solution.py:339
  131.9 5.0 %collective-permute-start.15 = (f32[8,256]{1,0:T(8,128)S(1)}, f32[8,256]{1,0:T(8,128)S(1)}, u32[]{:S(2)}, u32[]{:S(2)}) collective-permute-start(f32[8,256]{1,0:T(8,128)S(1)} %get-tuple-element.101), channel_id=1, source_target_pairs={{4,0},{8,4},{12,8},{16,12},{20,16},{24,20},{28,24},{32,28},{36,32}... | collective-permute-start | bytes 24584 | tf_op jit(solution)/shard_map/ppermute | solution.py:339
  138.2 24.7 %all-to-all-start.5 = ((bf16[128,8,128]{2,1,0:T(8,128)(2,1)}), bf16[128,8,128]{2,1,0:T(8,128)(2,1)S(1)}, u32[]{:S(2)}, u32[]{:S(2)}) async-start(bf16[128,8,128]{2,1,0:T(8,128)(2,1)} %bitcast.12), calls=%async_computation.5 | async-start | bytes 524288 | tf_op jit(solution)/shard_map/all_to_all | solution.py:332
  149.5 13.4 %collective-permute-start.16 = (f32[16,256]{1,0:T(8,128)S(1)}, f32[16,256]{1,0:T(8,128)S(1)}, u32[]{:S(2)}, u32[]{:S(2)}) collective-permute-start(f32[16,256]{1,0:T(8,128)S(1)} %get-tuple-element.106), channel_id=1, source_target_pairs={{0,1},{1,2},{2,3},{4,5},{5,6},{6,7},{8,9},{9,10},{10,11},{12,13},{... | collective-permute-start | bytes 49160 | tf_op jit(solution)/shard_map/ppermute | solution.py:339
  152.8 10.1 %collective-permute-start.17 = (f32[16,256]{1,0:T(8,128)S(1)}, f32[16,256]{1,0:T(8,128)S(1)}, u32[]{:S(2)}, u32[]{:S(2)}) collective-permute-start(f32[16,256]{1,0:T(8,128)S(1)} %get-tuple-element.107), channel_id=1, source_target_pairs={{1,0},{2,1},{3,2},{5,4},{6,5},{7,6},{9,8},{10,9},{11,10},{13,12},{... | collective-permute-start | bytes 49160 | tf_op jit(solution)/shard_map/ppermute | solution.py:339
  154.1 5.7 %collective-permute-start.18 = (f32[8,256]{1,0:T(8,128)S(1)}, f32[8,256]{1,0:T(8,128)S(1)}, u32[]{:S(2)}, u32[]{:S(2)}) collective-permute-start(f32[8,256]{1,0:T(8,128)S(1)} %get-tuple-element.108), channel_id=1, source_target_pairs={{0,4},{4,8},{8,12},{12,16},{16,20},{20,24},{24,28},{28,32},{32,36}... | collective-permute-start | bytes 24584 | tf_op jit(solution)/shard_map/ppermute | solution.py:339
  158.0 5.0 %collective-permute-start.19 = (f32[8,256]{1,0:T(8,128)S(1)}, f32[8,256]{1,0:T(8,128)S(1)}, u32[]{:S(2)}, u32[]{:S(2)}) collective-permute-start(f32[8,256]{1,0:T(8,128)S(1)} %get-tuple-element.109), channel_id=1, source_target_pairs={{4,0},{8,4},{12,8},{16,12},{20,16},{24,20},{28,24},{32,28},{36,32}... | collective-permute-start | bytes 24584 | tf_op jit(solution)/shard_map/ppermute | solution.py:339
  162.9 2.2 %copy-start.3 = (bf16[32,4,64,256]{3,2,1,0:T(8,128)(2,1)S(1)}, bf16[32,4,64,256]{3,2,1,0:T(8,128)(2,1)}, u32[]{:S(2)}) copy-start(bf16[32,4,64,256]{3,2,1,0:T(8,128)(2,1)} %param.6) | copy-start | bytes 12582916

commit v2 on v1

v2 whole, which is shorter than its diff:
```python
import functools

import jax
import jax.numpy as jnp
from jax import lax
from jax.experimental import pallas as pl
from jax.experimental.pallas import tpu as pltpu
from jax.sharding import PartitionSpec as P

ITERS = 3
MB_R = 8
MB_L = 16
FREEDOM = 4.0
DAMPING = 0.3

AXES = ("lat", "rad")
CHUNK = 8
NORM_ROW = 4
ID_ROW = 5
CELL_ROW = 6
LANES = 128
PARTS = 4

F32 = jnp.float32
BF16 = jnp.bfloat16
NT = (((1,), (1,)), ((), ()))


def iota(shape, dim):
    return lax.broadcasted_iota(jnp.int32, shape, dim)


def matmul(a, b):
    return jnp.dot(a, b, preferred_element_type=F32)


def total(x):
    return jnp.sum(jnp.sum(x, axis=1, keepdims=True), axis=0, keepdims=True)


def norm_row(partial):
    high = partial.astype(BF16).astype(F32)
    middle = (partial - high).astype(BF16).astype(F32)
    low = partial - high - middle
    lane = iota((1, LANES), 1)
    return jnp.where(lane == 0, high, jnp.where(lane == 1, middle, jnp.where(lane == 2, low, 0.0)))


def with_norm(packed, partial):
    rows = iota(packed.shape, 0) % CHUNK
    return jnp.where(rows == NORM_ROW, norm_row(partial), packed).astype(BF16)


def norm_of(sums):
    lane = iota((1, LANES), 1)
    return jnp.sqrt(jnp.sum(jnp.where(lane < 3, sums[0:1, :], 0.0), axis=1, keepdims=True))


def ones_where(condition):
    return jnp.where(condition, 1.0, 0.0).astype(BF16)


def write_cell_picks(ref, start, devices):
    rows = devices * CHUNK
    device, row = iota((devices, rows), 0), iota((devices, rows), 1)
    for j in range(2):
        ref[start + j * devices : start + (j + 1) * devices, :] = ones_where(row == device * CHUNK + CELL_ROW + j)
    ref[start + 2 * devices :, :] = ones_where(iota((16, rows), 1) % CHUNK == NORM_ROW)


def write_cell_places(ref, start, devices):
    rows = devices * CHUNK
    row, device = iota((rows, devices), 0), iota((rows, devices), 1)
    for j in range(2):
        ref[:, start + j * devices : start + (j + 1) * devices] = ones_where(row == device * CHUNK + CELL_ROW + j)


def stacked(x):
    return jnp.concatenate([x[:, :LANES], x[:, LANES:]], axis=0)


def unstacked(x):
    half = x.shape[0] // 2
    return jnp.concatenate([x[:half], x[half:]], axis=1)


def adjoint_products(kernel_ref, y, out_ref, ray_blocks, fanout, ready=None):
    high = y.astype(BF16).astype(F32)
    low = y - high
    high = jnp.concatenate([high] * fanout, axis=1)
    low = jnp.concatenate([low] * fanout, axis=1)
    width = high.shape[1]
    ray_len = width // fanout
    row, lane = iota((2 * fanout, width), 0), iota((2 * fanout, width), 1)
    own = lane // ray_len == row % fanout
    for b in range(ray_blocks):
        if ready is not None:
            ready(b)
        lhs = jnp.where(row < fanout, high[b : b + 1], low[b : b + 1])
        lhs = jnp.where(own, lhs, 0.0).astype(BF16)
        both = matmul(lhs, kernel_ref[b * width : (b + 1) * width, :])
        out_ref[b * fanout : (b + 1) * fanout, :] = both[:fanout] + both[fanout:]


def forward_products(kernel_ref, blocks, ray_blocks, fanout, ray_len):
    entries = ray_blocks * fanout
    lane = iota((ray_len, entries), 1)
    picked = jnp.zeros((ray_len, entries), F32)
    group = 16
    for start in range(0, entries, group):
        products = lax.dot_general(
            kernel_ref[start * ray_len : (start + group) * ray_len, :], blocks, NT, preferred_element_type=F32
        )
        for i in range(group):
            picked = jnp.where(lane == start + i, products[i * ray_len : (i + 1) * ray_len], picked)
    member = jnp.where(iota((ray_blocks, entries), 1) // fanout == iota((ray_blocks, entries), 0), 1.0, 0.0)
    return lax.dot_general(member, picked, NT, preferred_element_type=F32, precision=lax.Precision.HIGHEST)


def roughen(cell, rads):
    shape = cell.shape
    devices, blocks = shape
    device, block = iota(shape, 0), iota(shape, 1)
    rad, place = device % rads, block % MB_L
    lanes = lambda x, step: pltpu.roll(x, step % blocks, 1)
    owner = lambda x, step: pltpu.roll(x, step % devices, 0)
    up = lanes(cell, MB_L)
    north = jnp.where(block >= MB_L, up, jnp.where(rad > 0, owner(up, 1), 0.0))
    down = lanes(cell, -MB_L)
    south = jnp.where(block < blocks - MB_L, down, jnp.where(rad < rads - 1, owner(down, -1), 0.0))
    far = owner(lanes(cell, 1 - MB_L), rads)
    west = jnp.where(place > 0, lanes(cell, 1), jnp.where(device >= rads, far, 0.0))
    far = owner(lanes(cell, MB_L - 1), -rads)
    east = jnp.where(place < MB_L - 1, lanes(cell, -1), jnp.where(device < devices - rads, far, 0.0))
    return 4.0 * cell - (south + north + east + west)


def scalars_row(*values):
    lane = iota((8, LANES), 1)
    out = jnp.zeros((8, LANES), F32)
    for i, value in enumerate(values):
        out = jnp.where(lane == i, value, out)
    return out


def start_kernel(
    kernel_hbm, device_hbm, block_hbm, counts_hbm, times_hbm, prior_hbm,
    send_ref, tiles_ref, weights_ref, data_ref, pick_ref, place_ref,
    device_ref, block_ref, counts_ref, times_ref, prior_ref, partial_ref, small_sem, tile_sem,
):
    fanout, ray_blocks = device_ref.shape
    ray_len = times_ref.shape[1]
    entries = ray_blocks * fanout
    rows = send_ref.shape[0]
    devices = rows // CHUNK
    part = tiles_ref.shape[0] // PARTS

    small = [
        pltpu.make_async_copy(source, target, small_sem.at[i])
        for i, (source, target) in enumerate(
            ((device_hbm, device_ref), (block_hbm, block_ref), (counts_hbm, counts_ref),
             (times_hbm, times_ref), (prior_hbm, prior_ref))
        )
    ]
    large = [
        pltpu.make_async_copy(
            kernel_hbm.at[pl.ds(i * part, part), :], tiles_ref.at[pl.ds(i * part, part), :], tile_sem.at[i]
        )
        for i in range(PARTS)
    ]
    for copy in small + large:
        copy.start()
    write_cell_picks(pick_ref, 2 * entries, devices)
    write_cell_places(place_ref, 2 * entries, devices)
    for copy in small:
        copy.wait()

    member = ones_where(iota((entries, ray_blocks), 0) // fanout == iota((entries, ray_blocks), 1))
    turn = iota((entries, fanout), 0) % fanout == iota((entries, fanout), 1)

    def column(table_ref):
        table = table_ref[...].astype(F32).astype(BF16)
        spread = lax.dot_general(member, table, NT, preferred_element_type=F32)
        return jnp.sum(jnp.where(turn, spread, 0.0), axis=1, keepdims=True)

    diagonal = iota((entries, entries), 0) == iota((entries, entries), 1)

    def as_row(col):
        return jnp.sum(jnp.where(diagonal, col, 0.0), axis=0, keepdims=True)

    target = column(device_ref)
    block = column(block_ref)
    target_row = as_row(target)
    earlier = iota((entries, entries), 1) < iota((entries, entries), 0)
    rank = jnp.sum(jnp.where(earlier & (target == target_row), 1.0, 0.0), axis=1, keepdims=True)
    first = target * CHUNK + 2.0 * rank
    first_row = as_row(first)

    to_col = first.astype(jnp.int32)
    to_row = first_row.astype(jnp.int32)
    for half in range(2):
        here = slice(half * entries, (half + 1) * entries)
        pick_ref[here, :] = ones_where(iota((entries, rows), 1) == to_col + half)
        place_ref[:, here] = ones_where(iota((rows, entries), 0) == to_row + half)

    same = iota((ray_blocks, ray_blocks), 0) == iota((ray_blocks, ray_blocks), 1)
    counts = jnp.sum(jnp.where(same, counts_ref[...].astype(F32), 0.0), axis=1, keepdims=True)
    mask = jnp.where(iota((ray_blocks, ray_len), 1).astype(F32) < counts, 1.0, 0.0)
    prior = prior_ref[...]
    weights = mask * jnp.sqrt((FREEDOM + 1.0) / (FREEDOM + prior * prior))
    weights_ref[...] = weights
    data = weights * times_ref[...]
    data_ref[...] = data

    def ready(b):
        if b % (ray_blocks // PARTS) == 0:
            large[b // (ray_blocks // PARTS)].wait()

    adjoint_products(tiles_ref, weights * data, partial_ref, ray_blocks, fanout, ready)
    ids = jnp.where(iota((entries, LANES), 1).astype(F32) == rank, block + 1.0, 0.0).astype(BF16)
    id_rows = (target_row * CHUNK + ID_ROW).astype(jnp.int32)
    id_place = ones_where(iota((rows, entries), 0) == id_rows)
    packed = matmul(place_ref[:, : 2 * entries], stacked(partial_ref[...].astype(BF16))) + matmul(id_place, ids)
    send_ref[...] = with_norm(packed, total(data * data))


def send_field(send_ref, field, gather_ref):
    halves = [field[:, :LANES], field[:, LANES:]]
    packed = jnp.concatenate(halves + [half.T for half in halves], axis=0).astype(BF16)
    send_ref[...] = with_norm(matmul(gather_ref[...], packed), total(field * field))


def first_model_kernel(received_ref, send_ref, field_ref, state_ref, gather_ref, scatter_ref):
    received = received_ref[...]
    rows = received.shape[0]
    devices = rows // CHUNK
    blocks = MB_R * MB_L
    pick = ones_where(iota((devices, rows), 1) == iota((devices, rows), 0) * CHUNK + ID_ROW)
    ids = matmul(pick, received).astype(BF16)
    owner = ones_where(iota((rows, devices), 0) // CHUNK == iota((rows, devices), 1))
    spread = matmul(owner, ids)
    place = iota((rows, LANES), 0) % CHUNK
    lane = iota((rows, LANES), 1)
    slot = (place < NORM_ROW) & (lane == place // 2)
    ident = jnp.sum(jnp.where(slot, spread, 0.0), axis=1, keepdims=True) - 1.0
    hit = ident == lane.astype(F32)
    for half in range(2):
        here = slice(half * blocks, (half + 1) * blocks)
        chosen = jnp.where(hit & (place % 2 == half), 1.0, 0.0)
        gather_ref[:, here] = chosen.astype(BF16)
        scatter_ref[here, :] = chosen.T.astype(BF16)
    write_cell_picks(scatter_ref, 2 * blocks, devices)
    write_cell_places(gather_ref, 2 * blocks, devices)

    got = matmul(scatter_ref[...], received)
    beta = norm_of(got[2 * blocks + 2 * devices :])
    field = unstacked(got[: 2 * blocks]) / beta
    field_ref[...] = field
    state_ref[...] = scalars_row(beta)
    send_field(send_ref, field, gather_ref)


def ray_step(sweep, rads, received_ref, kernel_ref, pick_ref, weights_ref, data_ref, state_ref, pen_ref):
    received = received_ref[...]
    ray_blocks, ray_len = data_ref.shape
    devices = received.shape[0] // CHUNK
    got = matmul(pick_ref[...], received)
    entries = (got.shape[0] - 2 * devices - 16) // 2
    fanout = entries // ray_blocks
    alpha = norm_of(got[2 * entries + 2 * devices :])
    blocks = unstacked(got[: 2 * entries]).astype(BF16)
    products = forward_products(kernel_ref, blocks, ray_blocks, fanout, ray_len)
    beta = state_ref[0:1, 0:1]
    data = weights_ref[...] * (products / alpha) - alpha * (data_ref[...] / beta)
    partial = total(data * data)
    pens = []
    for j in range(2):
        cell = got[2 * entries + j * devices : 2 * entries + (j + 1) * devices]
        pen = DAMPING * (roughen(cell, rads) / alpha)
        if sweep:
            pen = pen - alpha * (pen_ref[j * devices : (j + 1) * devices] / beta)
        partial = partial + total(pen * pen)
        pens.append(pen)
    return alpha, data, pens, partial


def ray_kernel(sweep, rads, *refs):
    received_ref, kernel_ref, pick_ref, place_ref, weights_ref, data_ref, state_ref = refs[:7]
    pen_ref = refs[7] if sweep else None
    send_ref, data_out, pen_out, alpha_out, partial_ref = refs[-5:]
    alpha, data, pens, partial = ray_step(
        sweep, rads, received_ref, kernel_ref, pick_ref, weights_ref, data_ref, state_ref, pen_ref
    )
    data_out[...] = data
    pen_out[...] = jnp.concatenate(pens, axis=0)
    alpha_out[...] = scalars_row(alpha)
    ray_blocks = data.shape[0]
    fanout = partial_ref.shape[0] // ray_blocks
    adjoint_products(kernel_ref, weights_ref[...] * data, partial_ref, ray_blocks, fanout)
    rough = [DAMPING * roughen(pen, rads) for pen in pens]
    packed = jnp.concatenate([stacked(partial_ref[...])] + rough, axis=0).astype(BF16)
    send_ref[...] = with_norm(matmul(place_ref[...], packed), partial)


def last_ray_kernel(sweep, rads, *refs):
    send_ref, data_out, alpha_out = refs[-3:]
    alpha, data, pens, partial = ray_step(sweep, rads, *refs[:-3])
    data_out[...] = data
    alpha_out[...] = scalars_row(alpha)
    send_ref[...] = jnp.broadcast_to(partial, send_ref.shape)


def advance(sweep, beta, field_ref, alpha_ref, state_ref, search_ref, update_ref):
    alpha = alpha_ref[0:1, 0:1]
    direction = field_ref[...] / alpha
    if sweep:
        phi_bar, rho, cosine, sine = [state_ref[0:1, i : i + 1] for i in range(1, 5)]
        search = direction - (sine * alpha / rho) * search_ref[...]
        rho_bar = -cosine * alpha
    else:
        phi_bar, rho_bar = state_ref[0:1, 0:1], alpha
        search = direction
    rho = jnp.sqrt(rho_bar * rho_bar + beta * beta)
    cosine, sine = rho_bar / rho, beta / rho
    update = (cosine * phi_bar / rho) * search
    if sweep:
        update = update_ref[...] + update
    return direction, search, update, scalars_row(beta, sine * phi_bar, rho, cosine, sine)


def model_kernel(sweep, *refs):
    received_ref, scatter_ref, gather_ref, field_ref, alpha_ref, state_ref = refs[:6]
    search_ref, update_ref = refs[6:8] if sweep else (None, None)
    send_ref, field_out, state_out, search_out, update_out = refs[-5:]
    received = received_ref[...]
    devices = received.shape[0] // CHUNK
    got = matmul(scatter_ref[...], received)
    blocks = field_ref.shape[0]
    beta = norm_of(got[2 * blocks + 2 * devices :])
    direction, search, update, state = advance(
        sweep, beta, field_ref, alpha_ref, state_ref, search_ref, update_ref
    )
    rough = [got[2 * blocks + j * devices : 2 * blocks + (j + 1) * devices].T for j in range(2)]
    field = (unstacked(got[: 2 * blocks]) + jnp.concatenate(rough, axis=1)) / beta - beta * direction
    field_out[...] = field
    send_field(send_ref, field, gather_ref)
    state_out[...] = state
    search_out[...] = search
    update_out[...] = update


def last_kernel(norms_ref, data_ref, field_ref, alpha_ref, state_ref, search_ref, update_ref, update_out, data_out):
    beta = jnp.sqrt(jnp.sum(norms_ref[...], axis=0, keepdims=True)[:, 0:1])
    update_out[...] = advance(ITERS - 1, beta, field_ref, alpha_ref, state_ref, search_ref, update_ref)[2]
    data_out[...] = data_ref[...] / beta


def call(kernel, name, outputs, scratch, operands, flops=0, space=pltpu.VMEM):
    bytes_accessed = sum(x.size * x.dtype.itemsize for x in operands)
    return pl.pallas_call(
        kernel,
        name=name,
        out_shape=[jax.ShapeDtypeStruct(shape, dtype) for shape, dtype in outputs],
        in_specs=[pl.BlockSpec(memory_space=space)] * len(operands),
        out_specs=[pl.BlockSpec(memory_space=pltpu.VMEM)] * len(outputs),
        scratch_shapes=scratch,
        compiler_params=pltpu.CompilerParams(vmem_limit_bytes=40 << 20),
        cost_estimate=pl.CostEstimate(flops=flops, bytes_accessed=bytes_accessed, transcendentals=0),
    )(*operands)


def exchange(packed, devices):
    rows, lanes = packed.shape
    chunks = packed.reshape(devices, rows // devices, lanes)
    return lax.all_to_all(chunks, AXES, split_axis=0, concat_axis=0, tiled=True).reshape(rows, lanes)


def body(kernel, target_device, target_block, counts, traveltimes, prior_residual):
    rads = lax.axis_size("rad")
    devices = lax.axis_size("lat") * rads
    ray_blocks, fanout, ray_len, cells = kernel.shape
    entries = ray_blocks * fanout
    rows = devices * CHUNK
    blocks = MB_R * MB_L
    flops = 4 * entries * ray_len * cells

    packet = ((rows, LANES), BF16)
    ray = ((ray_blocks, ray_len), F32)
    model = ((blocks, cells), F32)
    scalar = ((8, LANES), F32)
    partials = pltpu.VMEM((entries, cells), F32)

    def picks(named):
        return ((2 * named + 2 * devices + 16, rows), BF16)

    def places(named):
        return ((rows, 2 * named + 2 * devices), BF16)

    send, tiles, weights, data, pick, place = call(
        start_kernel, "start",
        [packet, ((entries * ray_len, cells), BF16), ray, ray, picks(entries), places(entries)],
        [
            pltpu.VMEM((fanout, ray_blocks), jnp.int32), pltpu.VMEM((fanout, ray_blocks), jnp.int32),
            pltpu.VMEM((1, ray_blocks), jnp.int32), pltpu.VMEM((ray_blocks, ray_len), F32),
            pltpu.VMEM((ray_blocks, ray_len), F32), partials,
            pltpu.SemaphoreType.DMA((5,)), pltpu.SemaphoreType.DMA((PARTS,)),
        ],
        (kernel.reshape(entries * ray_len, cells), target_device.T, target_block.T,
         counts.reshape(1, ray_blocks), traveltimes, prior_residual),
        flops, pltpu.HBM,
    )
    received = exchange(send, devices)
    send, field, state, gather, scatter = call(
        first_model_kernel, "first_model", [packet, model, scalar, places(blocks), picks(blocks)], [], (received,),
    )
    carried, pens = (), ()
    for sweep in range(ITERS):
        received = exchange(send, devices)
        if sweep == ITERS - 1:
            break
        send, data, pen, alpha = call(
            functools.partial(ray_kernel, sweep, rads), "ray",
            [packet, ray, ((2 * devices, blocks), F32), scalar], [partials],
            (received, tiles, pick, place, weights, data, state) + pens, flops,
        )
        pens = (pen,)
        received = exchange(send, devices)
        send, field, state, *carried = call(
            functools.partial(model_kernel, sweep), "model", [packet, model, scalar, model, model], [],
            (received, scatter, gather, field, alpha, state, *carried), flops,
        )
    send, data, alpha = call(
        functools.partial(last_ray_kernel, ITERS - 1, rads), "last_ray", [((devices, LANES), F32), ray, scalar], [],
        (received, tiles, pick, weights, data, state) + pens, flops,
    )
    norms = exchange(send, devices)
    update, data = call(last_kernel, "last", [model, ray], [], (norms, data, field, alpha, state, *carried))
    return (update.reshape(MB_R, MB_L, cells), data)


def solution(mesh):
    in_specs = (
        P(("lat", "rad"), None, None, None),
        P(("lat", "rad"), None),
        P(("lat", "rad"), None),
        P(("lat", "rad")),
        P(("lat", "rad"), None),
        P(("lat", "rad"), None),
    )
    out_specs = (P("rad", "lat", None), P(("lat", "rad"), None))
    return jax.shard_map(body, mesh=mesh, in_specs=in_specs, out_specs=out_specs, check_vma=False)
```

time: 190 us -> 136 us (0.72)
  starting transfers between devices: 101 us -> 0 us
  blocking collectives: 43.6 us -> 111 us
  waiting for transfers between devices: 15 us -> 0 us
  local copies, waits for them, and re-layouts: 12.3 us -> 5.63 us
  Pallas kernels: 16.2 us -> 18.4 us
    all_to_all x1 -> x7, blocking collectives: 22.6 us -> 111 us  [exchange(): lax.all_to_all(chunks, AXES, split_axis=0, concat_axis=0, tiled=True)]
    ppermute x20 -> x0, starting transfers between devices: 51.7 us -> none  [shift(): return lax.ppermute(x, axis, pairs)]
    all_to_all x5 -> x0, starting transfers between devices: 49.1 us -> none  [exchange(): lax.all_to_all(chunks, AXES, split_axis=0, concat_axis=0, tiled=True)]
    all_to_all x1 -> x0, blocking collectives: 21 us -> none  [body(): lax.all_to_all(send.reshape(devices, 1, LANES), AXES, split_axis=0, conca...]
    ppermute x20 -> x0, waiting for transfers between devices: 15 us -> none  [shift(): return lax.ppermute(x, axis, pairs)]
    unnamed x16 -> x12, local copies, waits for them, and re-layouts: 12.3 us -> 5.63 us
    pallas_call x8, Pallas kernels: 16.2 us -> 18.4 us  [call(): pl.pallas_call(kernel, name=name, out_shape=[jax.ShapeDtypeStruct(shape,...]
  transfers between devices with their start and end apart: 25 -> 0, of which waited for: 5 -> 0; matrix products, arithmetic and copies ran while one was open for 0% -> 0% of each run, Pallas kernels for 0% -> 0%
where the time goes in v2:
time: 136 us
  blocking collectives  111 us (82%)
  Pallas kernels  18.4 us (14%)
  local copies, waits for them, and re-layouts  5.63 us (4%)
    all_to_all x7, blocking collectives, exchange(): lax.all_to_all(chunks, AXES, split_axis=0, concat_axis=0, tiled=True)  111 us
    pallas_call x8, Pallas kernels, call(): pl.pallas_call(kernel, name=name, out_shape=[jax.ShapeDtypeStruct(shape,...  18.4 us
    unnamed x12, local copies, waits for them, and re-layouts  5.63 us

profile of v2, /device:TPU:1, one launch (start us, length us, event | category | flops | bytes accessed | tf_op | source)
XLA Modules:
  0.0 135.9 jit_solution(12504318719364849719)
XLA Ops:
  0.6 0.0 copy-start
  0.6 2.2 %copy-done = bf16[32,4,64,256]{3,2,1,0:T(8,128)(2,1)S(1)} copy-done((bf16[32,4,64,256]{3,2,1,0:T(8,128)(2,1)S(1)}, bf16[32,4,64,256]{3,2,1,0:T(8,128)(2,1)}, u32[]{:S(2)}) %copy-start) | copy-done | bytes 4194328
  2.8 0.0 copy-start.1
  2.8 0.7 copy-done.1
  3.5 0.0 copy-start.2
  3.5 0.7 copy-done.2
  4.3 0.0 copy-start.3
  4.3 0.7 copy-done.3
  4.9 0.0 copy-start.4
  4.9 0.7 copy-done.4
  5.6 0.0 copy-start.5
  5.6 0.7 copy-done.5
  6.3 2.7 %start.1 = (bf16[1024,128]{1,0:T(8,128)(2,1)S(1)}, bf16[8192,256]{1,0:T(8,128)(2,1)S(1)}, f32[32,64]{1,0:T(8,128)S(1)}, f32[32,64]{1,0:T(8,128)S(1)}, bf16[528,1...) custom-call(bf16[8192,256]{1,0:T(8,128)(2,1)S(1)} %bitcast.21, s32[4,32]{1,0:T(4,128)S(1)} %bitcast.36, ...), custom_call_target="tpu_custom_call" | custom-call | flops 8388608 | bytes 4211840 | tf_op jit(solution)/shard_map/start/pallas_call | solution.py:360
  9.0 22.6 %all_to_all.35 = bf16[128,8,128]{2,1,0:T(8,128)(2,1)S(1)} all-to-all(bf16[128,8,128]{2,1,0:T(8,128)(2,1)S(1)} %bitcast.31), channel_id=1, replica_groups=mesh['lat'=32,'rad'=4] {'lat','rad'}, dimensions={0} | all-to-all | bytes 524288 | tf_op jit(solution)/shard_map/all_to_all | solution.py:375
  31.6 2.1 %first_model.1 = (bf16[1024,128]{1,0:T(8,128)(2,1)S(1)}, f32[128,256]{1,0:T(8,128)S(1)}, f32[8,128]{1,0:T(8,128)S(1)}, bf16[1024,512]{1,0:T(8,128)(2,1)S(1)}, bf16[528,1024]{1,0:T(8,128)(2,1)S(1)}) custom-call(bf16[1024,128]{1,0:T(8,128)(2,1)S(1)} %bitcast.26), custom_call_target="tpu_custom_call" | custom-call | bytes 262144 | tf_op jit(solution)/shard_map/first_model/pallas_call | solution.py:360
  33.7 15.0 %all_to_all.36 = bf16[128,8,128]{2,1,0:T(8,128)(2,1)S(1)} all-to-all(bf16[128,8,128]{2,1,0:T(8,128)(2,1)S(1)} %bitcast.32), channel_id=1, replica_groups=mesh['lat'=32,'rad'=4] {'lat','rad'}, dimensions={0} | all-to-all | bytes 524288 | tf_op jit(solution)/shard_map/all_to_all | solution.py:375
  48.7 3.6 %ray.2 = (bf16[1024,128]{1,0:T(8,128)(2,1)S(1)}, f32[32,64]{1,0:T(8,128)S(1)}, f32[256,128]{1,0:T(8,128)S(1)}, f32[8,128]{1,0:T(8,128)S(1)}) custom-call(bf16[1024,128]{1,0:T(8,128)(2,1)S(1)} %bitcast.25, bf16[8192,256]{1,0:T(8,128)(2,1)S(1)} %get-tuple-element.38.refs_1_, bf16[528,1024]{1,0:T(8,128)(2,1)S(1)} %get-tuple-element.39.refs_2_, ...), custom_call_target="tpu_custom_call" | custom-call | flops 8388608 | bytes 6606848 | tf_op jit(solution)/shard_map/ray/pallas_call | solution.py:360
  52.3 15.0 %all_to_all.37 = bf16[128,8,128]{2,1,0:T(8,128)(2,1)S(1)} all-to-all(bf16[128,8,128]{2,1,0:T(8,128)(2,1)S(1)} %bitcast.33), channel_id=1, replica_groups=mesh['lat'=32,'rad'=4] {'lat','rad'}, dimensions={0} | all-to-all | bytes 524288 | tf_op jit(solution)/shard_map/all_to_all | solution.py:375
  67.3 1.5 %model.2 = (bf16[1024,128]{1,0:T(8,128)(2,1)S(1)}, f32[128,256]{1,0:T(8,128)S(1)}, f32[8,128]{1,0:T(8,128)S(1)}, f32[128,256]{1,0:T(8,128)S(1)}, f32[128,256]{1,0:T(8,128)S(1)}) custom-call(bf16[1024,128]{1,0:T(8,128)(2,1)S(1)} %bitcast.22, bf16[528,1024]{1,0:T(8,128)(2,1)S(1)} %get-tuple-element.45.refs_1_, ...), custom_call_target="tpu_custom_call" | custom-call | flops 8388608 | bytes 2531328 | tf_op jit(solution)/shard_map/model/pallas_call | solution.py:360
  68.8 15.0 %all_to_all.38 = bf16[128,8,128]{2,1,0:T(8,128)(2,1)S(1)} all-to-all(bf16[128,8,128]{2,1,0:T(8,128)(2,1)S(1)} %bitcast.29), channel_id=1, replica_groups=mesh['lat'=32,'rad'=4] {'lat','rad'}, dimensions={0} | all-to-all | bytes 524288 | tf_op jit(solution)/shard_map/all_to_all | solution.py:375
  83.8 3.6 %ray.3 = (bf16[1024,128]{1,0:T(8,128)(2,1)S(1)}, f32[32,64]{1,0:T(8,128)S(1)}, f32[256,128]{1,0:T(8,128)S(1)}, f32[8,128]{1,0:T(8,128)S(1)}) custom-call(bf16[1024,128]{1,0:T(8,128)(2,1)S(1)} %bitcast.24, bf16[8192,256]{1,0:T(8,128)(2,1)S(1)} %get-tuple-element.38.refs_1_, bf16[528,1024]{1,0:T(8,128)(2,1)S(1)} %get-tuple-element.39.refs_2_, ...), custom_call_target="tpu_custom_call" | custom-call | flops 8388608 | bytes 6737920 | tf_op jit(solution)/shard_map/ray/pallas_call | solution.py:360
  87.4 15.0 %all_to_all.39 = bf16[128,8,128]{2,1,0:T(8,128)(2,1)S(1)} all-to-all(bf16[128,8,128]{2,1,0:T(8,128)(2,1)S(1)} %bitcast.30), channel_id=1, replica_groups=mesh['lat'=32,'rad'=4] {'lat','rad'}, dimensions={0} | all-to-all | bytes 524288 | tf_op jit(solution)/shard_map/all_to_all | solution.py:375
  102.4 1.5 %model.3 = (bf16[1024,128]{1,0:T(8,128)(2,1)S(1)}, f32[128,256]{1,0:T(8,128)S(1)}, f32[8,128]{1,0:T(8,128)S(1)}, f32[128,256]{1,0:T(8,128)S(1)}, f32[128,256]{1,0:T(8,128)S(1)}) custom-call(bf16[1024,128]{1,0:T(8,128)(2,1)S(1)} %bitcast.27, bf16[528,1024]{1,0:T(8,128)(2,1)S(1)} %get-tuple-element.45.refs_1_, ...), custom_call_target="tpu_custom_call" | custom-call | flops 8388608 | bytes 2793472 | tf_op jit(solution)/shard_map/model/pallas_call | solution.py:360
  104.0 15.0 %all_to_all.40 = bf16[128,8,128]{2,1,0:T(8,128)(2,1)S(1)} all-to-all(bf16[128,8,128]{2,1,0:T(8,128)(2,1)S(1)} %bitcast.28), channel_id=1, replica_groups=mesh['lat'=32,'rad'=4] {'lat','rad'}, dimensions={0} | all-to-all | bytes 524288 | tf_op jit(solution)/shard_map/all_to_all | solution.py:375
  119.0 2.5 %last_ray.1 = (f32[128,128]{1,0:T(8,128)S(1)}, f32[32,64]{1,0:T(8,128)S(1)}, f32[8,128]{1,0:T(8,128)S(1)}) custom-call(bf16[1024,128]{1,0:T(8,128)(2,1)S(1)} %bitcast.23, bf16[8192,256]{1,0:T(8,128)(2,1)S(1)} %get-tuple-element.38.refs_1_, bf16[528,1024]{1,0:T(8,128)(2,1)S(1)} %get-tuple-element.39.refs_2_, f32[32,64]{1,0:T(8,128)S(1)} %get-tuple-element.41.refs_4_.refs_3_, ...), custom_call_target="tpu_custom_call" | custom-call | flops 8388608 | bytes 5689344 | tf_op jit(solution)/shard_map/last_ray/pallas_call | solution.py:360
  121.5 13.6 %all_to_all.41 = f32[128,1,128]{2,1,0:T(1,128)S(1)} all-to-all(f32[128,1,128]{2,1,0:T(1,128)S(1)} %bitcast.35), channel_id=1, replica_groups=mesh['lat'=32,'rad'=4] {'lat','rad'}, dimensions={0} | all-to-all | bytes 131072 | tf_op jit(solution)/shard_map/all_to_all | solution.py:375
  135.0 0.9 last.1
Async XLA Ops:
  0.6 2.2 %copy-start = (bf16[32,4,64,256]{3,2,1,0:T(8,128)(2,1)S(1)}, bf16[32,4,64,256]{3,2,1,0:T(8,128)(2,1)}, u32[]{:S(2)}) copy-start(bf16[32,4,64,256]{3,2,1,0:T(8,128)(2,1)} %param.6) | copy-start | bytes 12582916
  2.8 0.7 copy-start.1
  3.5 0.7 copy-start.2
  4.3 0.7 copy-start.3
  4.9 0.7 copy-start.4
  5.6 0.7 copy-start.5

commit v3 on v2

--- a/solution.py
+++ b/solution.py
@@ -224,9 +224,9 @@
     send_ref[...] = with_norm(packed, total(data * data))
 
 
-def send_field(send_ref, field, gather_ref):
-    halves = [field[:, :LANES], field[:, LANES:]]
-    packed = jnp.concatenate(halves + [half.T for half in halves], axis=0).astype(BF16)
+def send_field(send_ref, gathered, field, gather_ref):
+    cells = [gathered[:, half * LANES : (half + 1) * LANES].T for half in range(2)]
+    packed = jnp.concatenate([stacked(field)] + cells, axis=0).astype(BF16)
     send_ref[...] = with_norm(matmul(gather_ref[...], packed), total(field * field))
 
 
@@ -254,13 +254,14 @@
 
     got = matmul(scatter_ref[...], received)
     beta = norm_of(got[2 * blocks + 2 * devices :])
-    field = unstacked(got[: 2 * blocks]) / beta
+    gathered = unstacked(got[: 2 * blocks]).astype(BF16).astype(F32)
+    field = gathered / beta
     field_ref[...] = field
     state_ref[...] = scalars_row(beta)
-    send_field(send_ref, field, gather_ref)
-
-
-def ray_step(sweep, rads, received_ref, kernel_ref, pick_ref, weights_ref, data_ref, state_ref, pen_ref):
+    send_field(send_ref, gathered, field, gather_ref)
+
+
+def ray_step(sweep, rads, received_ref, kernel_ref, pick_ref, weights_ref, data_ref, state_ref, cells_ref):
     received = received_ref[...]
     ray_blocks, ray_len = data_ref.shape
     devices = received.shape[0] // CHUNK
@@ -273,38 +274,44 @@
     beta = state_ref[0:1, 0:1]
     data = weights_ref[...] * (products / alpha) - alpha * (data_ref[...] / beta)
     partial = total(data * data)
-    pens = []
+    pens, directions = [], []
     for j in range(2):
         cell = got[2 * entries + j * devices : 2 * entries + (j + 1) * devices]
-        pen = DAMPING * (roughen(cell, rads) / alpha)
         if sweep:
-            pen = pen - alpha * (pen_ref[j * devices : (j + 1) * devices] / beta)
+            rough, before, pen = [cells_ref[i, j * devices : (j + 1) * devices] for i in range(3)]
+            direction = ((cell + rough) / beta - beta * before) / alpha
+            pen = DAMPING * roughen(direction, rads) - alpha * (pen / beta)
+        else:
+            direction = cell / (beta * alpha)
+            pen = DAMPING * roughen(direction, rads)
         partial = partial + total(pen * pen)
         pens.append(pen)
-    return alpha, data, pens, partial
+        directions.append(direction)
+    return alpha, data, pens, directions, partial
 
 
 def ray_kernel(sweep, rads, *refs):
     received_ref, kernel_ref, pick_ref, place_ref, weights_ref, data_ref, state_ref = refs[:7]
-    pen_ref = refs[7] if sweep else None
-    send_ref, data_out, pen_out, alpha_out, partial_ref = refs[-5:]
-    alpha, data, pens, partial = ray_step(
-        sweep, rads, received_ref, kernel_ref, pick_ref, weights_ref, data_ref, state_ref, pen_ref
+    cells_ref = refs[7] if sweep else None
+    send_ref, data_out, cells_out, alpha_out, partial_ref = refs[-5:]
+    alpha, data, pens, directions, partial = ray_step(
+        sweep, rads, received_ref, kernel_ref, pick_ref, weights_ref, data_ref, state_ref, cells_ref
     )
     data_out[...] = data
-    pen_out[...] = jnp.concatenate(pens, axis=0)
     alpha_out[...] = scalars_row(alpha)
     ray_blocks = data.shape[0]
     fanout = partial_ref.shape[0] // ray_blocks
     adjoint_products(kernel_ref, weights_ref[...] * data, partial_ref, ray_blocks, fanout)
     rough = [DAMPING * roughen(pen, rads) for pen in pens]
+    for i, kept in enumerate((rough, directions, pens)):
+        cells_out[i] = jnp.concatenate(kept, axis=0)
     packed = jnp.concatenate([stacked(partial_ref[...])] + rough, axis=0).astype(BF16)
     send_ref[...] = with_norm(matmul(place_ref[...], packed), partial)
 
 
 def last_ray_kernel(sweep, rads, *refs):
     send_ref, data_out, alpha_out = refs[-3:]
-    alpha, data, pens, partial = ray_step(sweep, rads, *refs[:-3])
+    alpha, data, _, _, partial = ray_step(sweep, rads, *refs[:-3])
     data_out[...] = data
     alpha_out[...] = scalars_row(alpha)
     send_ref[...] = jnp.broadcast_to(partial, send_ref.shape)
@@ -341,9 +348,10 @@
         sweep, beta, field_ref, alpha_ref, state_ref, search_ref, update_ref
     )
     rough = [got[2 * blocks + j * devices : 2 * blocks + (j + 1) * devices].T for j in range(2)]
-    field = (unstacked(got[: 2 * blocks]) + jnp.concatenate(rough, axis=1)) / beta - beta * direction
+    gathered = unstacked(got[: 2 * blocks]).astype(BF16).astype(F32)
+    field = (gathered + jnp.concatenate(rough, axis=1)) / beta - beta * direction
     field_out[...] = field
-    send_field(send_ref, field, gather_ref)
+    send_field(send_ref, gathered, field, gather_ref)
     state_out[...] = state
     search_out[...] = search
     update_out[...] = update
@@ -405,25 +413,28 @@
             pltpu.VMEM((ray_blocks, ray_len), F32), partials,
             pltpu.SemaphoreType.DMA((5,)), pltpu.SemaphoreType.DMA((PARTS,)),
         ],
-        (kernel.reshape(entries * ray_len, cells), target_device.T, target_block.T,
-         counts.reshape(1, ray_blocks), traveltimes, prior_residual),
+        tuple(
+            pltpu.with_memory_space_constraint(x, pltpu.HBM)
+            for x in (kernel.reshape(entries * ray_len, cells), target_device.T, target_block.T,
+                      counts.reshape(1, ray_blocks), traveltimes, prior_residual)
+        ),
         flops, pltpu.HBM,
     )
     received = exchange(send, devices)
     send, field, state, gather, scatter = call(
         first_model_kernel, "first_model", [packet, model, scalar, places(blocks), picks(blocks)], [], (received,),
     )
-    carried, pens = (), ()
+    carried, kept = (), ()
     for sweep in range(ITERS):
         received = exchange(send, devices)
         if sweep == ITERS - 1:
             break
-        send, data, pen, alpha = call(
+        send, data, cell_state, alpha = call(
             functools.partial(ray_kernel, sweep, rads), "ray",
-            [packet, ray, ((2 * devices, blocks), F32), scalar], [partials],
-            (received, tiles, pick, place, weights, data, state) + pens, flops,
+            [packet, ray, ((3, 2 * devices, blocks), F32), scalar], [partials],
+            (received, tiles, pick, place, weights, data, state) + kept, flops,
         )
-        pens = (pen,)
+        kept = (cell_state,)
         received = exchange(send, devices)
         send, field, state, *carried = call(
             functools.partial(model_kernel, sweep), "model", [packet, model, scalar, model, model], [],
@@ -431,7 +442,7 @@
         )
     send, data, alpha = call(
         functools.partial(last_ray_kernel, ITERS - 1, rads), "last_ray", [((devices, LANES), F32), ray, scalar], [],
-        (received, tiles, pick, weights, data, state) + pens, flops,
+        (received, tiles, pick, weights, data, state) + kept, flops,
     )
     norms = exchange(send, devices)
     update, data = call(last_kernel, "last", [model, ray], [], (norms, data, field, alpha, state, *carried))

time: 136 us -> 132 us (0.971)
  local copies, waits for them, and re-layouts: 5.63 us -> 0 us
    unnamed x12 -> x0, local copies, waits for them, and re-layouts: 5.63 us -> none
where the time goes in v3:
time: 132 us
  blocking collectives  111 us (84%)
  Pallas kernels  19.7 us (15%)
    all_to_all x7, blocking collectives, exchange(): lax.all_to_all(chunks, AXES, split_axis=0, concat_axis=0, tiled=True)  111 us
    pallas_call x8, Pallas kernels, call(): pl.pallas_call(kernel, name=name, out_shape=[jax.ShapeDtypeStruct(shape,...  19.7 us

profile of v3, /device:TPU:1, one launch (start us, length us, event | category | flops | bytes accessed | tf_op | source)
XLA Modules:
  0.0 131.5 jit_solution(17936276854938330593)
XLA Ops:
  0.6 3.9 %start.1 = (bf16[1024,128]{1,0:T(8,128)(2,1)S(1)}, bf16[8192,256]{1,0:T(8,128)(2,1)S(1)}, f32[32,64]{1,0:T(8,128)S(1)}, f32[32,64]{1,0:T(8,128)S(1)}, bf16[528,1...) custom-call(bf16[8192,256]{1,0:T(8,128)(2,1)} %bitcast.35, s32[4,32]{1,0:T(4,128)} %bitcast.36, s32[4,32]{1,0:T(4,128)} %bitcast.37, ...), custom_call_target="tpu_custom_call" | custom-call | flops 8388608 | bytes 4211840 | tf_op jit(solution)/shard_map/start/pallas_call | solution.py:368
  4.5 22.6 %all_to_all.35 = bf16[128,8,128]{2,1,0:T(8,128)(2,1)S(1)} all-to-all(bf16[128,8,128]{2,1,0:T(8,128)(2,1)S(1)} %bitcast.30), channel_id=1, replica_groups=mesh['lat'=32,'rad'=4] {'lat','rad'}, dimensions={0} | all-to-all | bytes 524288 | tf_op jit(solution)/shard_map/all_to_all | solution.py:383
  27.1 2.1 %first_model.1 = (bf16[1024,128]{1,0:T(8,128)(2,1)S(1)}, f32[128,256]{1,0:T(8,128)S(1)}, f32[8,128]{1,0:T(8,128)S(1)}, bf16[1024,512]{1,0:T(8,128)(2,1)S(1)}, bf16[528,1024]{1,0:T(8,128)(2,1)S(1)}) custom-call(bf16[1024,128]{1,0:T(8,128)(2,1)S(1)} %bitcast.25), custom_call_target="tpu_custom_call" | custom-call | bytes 262144 | tf_op jit(solution)/shard_map/first_model/pallas_call | solution.py:368
  29.3 15.0 %all_to_all.36 = bf16[128,8,128]{2,1,0:T(8,128)(2,1)S(1)} all-to-all(bf16[128,8,128]{2,1,0:T(8,128)(2,1)S(1)} %bitcast.31), channel_id=1, replica_groups=mesh['lat'=32,'rad'=4] {'lat','rad'}, dimensions={0} | all-to-all | bytes 524288 | tf_op jit(solution)/shard_map/all_to_all | solution.py:383
  44.3 3.6 %ray.2 = (bf16[1024,128]{1,0:T(8,128)(2,1)S(1)}, f32[32,64]{1,0:T(8,128)S(1)}, f32[3,256,128]{2,1,0:T(8,128)S(1)}, f32[8,128]{1,0:T(8,128)S(1)}) custom-call(bf16[1024,128]{1,0:T(8,128)(2,1)S(1)} %bitcast.24, bf16[8192,256]{1,0:T(8,128)(2,1)S(1)} %get-tuple-element.38.refs_1_, bf16[528,1024]{1,0:T(8,128)(2,1)S(1)} %get-tuple-element.39.refs_2_, ...), custom_call_target="tpu_custom_call" | custom-call | flops 8388608 | bytes 6606848 | tf_op jit(solution)/shard_map/ray/pallas_call | solution.py:368
  47.9 15.0 %all_to_all.37 = bf16[128,8,128]{2,1,0:T(8,128)(2,1)S(1)} all-to-all(bf16[128,8,128]{2,1,0:T(8,128)(2,1)S(1)} %bitcast.32), channel_id=1, replica_groups=mesh['lat'=32,'rad'=4] {'lat','rad'}, dimensions={0} | all-to-all | bytes 524288 | tf_op jit(solution)/shard_map/all_to_all | solution.py:383
  62.9 1.5 %model.2 = (bf16[1024,128]{1,0:T(8,128)(2,1)S(1)}, f32[128,256]{1,0:T(8,128)S(1)}, f32[8,128]{1,0:T(8,128)S(1)}, f32[128,256]{1,0:T(8,128)S(1)}, f32[128,256]{1,0:T(8,128)S(1)}) custom-call(bf16[1024,128]{1,0:T(8,128)(2,1)S(1)} %bitcast.21, bf16[528,1024]{1,0:T(8,128)(2,1)S(1)} %get-tuple-element.45.refs_1_, ...), custom_call_target="tpu_custom_call" | custom-call | flops 8388608 | bytes 2531328 | tf_op jit(solution)/shard_map/model/pallas_call | solution.py:368
  64.4 15.0 %all_to_all.38 = bf16[128,8,128]{2,1,0:T(8,128)(2,1)S(1)} all-to-all(bf16[128,8,128]{2,1,0:T(8,128)(2,1)S(1)} %bitcast.28), channel_id=1, replica_groups=mesh['lat'=32,'rad'=4] {'lat','rad'}, dimensions={0} | all-to-all | bytes 524288 | tf_op jit(solution)/shard_map/all_to_all | solution.py:383
  79.4 3.7 %ray.3 = (bf16[1024,128]{1,0:T(8,128)(2,1)S(1)}, f32[32,64]{1,0:T(8,128)S(1)}, f32[3,256,128]{2,1,0:T(8,128)S(1)}, f32[8,128]{1,0:T(8,128)S(1)}) custom-call(bf16[1024,128]{1,0:T(8,128)(2,1)S(1)} %bitcast.23, bf16[8192,256]{1,0:T(8,128)(2,1)S(1)} %get-tuple-element.38.refs_1_, bf16[528,1024]{1,0:T(8,128)(2,1)S(1)} %get-tuple-element.39.refs_2_, ...), custom_call_target="tpu_custom_call" | custom-call | flops 8388608 | bytes 7000064 | tf_op jit(solution)/shard_map/ray/pallas_call | solution.py:368
  83.1 15.0 %all_to_all.39 = bf16[128,8,128]{2,1,0:T(8,128)(2,1)S(1)} all-to-all(bf16[128,8,128]{2,1,0:T(8,128)(2,1)S(1)} %bitcast.29), channel_id=1, replica_groups=mesh['lat'=32,'rad'=4] {'lat','rad'}, dimensions={0} | all-to-all | bytes 524288 | tf_op jit(solution)/shard_map/all_to_all | solution.py:383
  98.1 1.5 %model.3 = (bf16[1024,128]{1,0:T(8,128)(2,1)S(1)}, f32[128,256]{1,0:T(8,128)S(1)}, f32[8,128]{1,0:T(8,128)S(1)}, f32[128,256]{1,0:T(8,128)S(1)}, f32[128,256]{1,0:T(8,128)S(1)}) custom-call(bf16[1024,128]{1,0:T(8,128)(2,1)S(1)} %bitcast.26, bf16[528,1024]{1,0:T(8,128)(2,1)S(1)} %get-tuple-element.45.refs_1_, ...), custom_call_target="tpu_custom_call" | custom-call | flops 8388608 | bytes 2793472 | tf_op jit(solution)/shard_map/model/pallas_call | solution.py:368
  99.6 15.0 %all_to_all.40 = bf16[128,8,128]{2,1,0:T(8,128)(2,1)S(1)} all-to-all(bf16[128,8,128]{2,1,0:T(8,128)(2,1)S(1)} %bitcast.27), channel_id=1, replica_groups=mesh['lat'=32,'rad'=4] {'lat','rad'}, dimensions={0} | all-to-all | bytes 524288 | tf_op jit(solution)/shard_map/all_to_all | solution.py:383
  114.6 2.5 %last_ray.1 = (f32[128,128]{1,0:T(8,128)S(1)}, f32[32,64]{1,0:T(8,128)S(1)}, f32[8,128]{1,0:T(8,128)S(1)}) custom-call(bf16[1024,128]{1,0:T(8,128)(2,1)S(1)} %bitcast.22, bf16[8192,256]{1,0:T(8,128)(2,1)S(1)} %get-tuple-element.38.refs_1_, bf16[528,1024]{1,0:T(8,128)(2,1)S(1)} %get-tuple-element.39.refs_2_, f32[32,64]{1,0:T(8,128)S(1)} %get-tuple-element.41.refs_4_.refs_3_, ...), custom_call_target="tpu_custom_call" | custom-call | flops 8388608 | bytes 5951488 | tf_op jit(solution)/shard_map/last_ray/pallas_call | solution.py:368
  117.1 13.6 %all_to_all.41 = f32[128,1,128]{2,1,0:T(1,128)S(1)} all-to-all(f32[128,1,128]{2,1,0:T(1,128)S(1)} %bitcast.34), channel_id=1, replica_groups=mesh['lat'=32,'rad'=4] {'lat','rad'}, dimensions={0} | all-to-all | bytes 131072 | tf_op jit(solution)/shard_map/all_to_all | solution.py:383
  130.6 0.9 last.1

commit v4 on v3

--- a/solution.py
+++ b/solution.py
@@ -38,41 +38,30 @@
     return jnp.sum(jnp.sum(x, axis=1, keepdims=True), axis=0, keepdims=True)
 
 
-def norm_row(partial):
-    high = partial.astype(BF16).astype(F32)
-    middle = (partial - high).astype(BF16).astype(F32)
-    low = partial - high - middle
-    lane = iota((1, LANES), 1)
-    return jnp.where(lane == 0, high, jnp.where(lane == 1, middle, jnp.where(lane == 2, low, 0.0)))
-
-
-def with_norm(packed, partial):
-    rows = iota(packed.shape, 0) % CHUNK
-    return jnp.where(rows == NORM_ROW, norm_row(partial), packed).astype(BF16)
-
-
-def norm_of(sums):
-    lane = iota((1, LANES), 1)
-    return jnp.sqrt(jnp.sum(jnp.where(lane < 3, sums[0:1, :], 0.0), axis=1, keepdims=True))
-
-
 def ones_where(condition):
     return jnp.where(condition, 1.0, 0.0).astype(BF16)
 
 
-def write_cell_picks(ref, start, devices):
-    rows = devices * CHUNK
-    device, row = iota((devices, rows), 0), iota((devices, rows), 1)
-    for j in range(2):
-        ref[start + j * devices : start + (j + 1) * devices, :] = ones_where(row == device * CHUNK + CELL_ROW + j)
-    ref[start + 2 * devices :, :] = ones_where(iota((16, rows), 1) % CHUNK == NORM_ROW)
-
-
-def write_cell_places(ref, start, devices):
-    rows = devices * CHUNK
-    row, device = iota((rows, devices), 0), iota((rows, devices), 1)
-    for j in range(2):
-        ref[:, start + j * devices : start + (j + 1) * devices] = ones_where(row == device * CHUNK + CELL_ROW + j)
+def norm_row(partial, rest):
+    high = partial.astype(BF16).astype(F32)
+    lane = iota(rest.shape, 1)
+    return jnp.where(lane == 0, high, jnp.where(lane == 1, partial - high, rest))
+
+
+def norm_of(sums):
+    sums = jnp.where(iota(sums.shape, 1) < 2, sums, 0.0)
+    return jnp.sqrt(total(sums))
+
+
+def row_of(ref, j):
+    return ref.at[pl.ds(j, ref.shape[0] // CHUNK, stride=CHUNK), :]
+
+
+def pack(send_ref, stage_ref, named, *rest):
+    for j, rows in enumerate(rest):
+        row_of(stage_ref, NORM_ROW + j)[...] = rows
+    data = iota(named.shape, 0) % CHUNK < NORM_ROW
+    send_ref[...] = jnp.where(data, named, stage_ref[...]).astype(BF16)
 
 
 def stacked(x):
@@ -145,8 +134,8 @@
 
 def start_kernel(
     kernel_hbm, device_hbm, block_hbm, counts_hbm, times_hbm, prior_hbm,
-    send_ref, tiles_ref, weights_ref, data_ref, pick_ref, place_ref,
-    device_ref, block_ref, counts_ref, times_ref, prior_ref, partial_ref, small_sem, tile_sem,
+    send_ref, tiles_ref, weights_ref, data_ref, place_ref, pick_ref,
+    device_ref, block_ref, counts_ref, times_ref, prior_ref, partial_ref, stage_ref, small_sem, tile_sem,
 ):
     fanout, ray_blocks = device_ref.shape
     ray_len = times_ref.shape[1]
@@ -170,8 +159,6 @@
     ]
     for copy in small + large:
         copy.start()
-    write_cell_picks(pick_ref, 2 * entries, devices)
-    write_cell_places(place_ref, 2 * entries, devices)
     for copy in small:
         copy.wait()
 
@@ -194,10 +181,8 @@
     earlier = iota((entries, entries), 1) < iota((entries, entries), 0)
     rank = jnp.sum(jnp.where(earlier & (target == target_row), 1.0, 0.0), axis=1, keepdims=True)
     first = target * CHUNK + 2.0 * rank
-    first_row = as_row(first)
-
     to_col = first.astype(jnp.int32)
-    to_row = first_row.astype(jnp.int32)
+    to_row = as_row(first).astype(jnp.int32)
     for half in range(2):
         here = slice(half * entries, (half + 1) * entries)
         pick_ref[here, :] = ones_where(iota((entries, rows), 1) == to_col + half)
@@ -218,65 +203,63 @@
 
     adjoint_products(tiles_ref, weights * data, partial_ref, ray_blocks, fanout, ready)
     ids = jnp.where(iota((entries, LANES), 1).astype(F32) == rank, block + 1.0, 0.0).astype(BF16)
-    id_rows = (target_row * CHUNK + ID_ROW).astype(jnp.int32)
-    id_place = ones_where(iota((rows, entries), 0) == id_rows)
-    packed = matmul(place_ref[:, : 2 * entries], stacked(partial_ref[...].astype(BF16))) + matmul(id_place, ids)
-    send_ref[...] = with_norm(packed, total(data * data))
-
-
-def send_field(send_ref, gathered, field, gather_ref):
+    named_by = ones_where(iota((devices, entries), 0).astype(F32) == target_row)
+    zeros = jnp.zeros((devices, LANES), F32)
+    pack(
+        send_ref, stage_ref, matmul(place_ref[...], stacked(partial_ref[...].astype(BF16))),
+        norm_row(total(data * data), zeros), matmul(named_by, ids), zeros, zeros,
+    )
+
+
+def send_field(send_ref, stage_ref, gathered, field, gather_ref):
     cells = [gathered[:, half * LANES : (half + 1) * LANES].T for half in range(2)]
-    packed = jnp.concatenate([stacked(field)] + cells, axis=0).astype(BF16)
-    send_ref[...] = with_norm(matmul(gather_ref[...], packed), total(field * field))
-
-
-def first_model_kernel(received_ref, send_ref, field_ref, state_ref, gather_ref, scatter_ref):
+    zeros = jnp.zeros(cells[0].shape, F32)
+    norms = norm_row(total(field * field), zeros)
+    pack(send_ref, stage_ref, matmul(gather_ref[...], stacked(field).astype(BF16)), norms, zeros, *cells)
+
+
+def first_model_kernel(received_ref, send_ref, field_ref, state_ref, gather_ref, scatter_ref, stage_ref):
     received = received_ref[...]
     rows = received.shape[0]
-    devices = rows // CHUNK
     blocks = MB_R * MB_L
-    pick = ones_where(iota((devices, rows), 1) == iota((devices, rows), 0) * CHUNK + ID_ROW)
-    ids = matmul(pick, received).astype(BF16)
-    owner = ones_where(iota((rows, devices), 0) // CHUNK == iota((rows, devices), 1))
-    spread = matmul(owner, ids)
-    place = iota((rows, LANES), 0) % CHUNK
-    lane = iota((rows, LANES), 1)
-    slot = (place < NORM_ROW) & (lane == place // 2)
-    ident = jnp.sum(jnp.where(slot, spread, 0.0), axis=1, keepdims=True) - 1.0
-    hit = ident == lane.astype(F32)
+    stage_ref[...] = received.astype(F32)
+    beta = norm_of(row_of(stage_ref, NORM_ROW)[...])
+    ids = row_of(stage_ref, ID_ROW)[...]
+    for j in range(CHUNK):
+        ident = ids[:, j // 2 : j // 2 + 1] if j < NORM_ROW else 0.0
+        row_of(stage_ref, j)[...] = jnp.broadcast_to(ident, ids.shape)
+    hit = stage_ref[...] - 1.0 == iota((rows, LANES), 1).astype(F32)
+    odd = iota((rows, LANES), 0) % 2
     for half in range(2):
         here = slice(half * blocks, (half + 1) * blocks)
-        chosen = jnp.where(hit & (place % 2 == half), 1.0, 0.0)
+        chosen = jnp.where(hit & (odd == half), 1.0, 0.0)
         gather_ref[:, here] = chosen.astype(BF16)
         scatter_ref[here, :] = chosen.T.astype(BF16)
-    write_cell_picks(scatter_ref, 2 * blocks, devices)
-    write_cell_places(gather_ref, 2 * blocks, devices)
-
-    got = matmul(scatter_ref[...], received)
-    beta = norm_of(got[2 * blocks + 2 * devices :])
-    gathered = unstacked(got[: 2 * blocks]).astype(BF16).astype(F32)
+
+    gathered = unstacked(matmul(scatter_ref[...], received)).astype(BF16).astype(F32)
     field = gathered / beta
     field_ref[...] = field
     state_ref[...] = scalars_row(beta)
-    send_field(send_ref, gathered, field, gather_ref)
-
-
-def ray_step(sweep, rads, received_ref, kernel_ref, pick_ref, weights_ref, data_ref, state_ref, cells_ref):
+    send_field(send_ref, stage_ref, gathered, field, gather_ref)
+
+
+def ray_step(
+    sweep, rads, received_ref, tiles_ref, pick_ref, weights_ref, data_ref, state_ref, cells_ref, stage_ref,
+):
     received = received_ref[...]
     ray_blocks, ray_len = data_ref.shape
     devices = received.shape[0] // CHUNK
-    got = matmul(pick_ref[...], received)
-    entries = (got.shape[0] - 2 * devices - 16) // 2
-    fanout = entries // ray_blocks
-    alpha = norm_of(got[2 * entries + 2 * devices :])
-    blocks = unstacked(got[: 2 * entries]).astype(BF16)
-    products = forward_products(kernel_ref, blocks, ray_blocks, fanout, ray_len)
+    fanout = pick_ref.shape[0] // 2 // ray_blocks
+    blocks = unstacked(matmul(pick_ref[...], received)).astype(BF16)
+    stage_ref[...] = received.astype(F32)
+    alpha = norm_of(row_of(stage_ref, NORM_ROW)[...])
+    products = forward_products(tiles_ref, blocks, ray_blocks, fanout, ray_len)
     beta = state_ref[0:1, 0:1]
     data = weights_ref[...] * (products / alpha) - alpha * (data_ref[...] / beta)
     partial = total(data * data)
     pens, directions = [], []
     for j in range(2):
-        cell = got[2 * entries + j * devices : 2 * entries + (j + 1) * devices]
+        cell = row_of(stage_ref, CELL_ROW + j)[...]
         if sweep:
             rough, before, pen = [cells_ref[i, j * devices : (j + 1) * devices] for i in range(3)]
             direction = ((cell + rough) / beta - beta * before) / alpha
@@ -291,27 +274,31 @@
 
 
 def ray_kernel(sweep, rads, *refs):
-    received_ref, kernel_ref, pick_ref, place_ref, weights_ref, data_ref, state_ref = refs[:7]
+    received_ref, tiles_ref, pick_ref, weights_ref, data_ref, state_ref, place_ref = refs[:7]
     cells_ref = refs[7] if sweep else None
-    send_ref, data_out, cells_out, alpha_out, partial_ref = refs[-5:]
+    send_ref, data_out, cells_out, alpha_out, stage_ref, partial_ref = refs[-6:]
     alpha, data, pens, directions, partial = ray_step(
-        sweep, rads, received_ref, kernel_ref, pick_ref, weights_ref, data_ref, state_ref, cells_ref
+        sweep, rads, received_ref, tiles_ref, pick_ref, weights_ref, data_ref, state_ref, cells_ref, stage_ref
     )
     data_out[...] = data
     alpha_out[...] = scalars_row(alpha)
     ray_blocks = data.shape[0]
     fanout = partial_ref.shape[0] // ray_blocks
-    adjoint_products(kernel_ref, weights_ref[...] * data, partial_ref, ray_blocks, fanout)
+    adjoint_products(tiles_ref, weights_ref[...] * data, partial_ref, ray_blocks, fanout)
     rough = [DAMPING * roughen(pen, rads) for pen in pens]
     for i, kept in enumerate((rough, directions, pens)):
         cells_out[i] = jnp.concatenate(kept, axis=0)
-    packed = jnp.concatenate([stacked(partial_ref[...])] + rough, axis=0).astype(BF16)
-    send_ref[...] = with_norm(matmul(place_ref[...], packed), partial)
+    high = [x.astype(BF16).astype(F32) for x in rough]
+    low = [x - y for x, y in zip(rough, high)]
+    pack(
+        send_ref, stage_ref, matmul(place_ref[...], stacked(partial_ref[...]).astype(BF16)),
+        norm_row(partial, low[1]), low[0], *high,
+    )
 
 
 def last_ray_kernel(sweep, rads, *refs):
-    send_ref, data_out, alpha_out = refs[-3:]
-    alpha, data, _, _, partial = ray_step(sweep, rads, *refs[:-3])
+    send_ref, data_out, alpha_out, stage_ref = refs[-4:]
+    alpha, data, _, _, partial = ray_step(sweep, rads, *refs[:-4], stage_ref)
     data_out[...] = data
     alpha_out[...] = scalars_row(alpha)
     send_ref[...] = jnp.broadcast_to(partial, send_ref.shape)
@@ -338,20 +325,20 @@
 def model_kernel(sweep, *refs):
     received_ref, scatter_ref, gather_ref, field_ref, alpha_ref, state_ref = refs[:6]
     search_ref, update_ref = refs[6:8] if sweep else (None, None)
-    send_ref, field_out, state_out, search_out, update_out = refs[-5:]
+    send_ref, field_out, state_out, search_out, update_out, stage_ref = refs[-6:]
     received = received_ref[...]
-    devices = received.shape[0] // CHUNK
-    got = matmul(scatter_ref[...], received)
-    blocks = field_ref.shape[0]
-    beta = norm_of(got[2 * blocks + 2 * devices :])
+    gathered = unstacked(matmul(scatter_ref[...], received)).astype(BF16).astype(F32)
+    stage_ref[...] = received.astype(F32)
+    first = row_of(stage_ref, NORM_ROW)[...]
+    beta = norm_of(first)
+    low = [row_of(stage_ref, ID_ROW)[...], jnp.where(iota(first.shape, 1) < 2, 0.0, first)]
+    rough = [(row_of(stage_ref, CELL_ROW + j)[...] + low[j]).T for j in range(2)]
     direction, search, update, state = advance(
         sweep, beta, field_ref, alpha_ref, state_ref, search_ref, update_ref
     )
-    rough = [got[2 * blocks + j * devices : 2 * blocks + (j + 1) * devices].T for j in range(2)]
-    gathered = unstacked(got[: 2 * blocks]).astype(BF16).astype(F32)
     field = (gathered + jnp.concatenate(rough, axis=1)) / beta - beta * direction
     field_out[...] = field
-    send_field(send_ref, gathered, field, gather_ref)
+    send_field(send_ref, stage_ref, gathered, field, gather_ref)
     state_out[...] = state
     search_out[...] = search
     update_out[...] = update
@@ -372,7 +359,7 @@
         in_specs=[pl.BlockSpec(memory_space=space)] * len(operands),
         out_specs=[pl.BlockSpec(memory_space=pltpu.VMEM)] * len(outputs),
         scratch_shapes=scratch,
-        compiler_params=pltpu.CompilerParams(vmem_limit_bytes=40 << 20),
+        compiler_params=pltpu.CompilerParams(vmem_limit_bytes=12 << 20),
         cost_estimate=pl.CostEstimate(flops=flops, bytes_accessed=bytes_accessed, transcendentals=0),
     )(*operands)
 
@@ -398,19 +385,15 @@
     scalar = ((8, LANES), F32)
     partials = pltpu.VMEM((entries, cells), F32)
 
-    def picks(named):
-        return ((2 * named + 2 * devices + 16, rows), BF16)
-
-    def places(named):
-        return ((rows, 2 * named + 2 * devices), BF16)
-
-    send, tiles, weights, data, pick, place = call(
+    stage = pltpu.VMEM((rows, LANES), F32)
+    send, tiles, weights, data, place, pick = call(
         start_kernel, "start",
-        [packet, ((entries * ray_len, cells), BF16), ray, ray, picks(entries), places(entries)],
+        [packet, ((entries * ray_len, cells), BF16), ray, ray,
+         ((rows, 2 * entries), BF16), ((2 * entries, rows), BF16)],
         [
             pltpu.VMEM((fanout, ray_blocks), jnp.int32), pltpu.VMEM((fanout, ray_blocks), jnp.int32),
             pltpu.VMEM((1, ray_blocks), jnp.int32), pltpu.VMEM((ray_blocks, ray_len), F32),
-            pltpu.VMEM((ray_blocks, ray_len), F32), partials,
+            pltpu.VMEM((ray_blocks, ray_len), F32), partials, stage,
             pltpu.SemaphoreType.DMA((5,)), pltpu.SemaphoreType.DMA((PARTS,)),
         ],
         tuple(
@@ -422,7 +405,8 @@
     )
     received = exchange(send, devices)
     send, field, state, gather, scatter = call(
-        first_model_kernel, "first_model", [packet, model, scalar, places(blocks), picks(blocks)], [], (received,),
+        first_model_kernel, "first_model",
+        [packet, model, scalar, ((rows, 2 * blocks), BF16), ((2 * blocks, rows), BF16)], [stage], (received,),
     )
     carried, kept = (), ()
     for sweep in range(ITERS):
@@ -431,18 +415,18 @@
             break
         send, data, cell_state, alpha = call(
             functools.partial(ray_kernel, sweep, rads), "ray",
-            [packet, ray, ((3, 2 * devices, blocks), F32), scalar], [partials],
-            (received, tiles, pick, place, weights, data, state) + kept, flops,
+            [packet, ray, ((3, 2 * devices, blocks), F32), scalar], [stage, partials],
+            (received, tiles, pick, weights, data, state, place) + kept, flops,
         )
         kept = (cell_state,)
         received = exchange(send, devices)
         send, field, state, *carried = call(
-            functools.partial(model_kernel, sweep), "model", [packet, model, scalar, model, model], [],
+            functools.partial(model_kernel, sweep), "model", [packet, model, scalar, model, model], [stage],
             (received, scatter, gather, field, alpha, state, *carried), flops,
         )
     send, data, alpha = call(
-        functools.partial(last_ray_kernel, ITERS - 1, rads), "last_ray", [((devices, LANES), F32), ray, scalar], [],
-        (received, tiles, pick, weights, data, state) + kept, flops,
+        functools.partial(last_ray_kernel, ITERS - 1, rads), "last_ray", [((devices, LANES), F32), ray, scalar],
+        [stage], (received, tiles, pick, weights, data, state) + kept, flops,
     )
     norms = exchange(send, devices)
     update, data = call(last_kernel, "last", [model, ray], [], (norms, data, field, alpha, state, *carried))

time: 132 us -> 127 us (0.962)
  Pallas kernels: 19.7 us -> 15.2 us
    pallas_call x8, Pallas kernels: 19.7 us -> 15.2 us  [call(): pl.pallas_call(kernel, name=name, out_shape=[jax.ShapeDtypeStruct(shape,...]
where the time goes in v4:
time: 127 us
  blocking collectives  111 us (87%)
  Pallas kernels  15.2 us (12%)
    all_to_all x7, blocking collectives, exchange(): lax.all_to_all(chunks, AXES, split_axis=0, concat_axis=0, tiled=True)  111 us
    pallas_call x8, Pallas kernels, call(): pl.pallas_call(kernel, name=name, out_shape=[jax.ShapeDtypeStruct(shape,...  15.2 us

profile of v4, /device:TPU:1, one launch (start us, length us, event | category | flops | bytes accessed | tf_op | source)
XLA Modules:
  0.0 127.1 jit_solution(8244016584540619575)
XLA Ops:
  0.6 3.9 %start.1 = (bf16[1024,128]{1,0:T(8,128)(2,1)S(1)}, bf16[8192,256]{1,0:T(8,128)(2,1)S(1)}, f32[32,64]{1,0:T(8,128)S(1)}, f32[32,64]{1,0:T(8,128)S(1)}, bf16[1024,...) custom-call(bf16[8192,256]{1,0:T(8,128)(2,1)} %bitcast.35, s32[4,32]{1,0:T(4,128)} %bitcast.36, s32[4,32]{1,0:T(4,128)} %bitcast.37, ...), custom_call_target="tpu_custom_call" | custom-call | flops 8388608 | bytes 4211840 | tf_op jit(solution)/shard_map/start/pallas_call | solution.py:355
  4.5 22.6 %all_to_all.35 = bf16[128,8,128]{2,1,0:T(8,128)(2,1)S(1)} all-to-all(bf16[128,8,128]{2,1,0:T(8,128)(2,1)S(1)} %bitcast.30), channel_id=1, replica_groups=mesh['lat'=32,'rad'=4] {'lat','rad'}, dimensions={0} | all-to-all | bytes 524288 | tf_op jit(solution)/shard_map/all_to_all | solution.py:370
  27.2 0.9 first_model.1
  28.1 15.0 %all_to_all.36 = bf16[128,8,128]{2,1,0:T(8,128)(2,1)S(1)} all-to-all(bf16[128,8,128]{2,1,0:T(8,128)(2,1)S(1)} %bitcast.31), channel_id=1, replica_groups=mesh['lat'=32,'rad'=4] {'lat','rad'}, dimensions={0} | all-to-all | bytes 524288 | tf_op jit(solution)/shard_map/all_to_all | solution.py:370
  43.1 3.2 %ray.2 = (bf16[1024,128]{1,0:T(8,128)(2,1)S(1)}, f32[32,64]{1,0:T(8,128)S(1)}, f32[3,256,128]{2,1,0:T(8,128)S(1)}, f32[8,128]{1,0:T(8,128)S(1)}) custom-call(bf16[1024,128]{1,0:T(8,128)(2,1)S(1)} %bitcast.23, bf16[8192,256]{1,0:T(8,128)(2,1)S(1)} %get-tuple-element.38.refs_1_, bf16[256,1024]{1,0:T(8,128)(2,1)S(1)} %get-tuple-element.39.refs_2_, ...), custom_call_target="tpu_custom_call" | custom-call | flops 8388608 | bytes 5525504 | tf_op jit(solution)/shard_map/ray/pallas_call | solution.py:355
  46.3 15.0 %all_to_all.37 = bf16[128,8,128]{2,1,0:T(8,128)(2,1)S(1)} all-to-all(bf16[128,8,128]{2,1,0:T(8,128)(2,1)S(1)} %bitcast.32), channel_id=1, replica_groups=mesh['lat'=32,'rad'=4] {'lat','rad'}, dimensions={0} | all-to-all | bytes 524288 | tf_op jit(solution)/shard_map/all_to_all | solution.py:370
  61.3 0.6 model.2
  61.9 15.0 %all_to_all.38 = bf16[128,8,128]{2,1,0:T(8,128)(2,1)S(1)} all-to-all(bf16[128,8,128]{2,1,0:T(8,128)(2,1)S(1)} %bitcast.28), channel_id=1, replica_groups=mesh['lat'=32,'rad'=4] {'lat','rad'}, dimensions={0} | all-to-all | bytes 524288 | tf_op jit(solution)/shard_map/all_to_all | solution.py:370
  76.9 3.2 %ray.3 = (bf16[1024,128]{1,0:T(8,128)(2,1)S(1)}, f32[32,64]{1,0:T(8,128)S(1)}, f32[3,256,128]{2,1,0:T(8,128)S(1)}, f32[8,128]{1,0:T(8,128)S(1)}) custom-call(bf16[1024,128]{1,0:T(8,128)(2,1)S(1)} %bitcast.22, bf16[8192,256]{1,0:T(8,128)(2,1)S(1)} %get-tuple-element.38.refs_1_, bf16[256,1024]{1,0:T(8,128)(2,1)S(1)} %get-tuple-element.39.refs_2_, ...), custom_call_target="tpu_custom_call" | custom-call | flops 8388608 | bytes 5918720 | tf_op jit(solution)/shard_map/ray/pallas_call | solution.py:355
  80.0 15.0 %all_to_all.39 = bf16[128,8,128]{2,1,0:T(8,128)(2,1)S(1)} all-to-all(bf16[128,8,128]{2,1,0:T(8,128)(2,1)S(1)} %bitcast.29), channel_id=1, replica_groups=mesh['lat'=32,'rad'=4] {'lat','rad'}, dimensions={0} | all-to-all | bytes 524288 | tf_op jit(solution)/shard_map/all_to_all | solution.py:370
  95.0 0.6 model.3
  95.7 15.0 %all_to_all.40 = bf16[128,8,128]{2,1,0:T(8,128)(2,1)S(1)} all-to-all(bf16[128,8,128]{2,1,0:T(8,128)(2,1)S(1)} %bitcast.27), channel_id=1, replica_groups=mesh['lat'=32,'rad'=4] {'lat','rad'}, dimensions={0} | all-to-all | bytes 524288 | tf_op jit(solution)/shard_map/all_to_all | solution.py:370
  110.7 1.9 %last_ray.1 = (f32[128,128]{1,0:T(8,128)S(1)}, f32[32,64]{1,0:T(8,128)S(1)}, f32[8,128]{1,0:T(8,128)S(1)}) custom-call(bf16[1024,128]{1,0:T(8,128)(2,1)S(1)} %bitcast.21, bf16[8192,256]{1,0:T(8,128)(2,1)S(1)} %get-tuple-element.38.refs_1_, bf16[256,1024]{1,0:T(8,128)(2,1)S(1)} %get-tuple-element.39.refs_2_, f32[32,64]{1,0:T(8,128)S(1)} %get-tuple-element.40.refs_3_, ...), custom_call_target="tpu_custom_call" | custom-call | flops 8388608 | bytes 5394432 | tf_op jit(solution)/shard_map/last_ray/pallas_call | solution.py:355
  112.6 13.6 %all_to_all.41 = f32[128,1,128]{2,1,0:T(1,128)S(1)} all-to-all(f32[128,1,128]{2,1,0:T(1,128)S(1)} %bitcast.34), channel_id=1, replica_groups=mesh['lat'=32,'rad'=4] {'lat','rad'}, dimensions={0} | all-to-all | bytes 131072 | tf_op jit(solution)/shard_map/all_to_all | solution.py:370
  126.2 0.9 last.1

commit v5 on v4

--- a/solution.py
+++ b/solution.py
@@ -19,7 +19,7 @@
 ID_ROW = 5
 CELL_ROW = 6
 LANES = 128
-PARTS = 4
+GROUP = 8
 
 F32 = jnp.float32
 BF16 = jnp.bfloat16
@@ -73,37 +73,34 @@
     return jnp.concatenate([x[:half], x[half:]], axis=1)
 
 
-def adjoint_products(kernel_ref, y, out_ref, ray_blocks, fanout, ready=None):
+def forward_group(tiles_ref, blocks_ref, start, count, fanout, ray_len):
+    lane = iota((ray_len, LANES), 1)
+    sums = jnp.zeros((ray_len, LANES), F32)
+    for i in range(count):
+        products = None
+        for e in range((start + i) * fanout, (start + i + 1) * fanout):
+            product = tiles_ref[e * ray_len : (e + 1) * ray_len, :].astype(F32) * blocks_ref[e : e + 1, :]
+            product = product[:, :LANES] + product[:, LANES:]
+            products = product if products is None else products + product
+        sums = jnp.where(lane == i, jnp.sum(products, axis=1, keepdims=True), sums)
+    return sums.T[:count]
+
+
+def adjoint_group(tiles_ref, y, out_ref, start, fanout):
     high = y.astype(BF16).astype(F32)
     low = y - high
     high = jnp.concatenate([high] * fanout, axis=1)
     low = jnp.concatenate([low] * fanout, axis=1)
-    width = high.shape[1]
+    count, width = high.shape
     ray_len = width // fanout
     row, lane = iota((2 * fanout, width), 0), iota((2 * fanout, width), 1)
     own = lane // ray_len == row % fanout
-    for b in range(ray_blocks):
-        if ready is not None:
-            ready(b)
-        lhs = jnp.where(row < fanout, high[b : b + 1], low[b : b + 1])
+    for i in range(count):
+        b = start + i
+        lhs = jnp.where(row < fanout, high[i : i + 1], low[i : i + 1])
         lhs = jnp.where(own, lhs, 0.0).astype(BF16)
-        both = matmul(lhs, kernel_ref[b * width : (b + 1) * width, :])
+        both = matmul(lhs, tiles_ref[b * width : (b + 1) * width, :])
         out_ref[b * fanout : (b + 1) * fanout, :] = both[:fanout] + both[fanout:]
-
-
-def forward_products(kernel_ref, blocks, ray_blocks, fanout, ray_len):
-    entries = ray_blocks * fanout
-    lane = iota((ray_len, entries), 1)
-    picked = jnp.zeros((ray_len, entries), F32)
-    group = 16
-    for start in range(0, entries, group):
-        products = lax.dot_general(
-            kernel_ref[start * ray_len : (start + group) * ray_len, :], blocks, NT, preferred_element_type=F32
-        )
-        for i in range(group):
-            picked = jnp.where(lane == start + i, products[i * ray_len : (i + 1) * ray_len], picked)
-    member = jnp.where(iota((ray_blocks, entries), 1) // fanout == iota((ray_blocks, entries), 0), 1.0, 0.0)
-    return lax.dot_general(member, picked, NT, preferred_element_type=F32, precision=lax.Precision.HIGHEST)
 
 
 def roughen(cell, rads):
@@ -142,7 +139,6 @@
     entries = ray_blocks * fanout
     rows = send_ref.shape[0]
     devices = rows // CHUNK
-    part = tiles_ref.shape[0] // PARTS
 
     small = [
         pltpu.make_async_copy(source, target, small_sem.at[i])
@@ -151,13 +147,8 @@
              (times_hbm, times_ref), (prior_hbm, prior_ref))
         )
     ]
-    large = [
-        pltpu.make_async_copy(
-            kernel_hbm.at[pl.ds(i * part, part), :], tiles_ref.at[pl.ds(i * part, part), :], tile_sem.at[i]
-        )
-        for i in range(PARTS)
-    ]
-    for copy in small + large:
+    large = pltpu.make_async_copy(kernel_hbm, tiles_ref, tile_sem)
+    for copy in small + [large]:
         copy.start()
     for copy in small:
         copy.wait()
@@ -197,11 +188,8 @@
     data = weights * times_ref[...]
     data_ref[...] = data
 
-    def ready(b):
-        if b % (ray_blocks // PARTS) == 0:
-            large[b // (ray_blocks // PARTS)].wait()
-
-    adjoint_products(tiles_ref, weights * data, partial_ref, ray_blocks, fanout, ready)
+    large.wait()
+    adjoint_group(tiles_ref, weights * data, partial_ref, 0, fanout)
     ids = jnp.where(iota((entries, LANES), 1).astype(F32) == rank, block + 1.0, 0.0).astype(BF16)
     named_by = ones_where(iota((devices, entries), 0).astype(F32) == target_row)
     zeros = jnp.zeros((devices, LANES), F32)
@@ -244,18 +232,34 @@
 
 
 def ray_step(
-    sweep, rads, received_ref, tiles_ref, pick_ref, weights_ref, data_ref, state_ref, cells_ref, stage_ref,
+    sweep, rads, received_ref, tiles_ref, pick_ref, weights_ref, data_ref, state_ref, cells_ref, data_out, alpha_out,
+    stage_ref, blocks_ref, partial_ref=None,
 ):
     received = received_ref[...]
     ray_blocks, ray_len = data_ref.shape
     devices = received.shape[0] // CHUNK
-    fanout = pick_ref.shape[0] // 2 // ray_blocks
-    blocks = unstacked(matmul(pick_ref[...], received)).astype(BF16)
+    fanout = blocks_ref.shape[0] // ray_blocks
+    blocks_ref[...] = unstacked(matmul(pick_ref[...], received))
     stage_ref[...] = received.astype(F32)
     alpha = norm_of(row_of(stage_ref, NORM_ROW)[...])
-    products = forward_products(tiles_ref, blocks, ray_blocks, fanout, ray_len)
+    alpha_out[...] = scalars_row(alpha)
     beta = state_ref[0:1, 0:1]
-    data = weights_ref[...] * (products / alpha) - alpha * (data_ref[...] / beta)
+
+    waiting = None
+    for start in range(0, ray_blocks, GROUP):
+        here = slice(start, start + GROUP)
+        products = forward_group(tiles_ref, blocks_ref, start, GROUP, fanout, ray_len)
+        weights = weights_ref[here, :]
+        data = weights * (products / alpha) - alpha * (data_ref[here, :] / beta)
+        data_out[here, :] = data
+        if partial_ref is not None:
+            if waiting is not None:
+                adjoint_group(tiles_ref, waiting[0], partial_ref, waiting[1], fanout)
+            waiting = weights * data, start
+    if partial_ref is not None:
+        adjoint_group(tiles_ref, waiting[0], partial_ref, waiting[1], fanout)
+
+    data = data_out[...]
     partial = total(data * data)
     pens, directions = [], []
     for j in range(2):
@@ -270,21 +274,16 @@
         partial = partial + total(pen * pen)
         pens.append(pen)
         directions.append(direction)
-    return alpha, data, pens, directions, partial
+    return partial, pens, directions
 
 
 def ray_kernel(sweep, rads, *refs):
-    received_ref, tiles_ref, pick_ref, weights_ref, data_ref, state_ref, place_ref = refs[:7]
+    inputs, place_ref = refs[:6], refs[6]
     cells_ref = refs[7] if sweep else None
-    send_ref, data_out, cells_out, alpha_out, stage_ref, partial_ref = refs[-6:]
-    alpha, data, pens, directions, partial = ray_step(
-        sweep, rads, received_ref, tiles_ref, pick_ref, weights_ref, data_ref, state_ref, cells_ref, stage_ref
-    )
-    data_out[...] = data
-    alpha_out[...] = scalars_row(alpha)
-    ray_blocks = data.shape[0]
-    fanout = partial_ref.shape[0] // ray_blocks
-    adjoint_products(tiles_ref, weights_ref[...] * data, partial_ref, ray_blocks, fanout)
+    send_ref, data_out, cells_out, alpha_out, stage_ref, blocks_ref, partial_ref = refs[-7:]
+    partial, pens, directions = ray_step(
+        sweep, rads, *inputs, cells_ref, data_out, alpha_out, stage_ref, blocks_ref, partial_ref
+    )
     rough = [DAMPING * roughen(pen, rads) for pen in pens]
     for i, kept in enumerate((rough, directions, pens)):
         cells_out[i] = jnp.concatenate(kept, axis=0)
@@ -297,11 +296,9 @@
 
 
 def last_ray_kernel(sweep, rads, *refs):
-    send_ref, data_out, alpha_out, stage_ref = refs[-4:]
-    alpha, data, _, _, partial = ray_step(sweep, rads, *refs[:-4], stage_ref)
-    data_out[...] = data
-    alpha_out[...] = scalars_row(alpha)
-    send_ref[...] = jnp.broadcast_to(partial, send_ref.shape)
+    send_ref, data_out, alpha_out, stage_ref, blocks_ref = refs[-5:]
+    partial, _, _ = ray_step(sweep, rads, *refs[:-5], data_out, alpha_out, stage_ref, blocks_ref)
+    send_ref[...] = jnp.broadcast_to(partial.reshape(1, 1, 1), send_ref.shape)
 
 
 def advance(sweep, beta, field_ref, alpha_ref, state_ref, search_ref, update_ref):
@@ -345,7 +342,7 @@
 
 
 def last_kernel(norms_ref, data_ref, field_ref, alpha_ref, state_ref, search_ref, update_ref, update_out, data_out):
-    beta = jnp.sqrt(jnp.sum(norms_ref[...], axis=0, keepdims=True)[:, 0:1])
+    beta = jnp.sqrt(jnp.sum(norms_ref[...], axis=0))
     update_out[...] = advance(ITERS - 1, beta, field_ref, alpha_ref, state_ref, search_ref, update_ref)[2]
     data_out[...] = data_ref[...] / beta
 
@@ -394,7 +391,7 @@
             pltpu.VMEM((fanout, ray_blocks), jnp.int32), pltpu.VMEM((fanout, ray_blocks), jnp.int32),
             pltpu.VMEM((1, ray_blocks), jnp.int32), pltpu.VMEM((ray_blocks, ray_len), F32),
             pltpu.VMEM((ray_blocks, ray_len), F32), partials, stage,
-            pltpu.SemaphoreType.DMA((5,)), pltpu.SemaphoreType.DMA((PARTS,)),
+            pltpu.SemaphoreType.DMA((5,)), pltpu.SemaphoreType.DMA,
         ],
         tuple(
             pltpu.with_memory_space_constraint(x, pltpu.HBM)
@@ -415,7 +412,7 @@
             break
         send, data, cell_state, alpha = call(
             functools.partial(ray_kernel, sweep, rads), "ray",
-            [packet, ray, ((3, 2 * devices, blocks), F32), scalar], [stage, partials],
+            [packet, ray, ((3, 2 * devices, blocks), F32), scalar], [stage, partials, partials],
             (received, tiles, pick, weights, data, state, place) + kept, flops,
         )
         kept = (cell_state,)
@@ -425,10 +422,10 @@
             (received, scatter, gather, field, alpha, state, *carried), flops,
         )
     send, data, alpha = call(
-        functools.partial(last_ray_kernel, ITERS - 1, rads), "last_ray", [((devices, LANES), F32), ray, scalar],
-        [stage], (received, tiles, pick, weights, data, state) + kept, flops,
-    )
-    norms = exchange(send, devices)
+        functools.partial(last_ray_kernel, ITERS - 1, rads), "last_ray", [((devices, 1, 1), F32), ray, scalar],
+        [stage, partials], (received, tiles, pick, weights, data, state) + kept, flops,
+    )
+    norms = lax.all_to_all(send, AXES, split_axis=0, concat_axis=0, tiled=True)
     update, data = call(last_kernel, "last", [model, ray], [], (norms, data, field, alpha, state, *carried))
     return (update.reshape(MB_R, MB_L, cells), data)
 

time: 127 us -> 125 us (0.984)
  Pallas kernels: 15.2 us -> 12.9 us
    all_to_all x0 -> x1, blocking collectives: none -> 13.6 us  [body(): norms = lax.all_to_all(send, AXES, split_axis=0, concat_axis=0, tiled=True)]
    all_to_all x7 -> x6, blocking collectives: 111 us -> 97.7 us  [exchange(): lax.all_to_all(chunks, AXES, split_axis=0, concat_axis=0, tiled=True)]
    pallas_call x8, Pallas kernels: 15.2 us -> 12.9 us  [call(): pl.pallas_call(kernel, name=name, out_shape=[jax.ShapeDtypeStruct(shape,...]
where the time goes in v5:
time: 125 us
  blocking collectives  111 us (89%)
  Pallas kernels  12.9 us (10%)
    all_to_all x6, blocking collectives, exchange(): lax.all_to_all(chunks, AXES, split_axis=0, concat_axis=0, tiled=True)  97.7 us
    all_to_all x1, blocking collectives, body(): norms = lax.all_to_all(send, AXES, split_axis=0, concat_axis=0, tiled=True)  13.6 us
    pallas_call x8, Pallas kernels, call(): pl.pallas_call(kernel, name=name, out_shape=[jax.ShapeDtypeStruct(shape,...  12.9 us

profile of v5, /device:TPU:1, one launch (start us, length us, event | category | flops | bytes accessed | tf_op | source)
XLA Modules:
  0.0 124.8 jit_solution(9237832541316026432)
XLA Ops:
  0.6 3.4 %start.1 = (bf16[1024,128]{1,0:T(8,128)(2,1)S(1)}, bf16[8192,256]{1,0:T(8,128)(2,1)S(1)}, f32[32,64]{1,0:T(8,128)S(1)}, f32[32,64]{1,0:T(8,128)S(1)}, bf16[1024,...) custom-call(bf16[8192,256]{1,0:T(8,128)(2,1)} %bitcast.29, s32[4,32]{1,0:T(4,128)} %bitcast.30, s32[4,32]{1,0:T(4,128)} %bitcast.31, ...), custom_call_target="tpu_custom_call" | custom-call | flops 8388608 | bytes 4211840 | tf_op jit(solution)/shard_map/start/pallas_call | solution.py:352
  4.0 22.6 %all_to_all.35 = bf16[128,8,128]{2,1,0:T(8,128)(2,1)S(1)} all-to-all(bf16[128,8,128]{2,1,0:T(8,128)(2,1)S(1)} %bitcast.26), channel_id=1, replica_groups=mesh['lat'=32,'rad'=4] {'lat','rad'}, dimensions={0} | all-to-all | bytes 524288 | tf_op jit(solution)/shard_map/all_to_all | solution.py:367
  26.7 0.9 first_model.1
  27.6 15.0 %all_to_all.36 = bf16[128,8,128]{2,1,0:T(8,128)(2,1)S(1)} all-to-all(bf16[128,8,128]{2,1,0:T(8,128)(2,1)S(1)} %bitcast.27), channel_id=1, replica_groups=mesh['lat'=32,'rad'=4] {'lat','rad'}, dimensions={0} | all-to-all | bytes 524288 | tf_op jit(solution)/shard_map/all_to_all | solution.py:367
  42.6 2.3 %ray.2 = (bf16[1024,128]{1,0:T(8,128)(2,1)S(1)}, f32[32,64]{1,0:T(8,128)S(1)}, f32[3,256,128]{2,1,0:T(8,128)S(1)}, f32[8,128]{1,0:T(8,128)S(1)}) custom-call(bf16[1024,128]{1,0:T(8,128)(2,1)S(1)} %bitcast.19, bf16[8192,256]{1,0:T(8,128)(2,1)S(1)} %get-tuple-element.38.refs_1_, bf16[256,1024]{1,0:T(8,128)(2,1)S(1)} %get-tuple-element.39.refs_2_, ...), custom_call_target="tpu_custom_call" | custom-call | flops 8388608 | bytes 5525504 | tf_op jit(solution)/shard_map/ray/pallas_call | solution.py:352
  44.8 15.0 %all_to_all.37 = bf16[128,8,128]{2,1,0:T(8,128)(2,1)S(1)} all-to-all(bf16[128,8,128]{2,1,0:T(8,128)(2,1)S(1)} %bitcast.28), channel_id=1, replica_groups=mesh['lat'=32,'rad'=4] {'lat','rad'}, dimensions={0} | all-to-all | bytes 524288 | tf_op jit(solution)/shard_map/all_to_all | solution.py:367
  59.9 0.6 model.2
  60.5 15.0 %all_to_all.38 = bf16[128,8,128]{2,1,0:T(8,128)(2,1)S(1)} all-to-all(bf16[128,8,128]{2,1,0:T(8,128)(2,1)S(1)} %bitcast.24), channel_id=1, replica_groups=mesh['lat'=32,'rad'=4] {'lat','rad'}, dimensions={0} | all-to-all | bytes 524288 | tf_op jit(solution)/shard_map/all_to_all | solution.py:367
  75.5 2.3 %ray.3 = (bf16[1024,128]{1,0:T(8,128)(2,1)S(1)}, f32[32,64]{1,0:T(8,128)S(1)}, f32[3,256,128]{2,1,0:T(8,128)S(1)}, f32[8,128]{1,0:T(8,128)S(1)}) custom-call(bf16[1024,128]{1,0:T(8,128)(2,1)S(1)} %bitcast.18, bf16[8192,256]{1,0:T(8,128)(2,1)S(1)} %get-tuple-element.38.refs_1_, bf16[256,1024]{1,0:T(8,128)(2,1)S(1)} %get-tuple-element.39.refs_2_, ...), custom_call_target="tpu_custom_call" | custom-call | flops 8388608 | bytes 5918720 | tf_op jit(solution)/shard_map/ray/pallas_call | solution.py:352
  77.8 15.0 %all_to_all.39 = bf16[128,8,128]{2,1,0:T(8,128)(2,1)S(1)} all-to-all(bf16[128,8,128]{2,1,0:T(8,128)(2,1)S(1)} %bitcast.25), channel_id=1, replica_groups=mesh['lat'=32,'rad'=4] {'lat','rad'}, dimensions={0} | all-to-all | bytes 524288 | tf_op jit(solution)/shard_map/all_to_all | solution.py:367
  92.8 0.6 model.3
  93.4 15.0 %all_to_all.40 = bf16[128,8,128]{2,1,0:T(8,128)(2,1)S(1)} all-to-all(bf16[128,8,128]{2,1,0:T(8,128)(2,1)S(1)} %bitcast.23), channel_id=1, replica_groups=mesh['lat'=32,'rad'=4] {'lat','rad'}, dimensions={0} | all-to-all | bytes 524288 | tf_op jit(solution)/shard_map/all_to_all | solution.py:367
  108.4 1.8 %last_ray.1 = (f32[128,1,1]{2,1,0:T(1,128)S(1)}, f32[32,64]{1,0:T(8,128)S(1)}, f32[8,128]{1,0:T(8,128)S(1)}) custom-call(bf16[1024,128]{1,0:T(8,128)(2,1)S(1)} %bitcast.17, bf16[8192,256]{1,0:T(8,128)(2,1)S(1)} %get-tuple-element.38.refs_1_, bf16[256,1024]{1,0:T(8,128)(2,1)S(1)} %get-tuple-element.39.refs_2_, f32[32,64]{1,0:T(8,128)S(1)} %get-tuple-element.40.refs_3_, ...), custom_call_target="tpu_custom_call" | custom-call | flops 8388608 | bytes 5394432 | tf_op jit(solution)/shard_map/last_ray/pallas_call | solution.py:352
  110.2 13.6 %all_to_all.41.norms_ref = f32[128,1,1]{2,1,0:T(1,128)S(1)} all-to-all(f32[128,1,1]{2,1,0:T(1,128)S(1)} %get-tuple-element.62), channel_id=1, replica_groups=mesh['lat'=32,'rad'=4] {'lat','rad'}, dimensions={0} | all-to-all | bytes 1024 | tf_op jit(solution)/shard_map/all_to_all | solution.py:428
  123.8 1.0 last.1

commit v6 on v5

--- a/solution.py
+++ b/solution.py
@@ -225,7 +225,7 @@
         scatter_ref[here, :] = chosen.T.astype(BF16)
 
     gathered = unstacked(matmul(scatter_ref[...], received)).astype(BF16).astype(F32)
-    field = gathered / beta
+    field = gathered * (1.0 / beta)
     field_ref[...] = field
     state_ref[...] = scalars_row(beta)
     send_field(send_ref, stage_ref, gathered, field, gather_ref)
@@ -244,13 +244,15 @@
     alpha = norm_of(row_of(stage_ref, NORM_ROW)[...])
     alpha_out[...] = scalars_row(alpha)
     beta = state_ref[0:1, 0:1]
+    inverse_alpha, inverse_beta = 1.0 / alpha, 1.0 / beta
+    ratio = alpha / beta
 
     waiting = None
     for start in range(0, ray_blocks, GROUP):
         here = slice(start, start + GROUP)
         products = forward_group(tiles_ref, blocks_ref, start, GROUP, fanout, ray_len)
         weights = weights_ref[here, :]
-        data = weights * (products / alpha) - alpha * (data_ref[here, :] / beta)
+        data = weights * (products * inverse_alpha) - ratio * data_ref[here, :]
         data_out[here, :] = data
         if partial_ref is not None:
             if waiting is not None:
@@ -266,10 +268,10 @@
         cell = row_of(stage_ref, CELL_ROW + j)[...]
         if sweep:
             rough, before, pen = [cells_ref[i, j * devices : (j + 1) * devices] for i in range(3)]
-            direction = ((cell + rough) / beta - beta * before) / alpha
-            pen = DAMPING * roughen(direction, rads) - alpha * (pen / beta)
+            direction = ((cell + rough) * inverse_beta - beta * before) * inverse_alpha
+            pen = DAMPING * roughen(direction, rads) - ratio * pen
         else:
-            direction = cell / (beta * alpha)
+            direction = (cell * inverse_beta) * inverse_alpha
             pen = DAMPING * roughen(direction, rads)
         partial = partial + total(pen * pen)
         pens.append(pen)
@@ -298,25 +300,16 @@
 def last_ray_kernel(sweep, rads, *refs):
     send_ref, data_out, alpha_out, stage_ref, blocks_ref = refs[-5:]
     partial, _, _ = ray_step(sweep, rads, *refs[:-5], data_out, alpha_out, stage_ref, blocks_ref)
-    send_ref[...] = jnp.broadcast_to(partial.reshape(1, 1, 1), send_ref.shape)
-
-
-def advance(sweep, beta, field_ref, alpha_ref, state_ref, search_ref, update_ref):
+    send_ref[...] = jnp.broadcast_to(partial, send_ref.shape)
+
+
+def turn(sweep, field_ref, alpha_ref, state_ref, search_ref):
     alpha = alpha_ref[0:1, 0:1]
-    direction = field_ref[...] / alpha
-    if sweep:
-        phi_bar, rho, cosine, sine = [state_ref[0:1, i : i + 1] for i in range(1, 5)]
-        search = direction - (sine * alpha / rho) * search_ref[...]
-        rho_bar = -cosine * alpha
-    else:
-        phi_bar, rho_bar = state_ref[0:1, 0:1], alpha
-        search = direction
-    rho = jnp.sqrt(rho_bar * rho_bar + beta * beta)
-    cosine, sine = rho_bar / rho, beta / rho
-    update = (cosine * phi_bar / rho) * search
-    if sweep:
-        update = update_ref[...] + update
-    return direction, search, update, scalars_row(beta, sine * phi_bar, rho, cosine, sine)
+    direction = field_ref[...] * (1.0 / alpha)
+    if sweep == 0:
+        return direction, direction, state_ref[0:1, 0:1], alpha
+    phi_bar, rho, cosine, sine = [state_ref[0:1, i : i + 1] for i in range(1, 5)]
+    return direction, direction - (sine * alpha / rho) * search_ref[...], phi_bar, -cosine * alpha
 
 
 def model_kernel(sweep, *refs):
@@ -330,21 +323,24 @@
     beta = norm_of(first)
     low = [row_of(stage_ref, ID_ROW)[...], jnp.where(iota(first.shape, 1) < 2, 0.0, first)]
     rough = [(row_of(stage_ref, CELL_ROW + j)[...] + low[j]).T for j in range(2)]
-    direction, search, update, state = advance(
-        sweep, beta, field_ref, alpha_ref, state_ref, search_ref, update_ref
-    )
-    field = (gathered + jnp.concatenate(rough, axis=1)) / beta - beta * direction
+    direction, search, phi_bar, rho_bar = turn(sweep, field_ref, alpha_ref, state_ref, search_ref)
+    field = (gathered + jnp.concatenate(rough, axis=1)) * (1.0 / beta) - beta * direction
     field_out[...] = field
     send_field(send_ref, stage_ref, gathered, field, gather_ref)
-    state_out[...] = state
+    rho = jnp.sqrt(rho_bar * rho_bar + beta * beta)
+    cosine, sine = rho_bar / rho, beta / rho
+    state_out[...] = scalars_row(beta, sine * phi_bar, rho, cosine, sine)
     search_out[...] = search
-    update_out[...] = update
+    update = (cosine * phi_bar / rho) * search
+    update_out[...] = update_ref[...] + update if sweep else update
 
 
 def last_kernel(norms_ref, data_ref, field_ref, alpha_ref, state_ref, search_ref, update_ref, update_out, data_out):
-    beta = jnp.sqrt(jnp.sum(norms_ref[...], axis=0))
-    update_out[...] = advance(ITERS - 1, beta, field_ref, alpha_ref, state_ref, search_ref, update_ref)[2]
-    data_out[...] = data_ref[...] / beta
+    squares = jnp.sum(norms_ref[...], axis=0, keepdims=True)[:, 0:1]
+    _, search, phi_bar, rho_bar = turn(ITERS - 1, field_ref, alpha_ref, state_ref, search_ref)
+    step = rho_bar * phi_bar / (rho_bar * rho_bar + squares)
+    update_out[...] = update_ref[...] + step * search
+    data_out[...] = data_ref[...] * (1.0 / jnp.sqrt(squares))
 
 
 def call(kernel, name, outputs, scratch, operands, flops=0, space=pltpu.VMEM):
@@ -422,10 +418,10 @@
             (received, scatter, gather, field, alpha, state, *carried), flops,
         )
     send, data, alpha = call(
-        functools.partial(last_ray_kernel, ITERS - 1, rads), "last_ray", [((devices, 1, 1), F32), ray, scalar],
+        functools.partial(last_ray_kernel, ITERS - 1, rads), "last_ray", [((devices, LANES), F32), ray, scalar],
         [stage, partials], (received, tiles, pick, weights, data, state) + kept, flops,
     )
-    norms = lax.all_to_all(send, AXES, split_axis=0, concat_axis=0, tiled=True)
+    norms = exchange(send, devices)
     update, data = call(last_kernel, "last", [model, ray], [], (norms, data, field, alpha, state, *carried))
     return (update.reshape(MB_R, MB_L, cells), data)
 

time: 125 us -> 125 us (level)
    all_to_all x1 -> x0, blocking collectives: 13.6 us -> none  [body(): norms = lax.all_to_all(send, AXES, split_axis=0, concat_axis=0, tiled=True)]
    all_to_all x6 -> x7, blocking collectives: 97.7 us -> 111 us  [exchange(): lax.all_to_all(chunks, AXES, split_axis=0, concat_axis=0, tiled=True)]
where the time goes in v6:
time: 125 us
  blocking collectives  111 us (89%)
  Pallas kernels  12.7 us (10%)
    all_to_all x7, blocking collectives, exchange(): lax.all_to_all(chunks, AXES, split_axis=0, concat_axis=0, tiled=True)  111 us
    pallas_call x8, Pallas kernels, call(): pl.pallas_call(kernel, name=name, out_shape=[jax.ShapeDtypeStruct(shape,...  12.7 us

profile of v6, /device:TPU:1, one launch (start us, length us, event | category | flops | bytes accessed | tf_op | source)
XLA Modules:
  0.0 124.6 jit_solution(1186987763094330932)
XLA Ops:
  0.6 3.4 %start.1 = (bf16[1024,128]{1,0:T(8,128)(2,1)S(1)}, bf16[8192,256]{1,0:T(8,128)(2,1)S(1)}, f32[32,64]{1,0:T(8,128)S(1)}, f32[32,64]{1,0:T(8,128)S(1)}, bf16[1024,...) custom-call(bf16[8192,256]{1,0:T(8,128)(2,1)} %bitcast.35, s32[4,32]{1,0:T(4,128)} %bitcast.36, s32[4,32]{1,0:T(4,128)} %bitcast.37, ...), custom_call_target="tpu_custom_call" | custom-call | flops 8388608 | bytes 4211840 | tf_op jit(solution)/shard_map/start/pallas_call | solution.py:348
  4.0 22.6 %all_to_all.35 = bf16[128,8,128]{2,1,0:T(8,128)(2,1)S(1)} all-to-all(bf16[128,8,128]{2,1,0:T(8,128)(2,1)S(1)} %bitcast.30), channel_id=1, replica_groups=mesh['lat'=32,'rad'=4] {'lat','rad'}, dimensions={0} | all-to-all | bytes 524288 | tf_op jit(solution)/shard_map/all_to_all | solution.py:363
  26.7 0.9 first_model.1
  27.6 15.0 %all_to_all.36 = bf16[128,8,128]{2,1,0:T(8,128)(2,1)S(1)} all-to-all(bf16[128,8,128]{2,1,0:T(8,128)(2,1)S(1)} %bitcast.31), channel_id=1, replica_groups=mesh['lat'=32,'rad'=4] {'lat','rad'}, dimensions={0} | all-to-all | bytes 524288 | tf_op jit(solution)/shard_map/all_to_all | solution.py:363
  42.6 2.2 %ray.2 = (bf16[1024,128]{1,0:T(8,128)(2,1)S(1)}, f32[32,64]{1,0:T(8,128)S(1)}, f32[3,256,128]{2,1,0:T(8,128)S(1)}, f32[8,128]{1,0:T(8,128)S(1)}) custom-call(bf16[1024,128]{1,0:T(8,128)(2,1)S(1)} %bitcast.23, bf16[8192,256]{1,0:T(8,128)(2,1)S(1)} %get-tuple-element.38.refs_1_, bf16[256,1024]{1,0:T(8,128)(2,1)S(1)} %get-tuple-element.39.refs_2_, ...), custom_call_target="tpu_custom_call" | custom-call | flops 8388608 | bytes 5525504 | tf_op jit(solution)/shard_map/ray/pallas_call | solution.py:348
  44.8 15.0 %all_to_all.37 = bf16[128,8,128]{2,1,0:T(8,128)(2,1)S(1)} all-to-all(bf16[128,8,128]{2,1,0:T(8,128)(2,1)S(1)} %bitcast.32), channel_id=1, replica_groups=mesh['lat'=32,'rad'=4] {'lat','rad'}, dimensions={0} | all-to-all | bytes 524288 | tf_op jit(solution)/shard_map/all_to_all | solution.py:363
  59.8 0.6 model.2
  60.4 15.0 %all_to_all.38 = bf16[128,8,128]{2,1,0:T(8,128)(2,1)S(1)} all-to-all(bf16[128,8,128]{2,1,0:T(8,128)(2,1)S(1)} %bitcast.28), channel_id=1, replica_groups=mesh['lat'=32,'rad'=4] {'lat','rad'}, dimensions={0} | all-to-all | bytes 524288 | tf_op jit(solution)/shard_map/all_to_all | solution.py:363
  75.4 2.3 %ray.3 = (bf16[1024,128]{1,0:T(8,128)(2,1)S(1)}, f32[32,64]{1,0:T(8,128)S(1)}, f32[3,256,128]{2,1,0:T(8,128)S(1)}, f32[8,128]{1,0:T(8,128)S(1)}) custom-call(bf16[1024,128]{1,0:T(8,128)(2,1)S(1)} %bitcast.22, bf16[8192,256]{1,0:T(8,128)(2,1)S(1)} %get-tuple-element.38.refs_1_, bf16[256,1024]{1,0:T(8,128)(2,1)S(1)} %get-tuple-element.39.refs_2_, ...), custom_call_target="tpu_custom_call" | custom-call | flops 8388608 | bytes 5918720 | tf_op jit(solution)/shard_map/ray/pallas_call | solution.py:348
  77.7 15.0 %all_to_all.39 = bf16[128,8,128]{2,1,0:T(8,128)(2,1)S(1)} all-to-all(bf16[128,8,128]{2,1,0:T(8,128)(2,1)S(1)} %bitcast.29), channel_id=1, replica_groups=mesh['lat'=32,'rad'=4] {'lat','rad'}, dimensions={0} | all-to-all | bytes 524288 | tf_op jit(solution)/shard_map/all_to_all | solution.py:363
  92.7 0.6 model.3
  93.4 15.0 %all_to_all.40 = bf16[128,8,128]{2,1,0:T(8,128)(2,1)S(1)} all-to-all(bf16[128,8,128]{2,1,0:T(8,128)(2,1)S(1)} %bitcast.27), channel_id=1, replica_groups=mesh['lat'=32,'rad'=4] {'lat','rad'}, dimensions={0} | all-to-all | bytes 524288 | tf_op jit(solution)/shard_map/all_to_all | solution.py:363
  108.4 1.8 %last_ray.1 = (f32[128,128]{1,0:T(8,128)S(1)}, f32[32,64]{1,0:T(8,128)S(1)}, f32[8,128]{1,0:T(8,128)S(1)}) custom-call(bf16[1024,128]{1,0:T(8,128)(2,1)S(1)} %bitcast.21, bf16[8192,256]{1,0:T(8,128)(2,1)S(1)} %get-tuple-element.38.refs_1_, bf16[256,1024]{1,0:T(8,128)(2,1)S(1)} %get-tuple-element.39.refs_2_, f32[32,64]{1,0:T(8,128)S(1)} %get-tuple-element.40.refs_3_, ...), custom_call_target="tpu_custom_call" | custom-call | flops 8388608 | bytes 5394432 | tf_op jit(solution)/shard_map/last_ray/pallas_call | solution.py:348
  110.1 13.6 %all_to_all.41 = f32[128,1,128]{2,1,0:T(1,128)S(1)} all-to-all(f32[128,1,128]{2,1,0:T(1,128)S(1)} %bitcast.34), channel_id=1, replica_groups=mesh['lat'=32,'rad'=4] {'lat','rad'}, dimensions={0} | all-to-all | bytes 131072 | tf_op jit(solution)/shard_map/all_to_all | solution.py:363
  123.7 0.9 last.1

commit v7 on v6

--- a/solution.py
+++ b/solution.py
@@ -30,6 +30,16 @@
     return lax.broadcasted_iota(jnp.int32, shape, dim)
 
 
+def low(index, size):
+    assert size & (size - 1) == 0
+    return index & (size - 1)
+
+
+def high(index, size):
+    assert size & (size - 1) == 0
+    return lax.shift_right_logical(index, jnp.int32(size.bit_length() - 1))
+
+
 def matmul(a, b):
     return jnp.dot(a, b, preferred_element_type=F32)
 
@@ -43,9 +53,9 @@
 
 
 def norm_row(partial, rest):
-    high = partial.astype(BF16).astype(F32)
+    upper = partial.astype(BF16).astype(F32)
     lane = iota(rest.shape, 1)
-    return jnp.where(lane == 0, high, jnp.where(lane == 1, partial - high, rest))
+    return jnp.where(lane == 0, upper, jnp.where(lane == 1, partial - upper, rest))
 
 
 def norm_of(sums):
@@ -60,7 +70,7 @@
 def pack(send_ref, stage_ref, named, *rest):
     for j, rows in enumerate(rest):
         row_of(stage_ref, NORM_ROW + j)[...] = rows
-    data = iota(named.shape, 0) % CHUNK < NORM_ROW
+    data = low(iota(named.shape, 0), CHUNK) < NORM_ROW
     send_ref[...] = jnp.where(data, named, stage_ref[...]).astype(BF16)
 
 
@@ -86,28 +96,35 @@
     return sums.T[:count]
 
 
+def spread_rows(y, fanout):
+    upper = y.astype(BF16).astype(F32)
+    lower = y - upper
+    upper = jnp.concatenate([upper] * fanout, axis=1)
+    lower = jnp.concatenate([lower] * fanout, axis=1)
+    count, width = upper.shape
+    row, lane = iota((2 * fanout, width), 0), iota((2 * fanout, width), 1)
+    own = high(lane, width // fanout) == low(row, fanout)
+    return [
+        jnp.where(own, jnp.where(row < fanout, upper[i : i + 1], lower[i : i + 1]), 0.0) for i in range(count)
+    ]
+
+
+def adjoint_products(tiles_ref, lhs, out_ref, b, fanout):
+    width = lhs.shape[1]
+    both = matmul(lhs, tiles_ref[b * width : (b + 1) * width, :])
+    out_ref[b * fanout : (b + 1) * fanout, :] = both[:fanout] + both[fanout:]
+
+
 def adjoint_group(tiles_ref, y, out_ref, start, fanout):
-    high = y.astype(BF16).astype(F32)
-    low = y - high
-    high = jnp.concatenate([high] * fanout, axis=1)
-    low = jnp.concatenate([low] * fanout, axis=1)
-    count, width = high.shape
-    ray_len = width // fanout
-    row, lane = iota((2 * fanout, width), 0), iota((2 * fanout, width), 1)
-    own = lane // ray_len == row % fanout
-    for i in range(count):
-        b = start + i
-        lhs = jnp.where(row < fanout, high[i : i + 1], low[i : i + 1])
-        lhs = jnp.where(own, lhs, 0.0).astype(BF16)
-        both = matmul(lhs, tiles_ref[b * width : (b + 1) * width, :])
-        out_ref[b * fanout : (b + 1) * fanout, :] = both[:fanout] + both[fanout:]
+    for i, lhs in enumerate(spread_rows(y, fanout)):
+        adjoint_products(tiles_ref, lhs.astype(BF16), out_ref, start + i, fanout)
 
 
 def roughen(cell, rads):
     shape = cell.shape
     devices, blocks = shape
     device, block = iota(shape, 0), iota(shape, 1)
-    rad, place = device % rads, block % MB_L
+    rad, place = low(device, rads), low(block, MB_L)
     lanes = lambda x, step: pltpu.roll(x, step % blocks, 1)
     owner = lambda x, step: pltpu.roll(x, step % devices, 0)
     up = lanes(cell, MB_L)
@@ -132,7 +149,7 @@
 def start_kernel(
     kernel_hbm, device_hbm, block_hbm, counts_hbm, times_hbm, prior_hbm,
     send_ref, tiles_ref, weights_ref, data_ref, place_ref, pick_ref,
-    device_ref, block_ref, counts_ref, times_ref, prior_ref, partial_ref, stage_ref, small_sem, tile_sem,
+    device_ref, block_ref, counts_ref, times_ref, prior_ref, partial_ref, stage_ref, operand_ref, small_sem, tile_sem,
 ):
     fanout, ray_blocks = device_ref.shape
     ray_len = times_ref.shape[1]
@@ -153,8 +170,8 @@
     for copy in small:
         copy.wait()
 
-    member = ones_where(iota((entries, ray_blocks), 0) // fanout == iota((entries, ray_blocks), 1))
-    turn = iota((entries, fanout), 0) % fanout == iota((entries, fanout), 1)
+    member = ones_where(high(iota((entries, ray_blocks), 0), fanout) == iota((entries, ray_blocks), 1))
+    turn = low(iota((entries, fanout), 0), fanout) == iota((entries, fanout), 1)
 
     def column(table_ref):
         table = table_ref[...].astype(F32).astype(BF16)
@@ -188,15 +205,20 @@
     data = weights * times_ref[...]
     data_ref[...] = data
 
-    large.wait()
-    adjoint_group(tiles_ref, weights * data, partial_ref, 0, fanout)
+    operands = spread_rows(weights * data, fanout)
+    depth = 2 * fanout
+    for b in range(0, ray_blocks, 2):
+        operand_ref[b * depth : (b + 2) * depth, :] = jnp.concatenate(operands[b : b + 2], axis=0).astype(BF16)
     ids = jnp.where(iota((entries, LANES), 1).astype(F32) == rank, block + 1.0, 0.0).astype(BF16)
     named_by = ones_where(iota((devices, entries), 0).astype(F32) == target_row)
     zeros = jnp.zeros((devices, LANES), F32)
-    pack(
-        send_ref, stage_ref, matmul(place_ref[...], stacked(partial_ref[...].astype(BF16))),
-        norm_row(total(data * data), zeros), matmul(named_by, ids), zeros, zeros,
-    )
+    rest = norm_row(total(data * data), zeros), matmul(named_by, ids), zeros, zeros
+    for j, rows_of in enumerate(rest):
+        row_of(stage_ref, NORM_ROW + j)[...] = rows_of
+    large.wait()
+    for b in range(ray_blocks):
+        adjoint_products(tiles_ref, operand_ref[b * depth : (b + 1) * depth, :], partial_ref, b, fanout)
+    pack(send_ref, stage_ref, matmul(place_ref[...], stacked(partial_ref[...].astype(BF16))))
 
 
 def send_field(send_ref, stage_ref, gathered, field, gather_ref):
@@ -217,7 +239,7 @@
         ident = ids[:, j // 2 : j // 2 + 1] if j < NORM_ROW else 0.0
         row_of(stage_ref, j)[...] = jnp.broadcast_to(ident, ids.shape)
     hit = stage_ref[...] - 1.0 == iota((rows, LANES), 1).astype(F32)
-    odd = iota((rows, LANES), 0) % 2
+    odd = low(iota((rows, LANES), 0), 2)
     for half in range(2):
         here = slice(half * blocks, (half + 1) * blocks)
         chosen = jnp.where(hit & (odd == half), 1.0, 0.0)
@@ -289,11 +311,11 @@
     rough = [DAMPING * roughen(pen, rads) for pen in pens]
     for i, kept in enumerate((rough, directions, pens)):
         cells_out[i] = jnp.concatenate(kept, axis=0)
-    high = [x.astype(BF16).astype(F32) for x in rough]
-    low = [x - y for x, y in zip(rough, high)]
+    upper = [x.astype(BF16).astype(F32) for x in rough]
+    lower = [x - y for x, y in zip(rough, upper)]
     pack(
         send_ref, stage_ref, matmul(place_ref[...], stacked(partial_ref[...]).astype(BF16)),
-        norm_row(partial, low[1]), low[0], *high,
+        norm_row(partial, lower[1]), lower[0], *upper,
     )
 
 
@@ -321,8 +343,8 @@
     stage_ref[...] = received.astype(F32)
     first = row_of(stage_ref, NORM_ROW)[...]
     beta = norm_of(first)
-    low = [row_of(stage_ref, ID_ROW)[...], jnp.where(iota(first.shape, 1) < 2, 0.0, first)]
-    rough = [(row_of(stage_ref, CELL_ROW + j)[...] + low[j]).T for j in range(2)]
+    lower = [row_of(stage_ref, ID_ROW)[...], jnp.where(iota(first.shape, 1) < 2, 0.0, first)]
+    rough = [(row_of(stage_ref, CELL_ROW + j)[...] + lower[j]).T for j in range(2)]
     direction, search, phi_bar, rho_bar = turn(sweep, field_ref, alpha_ref, state_ref, search_ref)
     field = (gathered + jnp.concatenate(rough, axis=1)) * (1.0 / beta) - beta * direction
     field_out[...] = field
@@ -387,6 +409,7 @@
             pltpu.VMEM((fanout, ray_blocks), jnp.int32), pltpu.VMEM((fanout, ray_blocks), jnp.int32),
             pltpu.VMEM((1, ray_blocks), jnp.int32), pltpu.VMEM((ray_blocks, ray_len), F32),
             pltpu.VMEM((ray_blocks, ray_len), F32), partials, stage,
+            pltpu.VMEM((2 * entries, fanout * ray_len), BF16),
             pltpu.SemaphoreType.DMA((5,)), pltpu.SemaphoreType.DMA,
         ],
         tuple(

time: 125 us -> 125 us (level)
  no operation moved by 1% of the time
where the time goes in v7:
time: 125 us
  blocking collectives  111 us (89%)
  Pallas kernels  12.6 us (10%)
    all_to_all x7, blocking collectives, exchange(): lax.all_to_all(chunks, AXES, split_axis=0, concat_axis=0, tiled=True)  111 us
    pallas_call x8, Pallas kernels, call(): pl.pallas_call(kernel, name=name, out_shape=[jax.ShapeDtypeStruct(shape,...  12.6 us

profile of v7, /device:TPU:1, one launch (start us, length us, event | category | flops | bytes accessed | tf_op | source)
XLA Modules:
  0.0 124.5 jit_solution(18438132879289736736)
XLA Ops:
  0.6 3.3 %start.1 = (bf16[1024,128]{1,0:T(8,128)(2,1)S(1)}, bf16[8192,256]{1,0:T(8,128)(2,1)S(1)}, f32[32,64]{1,0:T(8,128)S(1)}, f32[32,64]{1,0:T(8,128)S(1)}, bf16[1024,...) custom-call(bf16[8192,256]{1,0:T(8,128)(2,1)} %bitcast.35, s32[4,32]{1,0:T(4,128)} %bitcast.36, s32[4,32]{1,0:T(4,128)} %bitcast.37, ...), custom_call_target="tpu_custom_call" | custom-call | flops 8388608 | bytes 4211840 | tf_op jit(solution)/shard_map/start/pallas_call | solution.py:370
  3.9 22.6 %all_to_all.35 = bf16[128,8,128]{2,1,0:T(8,128)(2,1)S(1)} all-to-all(bf16[128,8,128]{2,1,0:T(8,128)(2,1)S(1)} %bitcast.30), channel_id=1, replica_groups=mesh['lat'=32,'rad'=4] {'lat','rad'}, dimensions={0} | all-to-all | bytes 524288 | tf_op jit(solution)/shard_map/all_to_all | solution.py:385
  26.6 0.9 first_model.1
  27.5 15.0 %all_to_all.36 = bf16[128,8,128]{2,1,0:T(8,128)(2,1)S(1)} all-to-all(bf16[128,8,128]{2,1,0:T(8,128)(2,1)S(1)} %bitcast.31), channel_id=1, replica_groups=mesh['lat'=32,'rad'=4] {'lat','rad'}, dimensions={0} | all-to-all | bytes 524288 | tf_op jit(solution)/shard_map/all_to_all | solution.py:385
  42.5 2.3 %ray.2 = (bf16[1024,128]{1,0:T(8,128)(2,1)S(1)}, f32[32,64]{1,0:T(8,128)S(1)}, f32[3,256,128]{2,1,0:T(8,128)S(1)}, f32[8,128]{1,0:T(8,128)S(1)}) custom-call(bf16[1024,128]{1,0:T(8,128)(2,1)S(1)} %bitcast.23, bf16[8192,256]{1,0:T(8,128)(2,1)S(1)} %get-tuple-element.38.refs_1_, bf16[256,1024]{1,0:T(8,128)(2,1)S(1)} %get-tuple-element.39.refs_2_, ...), custom_call_target="tpu_custom_call" | custom-call | flops 8388608 | bytes 5525504 | tf_op jit(solution)/shard_map/ray/pallas_call | solution.py:370
  44.8 15.0 %all_to_all.37 = bf16[128,8,128]{2,1,0:T(8,128)(2,1)S(1)} all-to-all(bf16[128,8,128]{2,1,0:T(8,128)(2,1)S(1)} %bitcast.32), channel_id=1, replica_groups=mesh['lat'=32,'rad'=4] {'lat','rad'}, dimensions={0} | all-to-all | bytes 524288 | tf_op jit(solution)/shard_map/all_to_all | solution.py:385
  59.8 0.6 model.2
  60.4 15.0 %all_to_all.38 = bf16[128,8,128]{2,1,0:T(8,128)(2,1)S(1)} all-to-all(bf16[128,8,128]{2,1,0:T(8,128)(2,1)S(1)} %bitcast.28), channel_id=1, replica_groups=mesh['lat'=32,'rad'=4] {'lat','rad'}, dimensions={0} | all-to-all | bytes 524288 | tf_op jit(solution)/shard_map/all_to_all | solution.py:385
  75.3 2.3 %ray.3 = (bf16[1024,128]{1,0:T(8,128)(2,1)S(1)}, f32[32,64]{1,0:T(8,128)S(1)}, f32[3,256,128]{2,1,0:T(8,128)S(1)}, f32[8,128]{1,0:T(8,128)S(1)}) custom-call(bf16[1024,128]{1,0:T(8,128)(2,1)S(1)} %bitcast.22, bf16[8192,256]{1,0:T(8,128)(2,1)S(1)} %get-tuple-element.38.refs_1_, bf16[256,1024]{1,0:T(8,128)(2,1)S(1)} %get-tuple-element.39.refs_2_, ...), custom_call_target="tpu_custom_call" | custom-call | flops 8388608 | bytes 5918720 | tf_op jit(solution)/shard_map/ray/pallas_call | solution.py:370
  77.6 15.0 %all_to_all.39 = bf16[128,8,128]{2,1,0:T(8,128)(2,1)S(1)} all-to-all(bf16[128,8,128]{2,1,0:T(8,128)(2,1)S(1)} %bitcast.29), channel_id=1, replica_groups=mesh['lat'=32,'rad'=4] {'lat','rad'}, dimensions={0} | all-to-all | bytes 524288 | tf_op jit(solution)/shard_map/all_to_all | solution.py:385
  92.6 0.6 model.3
  93.3 15.0 %all_to_all.40 = bf16[128,8,128]{2,1,0:T(8,128)(2,1)S(1)} all-to-all(bf16[128,8,128]{2,1,0:T(8,128)(2,1)S(1)} %bitcast.27), channel_id=1, replica_groups=mesh['lat'=32,'rad'=4] {'lat','rad'}, dimensions={0} | all-to-all | bytes 524288 | tf_op jit(solution)/shard_map/all_to_all | solution.py:385
  108.3 1.8 %last_ray.1 = (f32[128,128]{1,0:T(8,128)S(1)}, f32[32,64]{1,0:T(8,128)S(1)}, f32[8,128]{1,0:T(8,128)S(1)}) custom-call(bf16[1024,128]{1,0:T(8,128)(2,1)S(1)} %bitcast.21, bf16[8192,256]{1,0:T(8,128)(2,1)S(1)} %get-tuple-element.38.refs_1_, bf16[256,1024]{1,0:T(8,128)(2,1)S(1)} %get-tuple-element.39.refs_2_, f32[32,64]{1,0:T(8,128)S(1)} %get-tuple-element.40.refs_3_, ...), custom_call_target="tpu_custom_call" | custom-call | flops 8388608 | bytes 5394432 | tf_op jit(solution)/shard_map/last_ray/pallas_call | solution.py:370
  110.1 13.6 %all_to_all.41 = f32[128,1,128]{2,1,0:T(1,128)S(1)} all-to-all(f32[128,1,128]{2,1,0:T(1,128)S(1)} %bitcast.34), channel_id=1, replica_groups=mesh['lat'=32,'rad'=4] {'lat','rad'}, dimensions={0} | all-to-all | bytes 131072 | tf_op jit(solution)/shard_map/all_to_all | solution.py:385
  123.6 0.9 last.1

commit v8 on v7

--- a/solution.py
+++ b/solution.py
@@ -120,22 +120,39 @@
         adjoint_products(tiles_ref, lhs.astype(BF16), out_ref, start + i, fanout)
 
 
-def roughen(cell, rads):
-    shape = cell.shape
-    devices, blocks = shape
-    device, block = iota(shape, 0), iota(shape, 1)
-    rad, place = low(device, rads), low(block, MB_L)
-    lanes = lambda x, step: pltpu.roll(x, step % blocks, 1)
-    owner = lambda x, step: pltpu.roll(x, step % devices, 0)
-    up = lanes(cell, MB_L)
-    north = jnp.where(block >= MB_L, up, jnp.where(rad > 0, owner(up, 1), 0.0))
-    down = lanes(cell, -MB_L)
-    south = jnp.where(block < blocks - MB_L, down, jnp.where(rad < rads - 1, owner(down, -1), 0.0))
-    far = owner(lanes(cell, 1 - MB_L), rads)
-    west = jnp.where(place > 0, lanes(cell, 1), jnp.where(device >= rads, far, 0.0))
-    far = owner(lanes(cell, MB_L - 1), -rads)
-    east = jnp.where(place < MB_L - 1, lanes(cell, -1), jnp.where(device < devices - rads, far, 0.0))
-    return 4.0 * cell - (south + north + east + west)
+def write_links(ref, blocks):
+    source, block = iota((blocks, blocks), 0), iota((blocks, blocks), 1)
+    place = low(block, MB_L)
+    links = (
+        (source == block - MB_L) | (source == block + MB_L)
+        | ((source == block - 1) & (place > 0)) | ((source == block + 1) & (place < MB_L - 1)),
+        source == block + blocks - MB_L,
+        source == block - blocks + MB_L,
+        (source == block + MB_L - 1) & (place == 0),
+        (source == block - MB_L + 1) & (place == MB_L - 1),
+    )
+    for i, link in enumerate(links):
+        for part in range(3):
+            ref[part * blocks : (part + 1) * blocks, i * blocks : (i + 1) * blocks] = ones_where(link)
+
+
+def roughen(cells, links_ref, rads):
+    rows, blocks = cells.shape
+    devices = rows // 2
+    upper = cells.astype(BF16)
+    rest = cells - upper.astype(F32)
+    middle = rest.astype(BF16)
+    lower = (rest - middle.astype(F32)).astype(BF16)
+    sums = matmul(jnp.concatenate([upper, middle, lower], axis=1), links_ref[...])
+    device = low(iota(cells.shape, 0), devices)
+    rad = low(device, rads)
+    piece = lambda i, step: pltpu.roll(sums[:, i * blocks : (i + 1) * blocks], step % rows, 0)
+    beside = sums[:, :blocks]
+    beside = beside + jnp.where(rad > 0, piece(1, 1), 0.0)
+    beside = beside + jnp.where(rad < rads - 1, piece(2, -1), 0.0)
+    beside = beside + jnp.where(device >= rads, piece(3, rads), 0.0)
+    beside = beside + jnp.where(device < devices - rads, piece(4, -rads), 0.0)
+    return 4.0 * cells - beside
 
 
 def scalars_row(*values):
@@ -148,7 +165,7 @@
 
 def start_kernel(
     kernel_hbm, device_hbm, block_hbm, counts_hbm, times_hbm, prior_hbm,
-    send_ref, tiles_ref, weights_ref, data_ref, place_ref, pick_ref,
+    send_ref, tiles_ref, weights_ref, data_ref, place_ref, pick_ref, links_ref,
     device_ref, block_ref, counts_ref, times_ref, prior_ref, partial_ref, stage_ref, operand_ref, small_sem, tile_sem,
 ):
     fanout, ray_blocks = device_ref.shape
@@ -167,6 +184,7 @@
     large = pltpu.make_async_copy(kernel_hbm, tiles_ref, tile_sem)
     for copy in small + [large]:
         copy.start()
+    write_links(links_ref, links_ref.shape[0] // 3)
     for copy in small:
         copy.wait()
 
@@ -254,7 +272,8 @@
 
 
 def ray_step(
-    sweep, rads, received_ref, tiles_ref, pick_ref, weights_ref, data_ref, state_ref, cells_ref, data_out, alpha_out,
+    sweep, rads, received_ref, tiles_ref, pick_ref, links_ref, weights_ref, data_ref, state_ref, cells_ref,
+    data_out, alpha_out,
     stage_ref, blocks_ref, partial_ref=None,
 ):
     received = received_ref[...]
@@ -284,38 +303,33 @@
         adjoint_group(tiles_ref, waiting[0], partial_ref, waiting[1], fanout)
 
     data = data_out[...]
-    partial = total(data * data)
-    pens, directions = [], []
-    for j in range(2):
-        cell = row_of(stage_ref, CELL_ROW + j)[...]
-        if sweep:
-            rough, before, pen = [cells_ref[i, j * devices : (j + 1) * devices] for i in range(3)]
-            direction = ((cell + rough) * inverse_beta - beta * before) * inverse_alpha
-            pen = DAMPING * roughen(direction, rads) - ratio * pen
-        else:
-            direction = (cell * inverse_beta) * inverse_alpha
-            pen = DAMPING * roughen(direction, rads)
-        partial = partial + total(pen * pen)
-        pens.append(pen)
-        directions.append(direction)
-    return partial, pens, directions
+    cell = jnp.concatenate([row_of(stage_ref, CELL_ROW + j)[...] for j in range(2)], axis=0)
+    if sweep:
+        direction = ((cell + cells_ref[0]) * inverse_beta - beta * cells_ref[1]) * inverse_alpha
+        pen = DAMPING * roughen(direction, links_ref, rads) - ratio * cells_ref[2]
+    else:
+        direction = (cell * inverse_beta) * inverse_alpha
+        pen = DAMPING * roughen(direction, links_ref, rads)
+    return total(data * data) + total(pen * pen), pen, direction
 
 
 def ray_kernel(sweep, rads, *refs):
-    inputs, place_ref = refs[:6], refs[6]
-    cells_ref = refs[7] if sweep else None
+    inputs, place_ref = refs[:7], refs[7]
+    links_ref = inputs[3]
+    cells_ref = refs[8] if sweep else None
     send_ref, data_out, cells_out, alpha_out, stage_ref, blocks_ref, partial_ref = refs[-7:]
-    partial, pens, directions = ray_step(
+    partial, pen, direction = ray_step(
         sweep, rads, *inputs, cells_ref, data_out, alpha_out, stage_ref, blocks_ref, partial_ref
     )
-    rough = [DAMPING * roughen(pen, rads) for pen in pens]
-    for i, kept in enumerate((rough, directions, pens)):
-        cells_out[i] = jnp.concatenate(kept, axis=0)
-    upper = [x.astype(BF16).astype(F32) for x in rough]
-    lower = [x - y for x, y in zip(rough, upper)]
+    rough = DAMPING * roughen(pen, links_ref, rads)
+    for i, kept in enumerate((rough, direction, pen)):
+        cells_out[i] = kept
+    upper = rough.astype(BF16).astype(F32)
+    lower = rough - upper
+    half = rough.shape[0] // 2
     pack(
         send_ref, stage_ref, matmul(place_ref[...], stacked(partial_ref[...]).astype(BF16)),
-        norm_row(partial, lower[1]), lower[0], *upper,
+        norm_row(partial, lower[half:]), lower[:half], upper[:half], upper[half:],
     )
 
 
@@ -401,10 +415,10 @@
     partials = pltpu.VMEM((entries, cells), F32)
 
     stage = pltpu.VMEM((rows, LANES), F32)
-    send, tiles, weights, data, place, pick = call(
+    send, tiles, weights, data, place, pick, links = call(
         start_kernel, "start",
         [packet, ((entries * ray_len, cells), BF16), ray, ray,
-         ((rows, 2 * entries), BF16), ((2 * entries, rows), BF16)],
+         ((rows, 2 * entries), BF16), ((2 * entries, rows), BF16), ((3 * blocks, 5 * blocks), BF16)],
         [
             pltpu.VMEM((fanout, ray_blocks), jnp.int32), pltpu.VMEM((fanout, ray_blocks), jnp.int32),
             pltpu.VMEM((1, ray_blocks), jnp.int32), pltpu.VMEM((ray_blocks, ray_len), F32),
@@ -432,7 +446,7 @@
         send, data, cell_state, alpha = call(
             functools.partial(ray_kernel, sweep, rads), "ray",
             [packet, ray, ((3, 2 * devices, blocks), F32), scalar], [stage, partials, partials],
-            (received, tiles, pick, weights, data, state, place) + kept, flops,
+            (received, tiles, pick, links, weights, data, state, place) + kept, flops,
         )
         kept = (cell_state,)
         received = exchange(send, devices)
@@ -442,7 +456,7 @@
         )
     send, data, alpha = call(
         functools.partial(last_ray_kernel, ITERS - 1, rads), "last_ray", [((devices, LANES), F32), ray, scalar],
-        [stage, partials], (received, tiles, pick, weights, data, state) + kept, flops,
+        [stage, partials], (received, tiles, pick, links, weights, data, state) + kept, flops,
     )
     norms = exchange(send, devices)
     update, data = call(last_kernel, "last", [model, ray], [], (norms, data, field, alpha, state, *carried))

time: 125 us -> 125 us (level)
  no operation moved by 1% of the time
where the time goes in v8:
time: 125 us
  blocking collectives  111 us (89%)
  Pallas kernels  12.8 us (10%)
    all_to_all x7, blocking collectives, exchange(): lax.all_to_all(chunks, AXES, split_axis=0, concat_axis=0, tiled=True)  111 us
    pallas_call x8, Pallas kernels, call(): pl.pallas_call(kernel, name=name, out_shape=[jax.ShapeDtypeStruct(shape,...  12.8 us

profile of v8, /device:TPU:1, one launch (start us, length us, event | category | flops | bytes accessed | tf_op | source)
XLA Modules:
  0.0 124.7 jit_solution(514215777478119727)
XLA Ops:
  0.6 3.3 %start.1 = (bf16[1024,128]{1,0:T(8,128)(2,1)S(1)}, bf16[8192,256]{1,0:T(8,128)(2,1)S(1)}, f32[32,64]{1,0:T(8,128)S(1)}, f32[32,64]{1,0:T(8,128)S(1)}, bf16[1024,...) custom-call(bf16[8192,256]{1,0:T(8,128)(2,1)} %bitcast.35, s32[4,32]{1,0:T(4,128)} %bitcast.36, ...), custom_call_target="tpu_custom_call" | custom-call | flops 8388608 | bytes 4211840 | tf_op jit(solution)/shard_map/start/pallas_call | solution.py:384
  3.9 22.6 %all_to_all.35 = bf16[128,8,128]{2,1,0:T(8,128)(2,1)S(1)} all-to-all(bf16[128,8,128]{2,1,0:T(8,128)(2,1)S(1)} %bitcast.30), channel_id=1, replica_groups=mesh['lat'=32,'rad'=4] {'lat','rad'}, dimensions={0} | all-to-all | bytes 524288 | tf_op jit(solution)/shard_map/all_to_all | solution.py:399
  26.6 0.9 first_model.1
  27.5 15.0 %all_to_all.36 = bf16[128,8,128]{2,1,0:T(8,128)(2,1)S(1)} all-to-all(bf16[128,8,128]{2,1,0:T(8,128)(2,1)S(1)} %bitcast.31), channel_id=1, replica_groups=mesh['lat'=32,'rad'=4] {'lat','rad'}, dimensions={0} | all-to-all | bytes 524288 | tf_op jit(solution)/shard_map/all_to_all | solution.py:399
  42.5 2.5 %ray.2 = (bf16[1024,128]{1,0:T(8,128)(2,1)S(1)}, f32[32,64]{1,0:T(8,128)S(1)}, f32[3,256,128]{2,1,0:T(8,128)S(1)}, f32[8,128]{1,0:T(8,128)S(1)}) custom-call(bf16[1024,128]{1,0:T(8,128)(2,1)S(1)} %bitcast.23, bf16[8192,256]{1,0:T(8,128)(2,1)S(1)} %get-tuple-element.39.refs_1_, bf16[256,1024]{1,0:T(8,128)(2,1)S(1)} %get-tuple-element.40.refs_2_, ...), custom_call_target="tpu_custom_call" | custom-call | flops 8388608 | bytes 6017024 | tf_op jit(solution)/shard_map/ray/pallas_call | solution.py:384
  44.9 15.0 %all_to_all.37 = bf16[128,8,128]{2,1,0:T(8,128)(2,1)S(1)} all-to-all(bf16[128,8,128]{2,1,0:T(8,128)(2,1)S(1)} %bitcast.32), channel_id=1, replica_groups=mesh['lat'=32,'rad'=4] {'lat','rad'}, dimensions={0} | all-to-all | bytes 524288 | tf_op jit(solution)/shard_map/all_to_all | solution.py:399
  59.9 0.6 model.2
  60.5 15.0 %all_to_all.38 = bf16[128,8,128]{2,1,0:T(8,128)(2,1)S(1)} all-to-all(bf16[128,8,128]{2,1,0:T(8,128)(2,1)S(1)} %bitcast.28), channel_id=1, replica_groups=mesh['lat'=32,'rad'=4] {'lat','rad'}, dimensions={0} | all-to-all | bytes 524288 | tf_op jit(solution)/shard_map/all_to_all | solution.py:399
  75.5 2.5 %ray.3 = (bf16[1024,128]{1,0:T(8,128)(2,1)S(1)}, f32[32,64]{1,0:T(8,128)S(1)}, f32[3,256,128]{2,1,0:T(8,128)S(1)}, f32[8,128]{1,0:T(8,128)S(1)}) custom-call(bf16[1024,128]{1,0:T(8,128)(2,1)S(1)} %bitcast.22, bf16[8192,256]{1,0:T(8,128)(2,1)S(1)} %get-tuple-element.39.refs_1_, bf16[256,1024]{1,0:T(8,128)(2,1)S(1)} %get-tuple-element.40.refs_2_, ...), custom_call_target="tpu_custom_call" | custom-call | flops 8388608 | bytes 6410240 | tf_op jit(solution)/shard_map/ray/pallas_call | solution.py:384
  78.0 15.0 %all_to_all.39 = bf16[128,8,128]{2,1,0:T(8,128)(2,1)S(1)} all-to-all(bf16[128,8,128]{2,1,0:T(8,128)(2,1)S(1)} %bitcast.29), channel_id=1, replica_groups=mesh['lat'=32,'rad'=4] {'lat','rad'}, dimensions={0} | all-to-all | bytes 524288 | tf_op jit(solution)/shard_map/all_to_all | solution.py:399
  93.0 0.6 model.3
  93.7 15.0 %all_to_all.40 = bf16[128,8,128]{2,1,0:T(8,128)(2,1)S(1)} all-to-all(bf16[128,8,128]{2,1,0:T(8,128)(2,1)S(1)} %bitcast.27), channel_id=1, replica_groups=mesh['lat'=32,'rad'=4] {'lat','rad'}, dimensions={0} | all-to-all | bytes 524288 | tf_op jit(solution)/shard_map/all_to_all | solution.py:399
  108.7 1.6 %last_ray.1 = (f32[128,128]{1,0:T(8,128)S(1)}, f32[32,64]{1,0:T(8,128)S(1)}, f32[8,128]{1,0:T(8,128)S(1)}) custom-call(bf16[1024,128]{1,0:T(8,128)(2,1)S(1)} %bitcast.21, bf16[8192,256]{1,0:T(8,128)(2,1)S(1)} %get-tuple-element.39.refs_1_, bf16[256,1024]{1,0:T(8,128)(2,1)S(1)} %get-tuple-element.40.refs_2_, bf16[384,640]{1,0:T(8,128)(2,1)S(1)} %get-tuple-element.41.refs_3_, ...), custom_call_target="tpu_custom_call" | custom-call | flops 8388608 | bytes 5885952 | tf_op jit(solution)/shard_map/last_ray/pallas_call | solution.py:384
  110.3 13.6 %all_to_all.41 = f32[128,1,128]{2,1,0:T(1,128)S(1)} all-to-all(f32[128,1,128]{2,1,0:T(1,128)S(1)} %bitcast.34), channel_id=1, replica_groups=mesh['lat'=32,'rad'=4] {'lat','rad'}, dimensions={0} | all-to-all | bytes 131072 | tf_op jit(solution)/shard_map/all_to_all | solution.py:399
  123.8 0.9 last.1

commit v9 on v8

--- a/solution.py
+++ b/solution.py
@@ -139,14 +139,24 @@
 def roughen(cells, links_ref, rads):
     rows, blocks = cells.shape
     devices = rows // 2
+    device, block = low(iota(cells.shape, 0), devices), iota(cells.shape, 1)
+    rad, place = low(device, rads), low(block, MB_L)
+    owner = lambda x, step: pltpu.roll(x, step % rows, 0)
+    lanes = lambda step: pltpu.roll(cells, step % blocks, 1)
+    if links_ref is None:
+        up, down = lanes(MB_L), lanes(-MB_L)
+        left, right = lanes(1 - MB_L), lanes(MB_L - 1)
+        north = jnp.where(block >= MB_L, up, jnp.where(rad > 0, owner(up, 1), 0.0))
+        south = jnp.where(block < blocks - MB_L, down, jnp.where(rad < rads - 1, owner(down, -1), 0.0))
+        west = jnp.where(place > 0, lanes(1), jnp.where(device >= rads, owner(left, rads), 0.0))
+        east = jnp.where(place < MB_L - 1, lanes(-1), jnp.where(device < devices - rads, owner(right, -rads), 0.0))
+        return 4.0 * cells - (south + north + east + west)
     upper = cells.astype(BF16)
     rest = cells - upper.astype(F32)
     middle = rest.astype(BF16)
     lower = (rest - middle.astype(F32)).astype(BF16)
     sums = matmul(jnp.concatenate([upper, middle, lower], axis=1), links_ref[...])
-    device = low(iota(cells.shape, 0), devices)
-    rad = low(device, rads)
-    piece = lambda i, step: pltpu.roll(sums[:, i * blocks : (i + 1) * blocks], step % rows, 0)
+    piece = lambda i, step: owner(sums[:, i * blocks : (i + 1) * blocks], step)
     beside = sums[:, :blocks]
     beside = beside + jnp.where(rad > 0, piece(1, 1), 0.0)
     beside = beside + jnp.where(rad < rads - 1, piece(2, -1), 0.0)
@@ -314,14 +324,13 @@
 
 
 def ray_kernel(sweep, rads, *refs):
-    inputs, place_ref = refs[:7], refs[7]
-    links_ref = inputs[3]
-    cells_ref = refs[8] if sweep else None
+    received_ref, tiles_ref, pick_ref, weights_ref, data_ref, state_ref, place_ref = refs[:7]
+    cells_ref = refs[7] if sweep else None
     send_ref, data_out, cells_out, alpha_out, stage_ref, blocks_ref, partial_ref = refs[-7:]
     partial, pen, direction = ray_step(
-        sweep, rads, *inputs, cells_ref, data_out, alpha_out, stage_ref, blocks_ref, partial_ref
-    )
-    rough = DAMPING * roughen(pen, links_ref, rads)
+        sweep, rads, received_ref, tiles_ref, pick_ref, None, weights_ref, data_ref, state_ref, cells_ref, data_out, alpha_out, stage_ref, blocks_ref, partial_ref
+    )
+    rough = DAMPING * roughen(pen, None, rads)
     for i, kept in enumerate((rough, direction, pen)):
         cells_out[i] = kept
     upper = rough.astype(BF16).astype(F32)
@@ -446,7 +455,7 @@
         send, data, cell_state, alpha = call(
             functools.partial(ray_kernel, sweep, rads), "ray",
             [packet, ray, ((3, 2 * devices, blocks), F32), scalar], [stage, partials, partials],
-            (received, tiles, pick, links, weights, data, state, place) + kept, flops,
+            (received, tiles, pick, weights, data, state, place) + kept, flops,
         )
         kept = (cell_state,)
         received = exchange(send, devices)

time: 125 us -> 125 us (level)
  no operation moved by 1% of the time
where the time goes in v9:
time: 125 us; the launch traced here: 124 us
  blocking collectives  111 us (89%)
  Pallas kernels  12.4 us (10%)
    all_to_all x7, blocking collectives, exchange(): lax.all_to_all(chunks, AXES, split_axis=0, concat_axis=0, tiled=True)  111 us
    pallas_call x8, Pallas kernels, call(): pl.pallas_call(kernel, name=name, out_shape=[jax.ShapeDtypeStruct(shape,...  12.4 us

profile of v9, /device:TPU:1, one launch (start us, length us, event | category | flops | bytes accessed | tf_op | source)
XLA Modules:
  0.0 124.2 jit_solution(2239537901831807712)
XLA Ops:
  0.6 3.3 %start.1 = (bf16[1024,128]{1,0:T(8,128)(2,1)S(1)}, bf16[8192,256]{1,0:T(8,128)(2,1)S(1)}, f32[32,64]{1,0:T(8,128)S(1)}, f32[32,64]{1,0:T(8,128)S(1)}, bf16[1024,...) custom-call(bf16[8192,256]{1,0:T(8,128)(2,1)} %bitcast.35, s32[4,32]{1,0:T(4,128)} %bitcast.36, ...), custom_call_target="tpu_custom_call" | custom-call | flops 8388608 | bytes 4211840 | tf_op jit(solution)/shard_map/start/pallas_call | solution.py:393
  3.9 22.6 %all_to_all.35 = bf16[128,8,128]{2,1,0:T(8,128)(2,1)S(1)} all-to-all(bf16[128,8,128]{2,1,0:T(8,128)(2,1)S(1)} %bitcast.30), channel_id=1, replica_groups=mesh['lat'=32,'rad'=4] {'lat','rad'}, dimensions={0} | all-to-all | bytes 524288 | tf_op jit(solution)/shard_map/all_to_all | solution.py:408
  26.6 0.9 first_model.1
  27.5 15.0 %all_to_all.36 = bf16[128,8,128]{2,1,0:T(8,128)(2,1)S(1)} all-to-all(bf16[128,8,128]{2,1,0:T(8,128)(2,1)S(1)} %bitcast.31), channel_id=1, replica_groups=mesh['lat'=32,'rad'=4] {'lat','rad'}, dimensions={0} | all-to-all | bytes 524288 | tf_op jit(solution)/shard_map/all_to_all | solution.py:408
  42.5 2.2 %ray.2 = (bf16[1024,128]{1,0:T(8,128)(2,1)S(1)}, f32[32,64]{1,0:T(8,128)S(1)}, f32[3,256,128]{2,1,0:T(8,128)S(1)}, f32[8,128]{1,0:T(8,128)S(1)}) custom-call(bf16[1024,128]{1,0:T(8,128)(2,1)S(1)} %bitcast.23, bf16[8192,256]{1,0:T(8,128)(2,1)S(1)} %get-tuple-element.39.refs_1_, bf16[256,1024]{1,0:T(8,128)(2,1)S(1)} %get-tuple-element.40.refs_2_, ...), custom_call_target="tpu_custom_call" | custom-call | flops 8388608 | bytes 5525504 | tf_op jit(solution)/shard_map/ray/pallas_call | solution.py:393
  44.7 15.0 %all_to_all.37 = bf16[128,8,128]{2,1,0:T(8,128)(2,1)S(1)} all-to-all(bf16[128,8,128]{2,1,0:T(8,128)(2,1)S(1)} %bitcast.32), channel_id=1, replica_groups=mesh['lat'=32,'rad'=4] {'lat','rad'}, dimensions={0} | all-to-all | bytes 524288 | tf_op jit(solution)/shard_map/all_to_all | solution.py:408
  59.7 0.6 model.2
  60.3 15.0 %all_to_all.38 = bf16[128,8,128]{2,1,0:T(8,128)(2,1)S(1)} all-to-all(bf16[128,8,128]{2,1,0:T(8,128)(2,1)S(1)} %bitcast.28), channel_id=1, replica_groups=mesh['lat'=32,'rad'=4] {'lat','rad'}, dimensions={0} | all-to-all | bytes 524288 | tf_op jit(solution)/shard_map/all_to_all | solution.py:408
  75.3 2.3 %ray.3 = (bf16[1024,128]{1,0:T(8,128)(2,1)S(1)}, f32[32,64]{1,0:T(8,128)S(1)}, f32[3,256,128]{2,1,0:T(8,128)S(1)}, f32[8,128]{1,0:T(8,128)S(1)}) custom-call(bf16[1024,128]{1,0:T(8,128)(2,1)S(1)} %bitcast.22, bf16[8192,256]{1,0:T(8,128)(2,1)S(1)} %get-tuple-element.39.refs_1_, bf16[256,1024]{1,0:T(8,128)(2,1)S(1)} %get-tuple-element.40.refs_2_, ...), custom_call_target="tpu_custom_call" | custom-call | flops 8388608 | bytes 5918720 | tf_op jit(solution)/shard_map/ray/pallas_call | solution.py:393
  77.6 15.0 %all_to_all.39 = bf16[128,8,128]{2,1,0:T(8,128)(2,1)S(1)} all-to-all(bf16[128,8,128]{2,1,0:T(8,128)(2,1)S(1)} %bitcast.29), channel_id=1, replica_groups=mesh['lat'=32,'rad'=4] {'lat','rad'}, dimensions={0} | all-to-all | bytes 524288 | tf_op jit(solution)/shard_map/all_to_all | solution.py:408
  92.6 0.6 model.3
  93.2 15.0 %all_to_all.40 = bf16[128,8,128]{2,1,0:T(8,128)(2,1)S(1)} all-to-all(bf16[128,8,128]{2,1,0:T(8,128)(2,1)S(1)} %bitcast.27), channel_id=1, replica_groups=mesh['lat'=32,'rad'=4] {'lat','rad'}, dimensions={0} | all-to-all | bytes 524288 | tf_op jit(solution)/shard_map/all_to_all | solution.py:408
  108.2 1.6 %last_ray.1 = (f32[128,128]{1,0:T(8,128)S(1)}, f32[32,64]{1,0:T(8,128)S(1)}, f32[8,128]{1,0:T(8,128)S(1)}) custom-call(bf16[1024,128]{1,0:T(8,128)(2,1)S(1)} %bitcast.21, bf16[8192,256]{1,0:T(8,128)(2,1)S(1)} %get-tuple-element.39.refs_1_, bf16[256,1024]{1,0:T(8,128)(2,1)S(1)} %get-tuple-element.40.refs_2_, bf16[384,640]{1,0:T(8,128)(2,1)S(1)} %get-tuple-element.60.refs_3_, ...), custom_call_target="tpu_custom_call" | custom-call | flops 8388608 | bytes 5885952 | tf_op jit(solution)/shard_map/last_ray/pallas_call | solution.py:393
  109.8 13.6 %all_to_all.41 = f32[128,1,128]{2,1,0:T(1,128)S(1)} all-to-all(f32[128,1,128]{2,1,0:T(1,128)S(1)} %bitcast.34), channel_id=1, replica_groups=mesh['lat'=32,'rad'=4] {'lat','rad'}, dimensions={0} | all-to-all | bytes 131072 | tf_op jit(solution)/shard_map/all_to_all | solution.py:408
  123.4 0.9 last.1

commit v10 on v9

--- a/solution.py
+++ b/solution.py
@@ -19,7 +19,7 @@
 ID_ROW = 5
 CELL_ROW = 6
 LANES = 128
-GROUP = 8
+GROUP = 16
 
 F32 = jnp.float32
 BF16 = jnp.bfloat16

time: 125 us -> 125 us (level)
  no operation moved by 1% of the time
where the time goes in v10:
time: 125 us; the launch traced here: 124 us
  blocking collectives  111 us (89%)
  Pallas kernels  12.4 us (10%)
    all_to_all x7, blocking collectives, exchange(): lax.all_to_all(chunks, AXES, split_axis=0, concat_axis=0, tiled=True)  111 us
    pallas_call x8, Pallas kernels, call(): pl.pallas_call(kernel, name=name, out_shape=[jax.ShapeDtypeStruct(shape,...  12.4 us

profile of v10, /device:TPU:1, one launch (start us, length us, event | category | flops | bytes accessed | tf_op | source)
XLA Modules:
  0.0 124.3 jit_solution(11119381197392742587)
XLA Ops:
  0.6 3.3 %start.1 = (bf16[1024,128]{1,0:T(8,128)(2,1)S(1)}, bf16[8192,256]{1,0:T(8,128)(2,1)S(1)}, f32[32,64]{1,0:T(8,128)S(1)}, f32[32,64]{1,0:T(8,128)S(1)}, bf16[1024,...) custom-call(bf16[8192,256]{1,0:T(8,128)(2,1)} %bitcast.35, s32[4,32]{1,0:T(4,128)} %bitcast.36, ...), custom_call_target="tpu_custom_call" | custom-call | flops 8388608 | bytes 4211840 | tf_op jit(solution)/shard_map/start/pallas_call | solution.py:393
  3.9 22.6 %all_to_all.35 = bf16[128,8,128]{2,1,0:T(8,128)(2,1)S(1)} all-to-all(bf16[128,8,128]{2,1,0:T(8,128)(2,1)S(1)} %bitcast.30), channel_id=1, replica_groups=mesh['lat'=32,'rad'=4] {'lat','rad'}, dimensions={0} | all-to-all | bytes 524288 | tf_op jit(solution)/shard_map/all_to_all | solution.py:408
  26.6 0.9 first_model.1
  27.5 15.0 %all_to_all.36 = bf16[128,8,128]{2,1,0:T(8,128)(2,1)S(1)} all-to-all(bf16[128,8,128]{2,1,0:T(8,128)(2,1)S(1)} %bitcast.31), channel_id=1, replica_groups=mesh['lat'=32,'rad'=4] {'lat','rad'}, dimensions={0} | all-to-all | bytes 524288 | tf_op jit(solution)/shard_map/all_to_all | solution.py:408
  42.5 2.3 %ray.2 = (bf16[1024,128]{1,0:T(8,128)(2,1)S(1)}, f32[32,64]{1,0:T(8,128)S(1)}, f32[3,256,128]{2,1,0:T(8,128)S(1)}, f32[8,128]{1,0:T(8,128)S(1)}) custom-call(bf16[1024,128]{1,0:T(8,128)(2,1)S(1)} %bitcast.23, bf16[8192,256]{1,0:T(8,128)(2,1)S(1)} %get-tuple-element.39.refs_1_, bf16[256,1024]{1,0:T(8,128)(2,1)S(1)} %get-tuple-element.40.refs_2_, ...), custom_call_target="tpu_custom_call" | custom-call | flops 8388608 | bytes 5525504 | tf_op jit(solution)/shard_map/ray/pallas_call | solution.py:393
  44.7 15.0 %all_to_all.37 = bf16[128,8,128]{2,1,0:T(8,128)(2,1)S(1)} all-to-all(bf16[128,8,128]{2,1,0:T(8,128)(2,1)S(1)} %bitcast.32), channel_id=1, replica_groups=mesh['lat'=32,'rad'=4] {'lat','rad'}, dimensions={0} | all-to-all | bytes 524288 | tf_op jit(solution)/shard_map/all_to_all | solution.py:408
  59.7 0.6 model.2
  60.3 15.0 %all_to_all.38 = bf16[128,8,128]{2,1,0:T(8,128)(2,1)S(1)} all-to-all(bf16[128,8,128]{2,1,0:T(8,128)(2,1)S(1)} %bitcast.28), channel_id=1, replica_groups=mesh['lat'=32,'rad'=4] {'lat','rad'}, dimensions={0} | all-to-all | bytes 524288 | tf_op jit(solution)/shard_map/all_to_all | solution.py:408
  75.3 2.3 %ray.3 = (bf16[1024,128]{1,0:T(8,128)(2,1)S(1)}, f32[32,64]{1,0:T(8,128)S(1)}, f32[3,256,128]{2,1,0:T(8,128)S(1)}, f32[8,128]{1,0:T(8,128)S(1)}) custom-call(bf16[1024,128]{1,0:T(8,128)(2,1)S(1)} %bitcast.22, bf16[8192,256]{1,0:T(8,128)(2,1)S(1)} %get-tuple-element.39.refs_1_, bf16[256,1024]{1,0:T(8,128)(2,1)S(1)} %get-tuple-element.40.refs_2_, ...), custom_call_target="tpu_custom_call" | custom-call | flops 8388608 | bytes 5918720 | tf_op jit(solution)/shard_map/ray/pallas_call | solution.py:393
  77.6 15.0 %all_to_all.39 = bf16[128,8,128]{2,1,0:T(8,128)(2,1)S(1)} all-to-all(bf16[128,8,128]{2,1,0:T(8,128)(2,1)S(1)} %bitcast.29), channel_id=1, replica_groups=mesh['lat'=32,'rad'=4] {'lat','rad'}, dimensions={0} | all-to-all | bytes 524288 | tf_op jit(solution)/shard_map/all_to_all | solution.py:408
  92.6 0.6 model.3
  93.2 15.0 %all_to_all.40 = bf16[128,8,128]{2,1,0:T(8,128)(2,1)S(1)} all-to-all(bf16[128,8,128]{2,1,0:T(8,128)(2,1)S(1)} %bitcast.27), channel_id=1, replica_groups=mesh['lat'=32,'rad'=4] {'lat','rad'}, dimensions={0} | all-to-all | bytes 524288 | tf_op jit(solution)/shard_map/all_to_all | solution.py:408
  108.2 1.6 %last_ray.1 = (f32[128,128]{1,0:T(8,128)S(1)}, f32[32,64]{1,0:T(8,128)S(1)}, f32[8,128]{1,0:T(8,128)S(1)}) custom-call(bf16[1024,128]{1,0:T(8,128)(2,1)S(1)} %bitcast.21, bf16[8192,256]{1,0:T(8,128)(2,1)S(1)} %get-tuple-element.39.refs_1_, bf16[256,1024]{1,0:T(8,128)(2,1)S(1)} %get-tuple-element.40.refs_2_, bf16[384,640]{1,0:T(8,128)(2,1)S(1)} %get-tuple-element.60.refs_3_, ...), custom_call_target="tpu_custom_call" | custom-call | flops 8388608 | bytes 5885952 | tf_op jit(solution)/shard_map/last_ray/pallas_call | solution.py:393
  109.8 13.6 %all_to_all.41 = f32[128,1,128]{2,1,0:T(1,128)S(1)} all-to-all(f32[128,1,128]{2,1,0:T(1,128)S(1)} %bitcast.34), channel_id=1, replica_groups=mesh['lat'=32,'rad'=4] {'lat','rad'}, dimensions={0} | all-to-all | bytes 131072 | tf_op jit(solution)/shard_map/all_to_all | solution.py:408
  123.4 0.9 last.1

commit v11 on v10

--- a/solution.py
+++ b/solution.py
@@ -324,11 +324,11 @@
 
 
 def ray_kernel(sweep, rads, *refs):
-    received_ref, tiles_ref, pick_ref, weights_ref, data_ref, state_ref, place_ref = refs[:7]
-    cells_ref = refs[7] if sweep else None
+    inputs, place_ref = refs[:7], refs[7]
+    cells_ref = refs[8] if sweep else None
     send_ref, data_out, cells_out, alpha_out, stage_ref, blocks_ref, partial_ref = refs[-7:]
     partial, pen, direction = ray_step(
-        sweep, rads, received_ref, tiles_ref, pick_ref, None, weights_ref, data_ref, state_ref, cells_ref, data_out, alpha_out, stage_ref, blocks_ref, partial_ref
+        sweep, rads, *inputs, cells_ref, data_out, alpha_out, stage_ref, blocks_ref, partial_ref
     )
     rough = DAMPING * roughen(pen, None, rads)
     for i, kept in enumerate((rough, direction, pen)):
@@ -455,7 +455,7 @@
         send, data, cell_state, alpha = call(
             functools.partial(ray_kernel, sweep, rads), "ray",
             [packet, ray, ((3, 2 * devices, blocks), F32), scalar], [stage, partials, partials],
-            (received, tiles, pick, weights, data, state, place) + kept, flops,
+            (received, tiles, pick, links, weights, data, state, place) + kept, flops,
         )
         kept = (cell_state,)
         received = exchange(send, devices)

time: 125 us -> 126 us (level)
  no operation moved by 1% of the time
where the time goes in v11:
time: 126 us; the launch traced here: 125 us
  blocking collectives  111 us (88%)
  Pallas kernels  13.6 us (11%)
    all_to_all x7, blocking collectives, exchange(): lax.all_to_all(chunks, AXES, split_axis=0, concat_axis=0, tiled=True)  111 us
    pallas_call x8, Pallas kernels, call(): pl.pallas_call(kernel, name=name, out_shape=[jax.ShapeDtypeStruct(shape,...  13.6 us

profile of v11, /device:TPU:1, one launch (start us, length us, event | category | flops | bytes accessed | tf_op | source)
XLA Modules:
  0.0 125.5 jit_solution(14541871739388578959)
XLA Ops:
  0.6 3.3 %start.1 = (bf16[1024,128]{1,0:T(8,128)(2,1)S(1)}, bf16[8192,256]{1,0:T(8,128)(2,1)S(1)}, f32[32,64]{1,0:T(8,128)S(1)}, f32[32,64]{1,0:T(8,128)S(1)}, bf16[1024,...) custom-call(bf16[8192,256]{1,0:T(8,128)(2,1)} %bitcast.35, s32[4,32]{1,0:T(4,128)} %bitcast.36, ...), custom_call_target="tpu_custom_call" | custom-call | flops 8388608 | bytes 4211840 | tf_op jit(solution)/shard_map/start/pallas_call | solution.py:393
  3.9 22.6 %all_to_all.35 = bf16[128,8,128]{2,1,0:T(8,128)(2,1)S(1)} all-to-all(bf16[128,8,128]{2,1,0:T(8,128)(2,1)S(1)} %bitcast.30), channel_id=1, replica_groups=mesh['lat'=32,'rad'=4] {'lat','rad'}, dimensions={0} | all-to-all | bytes 524288 | tf_op jit(solution)/shard_map/all_to_all | solution.py:408
  26.6 0.9 first_model.1
  27.5 15.0 %all_to_all.36 = bf16[128,8,128]{2,1,0:T(8,128)(2,1)S(1)} all-to-all(bf16[128,8,128]{2,1,0:T(8,128)(2,1)S(1)} %bitcast.31), channel_id=1, replica_groups=mesh['lat'=32,'rad'=4] {'lat','rad'}, dimensions={0} | all-to-all | bytes 524288 | tf_op jit(solution)/shard_map/all_to_all | solution.py:408
  42.5 2.8 %ray.2 = (bf16[1024,128]{1,0:T(8,128)(2,1)S(1)}, f32[32,64]{1,0:T(8,128)S(1)}, f32[3,256,128]{2,1,0:T(8,128)S(1)}, f32[8,128]{1,0:T(8,128)S(1)}) custom-call(bf16[1024,128]{1,0:T(8,128)(2,1)S(1)} %bitcast.23, bf16[8192,256]{1,0:T(8,128)(2,1)S(1)} %get-tuple-element.39.refs_1_, bf16[256,1024]{1,0:T(8,128)(2,1)S(1)} %get-tuple-element.40.refs_2_, ...), custom_call_target="tpu_custom_call" | custom-call | flops 8388608 | bytes 6017024 | tf_op jit(solution)/shard_map/ray/pallas_call | solution.py:393
  45.3 15.0 %all_to_all.37 = bf16[128,8,128]{2,1,0:T(8,128)(2,1)S(1)} all-to-all(bf16[128,8,128]{2,1,0:T(8,128)(2,1)S(1)} %bitcast.32), channel_id=1, replica_groups=mesh['lat'=32,'rad'=4] {'lat','rad'}, dimensions={0} | all-to-all | bytes 524288 | tf_op jit(solution)/shard_map/all_to_all | solution.py:408
  60.3 0.6 model.2
  60.9 15.0 %all_to_all.38 = bf16[128,8,128]{2,1,0:T(8,128)(2,1)S(1)} all-to-all(bf16[128,8,128]{2,1,0:T(8,128)(2,1)S(1)} %bitcast.28), channel_id=1, replica_groups=mesh['lat'=32,'rad'=4] {'lat','rad'}, dimensions={0} | all-to-all | bytes 524288 | tf_op jit(solution)/shard_map/all_to_all | solution.py:408
  75.9 2.9 %ray.3 = (bf16[1024,128]{1,0:T(8,128)(2,1)S(1)}, f32[32,64]{1,0:T(8,128)S(1)}, f32[3,256,128]{2,1,0:T(8,128)S(1)}, f32[8,128]{1,0:T(8,128)S(1)}) custom-call(bf16[1024,128]{1,0:T(8,128)(2,1)S(1)} %bitcast.22, bf16[8192,256]{1,0:T(8,128)(2,1)S(1)} %get-tuple-element.39.refs_1_, bf16[256,1024]{1,0:T(8,128)(2,1)S(1)} %get-tuple-element.40.refs_2_, ...), custom_call_target="tpu_custom_call" | custom-call | flops 8388608 | bytes 6410240 | tf_op jit(solution)/shard_map/ray/pallas_call | solution.py:393
  78.8 15.0 %all_to_all.39 = bf16[128,8,128]{2,1,0:T(8,128)(2,1)S(1)} all-to-all(bf16[128,8,128]{2,1,0:T(8,128)(2,1)S(1)} %bitcast.29), channel_id=1, replica_groups=mesh['lat'=32,'rad'=4] {'lat','rad'}, dimensions={0} | all-to-all | bytes 524288 | tf_op jit(solution)/shard_map/all_to_all | solution.py:408
  93.8 0.6 model.3
  94.4 15.0 %all_to_all.40 = bf16[128,8,128]{2,1,0:T(8,128)(2,1)S(1)} all-to-all(bf16[128,8,128]{2,1,0:T(8,128)(2,1)S(1)} %bitcast.27), channel_id=1, replica_groups=mesh['lat'=32,'rad'=4] {'lat','rad'}, dimensions={0} | all-to-all | bytes 524288 | tf_op jit(solution)/shard_map/all_to_all | solution.py:408
  109.4 1.6 %last_ray.1 = (f32[128,128]{1,0:T(8,128)S(1)}, f32[32,64]{1,0:T(8,128)S(1)}, f32[8,128]{1,0:T(8,128)S(1)}) custom-call(bf16[1024,128]{1,0:T(8,128)(2,1)S(1)} %bitcast.21, bf16[8192,256]{1,0:T(8,128)(2,1)S(1)} %get-tuple-element.39.refs_1_, bf16[256,1024]{1,0:T(8,128)(2,1)S(1)} %get-tuple-element.40.refs_2_, bf16[384,640]{1,0:T(8,128)(2,1)S(1)} %get-tuple-element.41.refs_3_, ...), custom_call_target="tpu_custom_call" | custom-call | flops 8388608 | bytes 5885952 | tf_op jit(solution)/shard_map/last_ray/pallas_call | solution.py:393
  111.0 13.6 %all_to_all.41 = f32[128,1,128]{2,1,0:T(1,128)S(1)} all-to-all(f32[128,1,128]{2,1,0:T(1,128)S(1)} %bitcast.34), channel_id=1, replica_groups=mesh['lat'=32,'rad'=4] {'lat','rad'}, dimensions={0} | all-to-all | bytes 131072 | tf_op jit(solution)/shard_map/all_to_all | solution.py:408
  124.6 0.9 last.1
